TPU v7x, 32 devices: a whole 2x2x4 slice. The times are simulated.
32 devices in a mesh: groups: 2 (over x), dom: 16 (over z, y, core).
Axes of the slice: x: 2, y: 2, z: 4, core: 2. Of those that a mesh axis runs over, the one named last changes fastest.
Arguments:
- cells: bfloat16 [32768, 256], P(('groups', 'dom')), parts along dimension 0, may hold values from -6 to 6
- counts: int32 [32], P(('groups', 'dom')), parts along dimension 0, may hold values from 256 to 1024, as said below
- w_x: bfloat16 [256, 256], replicated, may hold values from -0.375 to 0.375
- w_fx: bfloat16 [256, 256], replicated, may hold values from -0.375 to 0.375
- w_slice: bfloat16 [32, 64], replicated, may hold values from -3.59375 to 3.59375
- w_temp: bfloat16 [32], replicated, may hold values from -1.1953125 to 1.1953125
- w_qkv: bfloat16 [3, 32, 32], replicated, may hold values from -1 to 1
- w_out: bfloat16 [256, 256], replicated, may hold values from -0.375 to 0.375
- cotangent: bfloat16 [32768, 256], P(('groups', 'dom')), parts along dimension 0, may hold values from -6 to 6
Outputs:
- result: bfloat16 [32768, 256], P(('groups', 'dom')), parts along dimension 0
- grad_cells: bfloat16 [32768, 256], P(('groups', 'dom')), parts along dimension 0
- grad_w_x: float32 [512, 256], P('groups'), parts along dimension 0
- grad_w_fx: float32 [512, 256], P('groups'), parts along dimension 0
- grad_w_slice: float32 [64, 64], P('groups'), parts along dimension 0
- grad_w_temp: float32 [64], P('groups'), parts along dimension 0
- grad_w_qkv: float32 [6, 32, 32], P('groups'), parts along dimension 0
- grad_w_out: float32 [512, 256], P('groups'), parts along dimension 0
There are 2 independent parts, one for each index of `groups`. A program takes and returns all parts, laid end to end along the dimension named above; an argument that names none is the same for every part. Nothing has to cross between parts.
Inputs may be any that keep to these rules, and one draw needn't show every extreme that they name: `counts`: entry p is the number of live cells of partition p; they are its first rows, the rest of its 1024 rows are padding; some partition is full.
All inputs are finite; a program needn't handle non-finite values.
Results may differ from a plain program's by a relative error of at most 0.012.
The roundings to bfloat16 on the way count: a program that leaves them out, or rounds other values in their place, can miss the bound.
Values may be sent and summed in bfloat16 or wider, within the bound.
No kernel may reach another device: no remote copies, remote signals or barrier semaphores. Data moves between devices by JAX's collectives and lax.ppermute only.
A program may use at most 64 MiB of HBM per device.

v0:
```python
import math

import jax
import jax.numpy as jnp
from jax import lax
from jax.sharding import PartitionSpec as P

SLICES = 64


def matrix_product(form, left, right):
    return jnp.einsum(form, left, right, preferred_element_type=jnp.float32)


def slice_softmax(logits, temp_lin):
    temper = 0.5 + jax.nn.softplus(temp_lin)
    scaled = 10.0 * jnp.tanh(logits / 10.0) / temper
    powers = jnp.exp(scaled)
    return powers / jnp.sum(powers, axis=-1, keepdims=True)


def make_tokens(numerator_sums, denominators):
    return numerator_sums / (denominators[:, None] + 1e-05)


def project_tokens(tokens, qkv_weight):
    return jnp.einsum("rd,kde->kre", tokens, qkv_weight, precision=lax.Precision.HIGHEST)


def attend(query_rows, key_matrix, value_matrix):
    score_matrix = jnp.einsum(
        "zir,zjr->zij", query_rows, key_matrix, precision=lax.Precision.HIGHEST
    )
    score_matrix = score_matrix / math.sqrt(query_rows.shape[-1])
    powers = jnp.exp(10.0 * jnp.tanh(score_matrix / 10.0))
    attention_matrix = powers / jnp.sum(powers, axis=-1, keepdims=True)
    return jnp.einsum(
        "xwu,xut->xwt", attention_matrix, value_matrix, precision=lax.Precision.HIGHEST
    )


def mix_tokens(numerator_sums, denominators, qkv_weight):
    head_width = numerator_sums.shape[-1]
    maps = project_tokens(make_tokens(numerator_sums, denominators), qkv_weight)
    maps = maps.reshape(3, -1, SLICES, head_width)
    return attend(maps[0], maps[1], maps[2])


def cell_forward(cells, live_rows, w_x, w_fx, w_slice, w_temp):
    count_of_rows = cells.shape[0]
    head_width = w_slice.shape[0]
    count_of_heads = w_x.shape[1] // head_width
    projected = jnp.dot(cells, w_x, preferred_element_type=jnp.float32).astype(jnp.bfloat16)
    feature_rows = jnp.dot(cells, w_fx, preferred_element_type=jnp.float32).astype(jnp.bfloat16)
    per_head = projected.reshape(count_of_rows * count_of_heads, head_width)
    logits = jnp.dot(per_head, w_slice, preferred_element_type=jnp.float32)
    temp_lin = jnp.dot(per_head, w_temp.reshape(head_width, 1), preferred_element_type=jnp.float32)
    live_heads = jnp.repeat(live_rows, count_of_heads, axis=0)
    weight_matrix = (slice_softmax(logits, temp_lin) * live_heads).astype(jnp.bfloat16)
    weight_matrix = weight_matrix.reshape(count_of_rows, count_of_heads, -1)
    return (
        per_head,
        logits,
        temp_lin,
        live_heads,
        weight_matrix,
        feature_rows.reshape(count_of_rows, count_of_heads, head_width),
    )


def cell_backward(
    cells,
    per_head,
    logits,
    temp_lin,
    live_heads,
    weight_matrix,
    feature_rows,
    hidden_gradient3,
    mixed_lowp,
    numerator_gradient_lowp,
    denominator_gradient,
    w_x,
    w_fx,
    w_slice,
    w_temp,
):
    count_of_rows, count_of_heads, slice_count = weight_matrix.shape
    head_width = w_slice.shape[0]
    weight_gradient = matrix_product("fvo,vxo->fvx", hidden_gradient3, mixed_lowp)
    weight_gradient = (
        weight_gradient
        + matrix_product("fvo,vxo->fvx", feature_rows, numerator_gradient_lowp)
        + denominator_gradient[None]
    )
    feature_gradient = (
        matrix_product("rpc,pce->rpe", weight_matrix, numerator_gradient_lowp)
        .astype(jnp.bfloat16)
        .reshape(count_of_rows, -1)
    )
    _, soft_back = jax.vjp(slice_softmax, logits, temp_lin)
    d_logits, d_temp = soft_back(
        weight_gradient.reshape(count_of_rows * count_of_heads, slice_count) * live_heads
    )
    d_logits = d_logits.astype(jnp.bfloat16)
    d_temp = d_temp.astype(jnp.bfloat16)
    d_head = jnp.dot(d_logits, w_slice.T, preferred_element_type=jnp.float32)
    d_head = d_head + jnp.dot(
        d_temp, w_temp.reshape(1, head_width), preferred_element_type=jnp.float32
    )
    d_proj = d_head.reshape(count_of_rows, -1).astype(jnp.bfloat16)
    grad_cells = jnp.dot(d_proj, w_x.T, preferred_element_type=jnp.float32)
    grad_cells = (
        grad_cells + jnp.dot(feature_gradient, w_fx.T, preferred_element_type=jnp.float32)
    ).astype(jnp.bfloat16)
    grad_wx = jnp.dot(cells.T, d_proj, preferred_element_type=jnp.float32)
    grad_wfx = jnp.dot(cells.T, feature_gradient, preferred_element_type=jnp.float32)
    grad_slice = jnp.dot(per_head.T, d_logits, preferred_element_type=jnp.float32)
    grad_temp = jnp.dot(per_head.T, d_temp, preferred_element_type=jnp.float32).reshape(head_width)
    return (grad_cells, grad_wx, grad_wfx, grad_slice, grad_temp)


def body(cells, counts, w_x, w_fx, w_slice, w_temp, w_qkv, w_out, cotangent):
    count_of_rows, model_width = cells.shape
    positions = lax.iota(jnp.int32, count_of_rows)
    live_rows = (positions < counts[0]).astype(jnp.float32)[:, None]
    per_head, logits, temp_lin, live_heads, weight_matrix, feature_rows = cell_forward(
        cells, live_rows, w_x, w_fx, w_slice, w_temp
    )
    numerator_sums = matrix_product("skb,sko->kbo", weight_matrix, feature_rows)
    denominators = jnp.sum(weight_matrix, axis=0, dtype=jnp.float32)
    count_of_heads, slice_count, head_width = numerator_sums.shape
    flat_numer = numerator_sums.reshape(-1, head_width)
    flat_denom = denominators.reshape(-1)
    qkv_weight = w_qkv.astype(jnp.float32)
    total_numer, total_denom = lax.psum((flat_numer, flat_denom), "dom")
    mixed, mix_back = jax.vjp(mix_tokens, total_numer, total_denom, qkv_weight)
    mixed_lowp = mixed.astype(jnp.bfloat16)
    hidden_rows = (
        matrix_product("rpc,pce->rpe", weight_matrix, mixed_lowp)
        .astype(jnp.bfloat16)
        .reshape(count_of_rows, model_width)
    )
    result = jnp.dot(hidden_rows, w_out, preferred_element_type=jnp.float32).astype(jnp.bfloat16)
    hidden_gradient = jnp.dot(cotangent, w_out.T, preferred_element_type=jnp.float32).astype(
        jnp.bfloat16
    )
    hidden_gradient3 = hidden_gradient.reshape(count_of_rows, count_of_heads, head_width)
    out_grad = jnp.dot(hidden_rows.T, cotangent, preferred_element_type=jnp.float32)
    mixed_gradient = matrix_product("skb,sko->kbo", weight_matrix, hidden_gradient3)
    total_mixed = lax.psum(mixed_gradient, "dom")
    d_numer, denominator_gradient, d_qkv = mix_back(total_mixed)
    numerator_gradient_lowp = d_numer.reshape(count_of_heads, slice_count, head_width).astype(
        jnp.bfloat16
    )
    denominator_gradient = denominator_gradient.reshape(count_of_heads, slice_count)
    grad_cells, grad_wx, grad_wfx, grad_slice, grad_temp = cell_backward(
        cells,
        per_head,
        logits,
        temp_lin,
        live_heads,
        weight_matrix,
        feature_rows,
        hidden_gradient3,
        mixed_lowp,
        numerator_gradient_lowp,
        denominator_gradient,
        w_x,
        w_fx,
        w_slice,
        w_temp,
    )
    sum_wx, sum_wfx, sum_slice, sum_temp, total_out = lax.psum(
        (grad_wx, grad_wfx, grad_slice, grad_temp, out_grad), "dom"
    )
    scale = 1.0 / math.sqrt(count_of_rows * lax.axis_size("dom"))
    return (
        result,
        grad_cells,
        sum_wx * scale,
        sum_wfx * scale,
        sum_slice * scale,
        sum_temp * scale,
        d_qkv * scale,
        total_out * scale,
    )


def solution(mesh):
    placed = (
        P(("groups", "dom"), None),
        P(("groups", "dom")),
        P(),
        P(),
        P(),
        P(),
        P(),
        P(),
        P(("groups", "dom"), None),
    )
    return jax.shard_map(
        body,
        mesh=mesh,
        in_specs=placed,
        out_specs=(
            P(("groups", "dom"), None),
            P(("groups", "dom"), None),
            P("groups", None),
            P("groups", None),
            P("groups", None),
            P("groups"),
            P("groups", None, None),
            P("groups", None),
        ),
        check_vma=False,
    )
```

profile of v0, /device:TPU:0, one launch (start us, length us, event | category | flops | bytes accessed | tf_op | source)
XLA Modules:
  0.0 335.3 jit_solution(15764778787668835818)
XLA Ops:
  8.2 1.2 convolution_convert_fusion.5
  13.8 1.3 copy-done.3
  15.1 1.4 multiply_convert_fusion.1
  16.6 2.7 copy.40
  19.3 3.4 %copy.41 = bf16[1024,8,64]{0,2,1:T(8,128)(2,1)} copy(bf16[1024,8,64]{2,1,0:T(8,128)(2,1)} %bitcast.106) | data formatting | bytes 2097152 | tf_op jit(solution)/shard_map/reshape | solution.py:60
  23.9 1.6 fusion.36
  26.3 1.4 convolution_convert_fusion.1
  27.7 2.3 fusion.38
  30.1 2.7 convert_reduce_fusion
  33.5 35.1 %psum.57 = f32[512]{0:T(512)S(1)} all-reduce(f32[512]{0:T(512)S(1)} %reshape.140), channel_id=1, replica_groups=mesh['groups'=2,'dom'=16] {'dom'}, use_global_device_ids=true, to_apply=%region_3.4 | all-reduce | flops 512 | bytes 4096 | tf_op jit(solution)/shard_map/psum | solution.py:136
  69.2 54.7 %all-reduce.11.cloned.1.call-done = (f32[512,32]{0,1:T(8,128)}, f32[8,64,32]{1,2,0:T(8,128)}) async-done(((f32[512,32]{0,1:T(8,128)}, f32[8,64,32]{1,2,0:T(8,128)}), (f32[512,32]{0,1:T(8,128)}, f32[8,64,32]{1,2,0:T(8,128)})) %all-reduce.11.cloned.1.call-update) | async-done | bytes 131088 | tf_op jit(solution)/shard_map/psum | solution.py:136
  127.1 1.6 fusion.6
  128.7 1.6 squeeze.15
  130.3 1.5 convolution_bitcast_fusion.4
  131.8 1.6 multiply_reduce_fusion.2
  133.5 1.5 convolution_bitcast_fusion.3
  135.9 1.8 fusion.37
  140.0 1.5 convolution_convert_fusion
  141.5 3.6 %add_bitcast_fusion = f32[1024,8,64]{0,2,1:T(8,128)} fusion(f32[8,64,1024]{2,1,0:T(8,128)} %fusion.37, bf16[1024,8,32]{0,2,1:T(8,128)(2,1)} %bitcast.115, f32[8,64]{1,0:T(8,128)S(1)} %neg.38, bf16[8,64,32]{1,0,2:T(8,128)(2,1)S(1)} %convert_element_type.70), kind=kOutput, calls=%fused_computation.9 | convolution fusion | flops 34603008 | bytes 4753408 | tf_op jit(solution)/shard_map/fvo,vxo->fvx/dot_general | solution.py:12
  145.1 3.8 %copy.58 = f32[1024,8,64]{2,1,0:T(8,128)} copy(f32[1024,8,64]{0,2,1:T(8,128)} %add_bitcast_fusion) | data formatting | bytes 4194304 | tf_op jit(solution)/shard_map/add | solution.py:92
  149.0 3.8 %copy.59 = f32[8192,64]{0,1:T(8,128)} copy(f32[8192,64]{1,0:T(8,128)} %bitcast.107) | data formatting | bytes 4194304 | tf_op jit(solution)/shard_map/reshape | solution.py:103
  152.8 3.0 multiply_reduce_fusion.1
  156.3 1.4 multiply_reduce_fusion
  159.5 2.6 copy.60
  162.2 3.9 %convert_element_type.74 = bf16[1024,256]{1,0:T(8,128)(2,1)} reshape(bf16[8192,32]{1,0:T(8,128)(2,1)} %copy.60) | data formatting | bytes 1048576 | tf_op jit(solution)/shard_map/convert_element_type | solution.py:111
  166.1 2.2 convolution_bitcast_fusion.1
  168.2 2.4 fusion.39
  171.7 1.1 convolution_convert_fusion.2
  173.9 58.6 %all-reduce.3 = (f32[32,64]{1,0:T(8,128)S(1)}, f32[32]{0:T(128)S(1)}) all-reduce(f32[32,64]{1,0:T(8,128)S(1)} %fusion.40, f32[32]{0:T(128)S(1)} %convolution_bitcast_fusion.6), channel_id=1, replica_groups=mesh['groups'=2,'dom'=16] {'dom'}, use_global_device_ids=true, to_apply=%region_12.13 | all-reduce | flops 2080 | bytes 16640 | tf_op jit(solution)/shard_map/psum | solution.py:174
  234.7 1.1 fusion.2
  235.9 89.0 %all-reduce.9.cloned.1.call-done = (f32[256,256]{0,1:T(8,128)}, f32[256,256]{0,1:T(8,128)}, f32[256,256]{0,1:T(8,128)}) async-done(((f32[256,256]{0,1:T(8,128)}, f32[256,256]{0,1:T(8,128)}, f32[256,256]{0,1:T(8,128)}), (f32[256,256]{0,1:T(8,128)}, f32[256,256]{0,1:T(8,128)}, f32[256,256]{0,1:T(8,128)})) %all-reduce.9.cloned.1.call-update) | async-done | bytes 786448 | tf_op jit(solution)/shard_map/psum | solution.py:174
  324.9 1.1 broadcast_multiply_fusion
  (102 shorter events, 23.5 us)
Async XLA Ops:
  7.2 1.0 copy-start
  7.2 3.2 copy-start.24
  7.2 116.7 %all-reduce.11.cloned.1.call-start = ((), (), s32[]{:S(2)}) async-start(), calls=%async_computation.1 | async-start | bytes 393216 | tf_op jit(solution)/shard_map/psum | solution.py:136
  10.3 2.4 copy-start.22
  13.8 1.3 copy-start.3
  19.3 3.4 %copy-start.12 = (bf16[256,256]{1,0:T(8,128)(2,1)S(1)}, bf16[256,256]{1,0:T(8,128)(2,1)}, u32[]{:S(2)}) copy-start(bf16[256,256]{1,0:T(8,128)(2,1)} %param.12) | copy-start | bytes 393220
  22.7 3.6 %copy-start.10 = (bf16[256,256]{1,0:T(8,128)(2,1)S(1)}, bf16[256,256]{1,0:T(8,128)(2,1)}, u32[]{:S(2)}) copy-start(bf16[256,256]{1,0:T(8,128)(2,1)} %param.16) | copy-start | bytes 393220
  23.1 0.8 copy-start.6
  27.7 41.4 %copy-start.20 = (bf16[3,32,32]{2,1,0:T(8,128)(2,1)S(1)}, bf16[3,32,32]{2,1,0:T(8,128)(2,1)}, u32[]{:S(2)}) copy-start(bf16[3,32,32]{2,1,0:T(8,128)(2,1)} %param.15) | copy-start | bytes 18436
  30.0 294.8 %all-reduce.9.cloned.1.call-start = ((), (), s32[]{:S(2)}) async-start(), calls=%async_computation | async-start | bytes 1572864 | tf_op jit(solution)/shard_map/psum | solution.py:174
  130.3 4.7 %copy-start.15 = (f32[8,64,32]{1,0,2:T(8,128)S(1)}, f32[8,64,32]{1,0,2:T(8,128)}, u32[]{:S(2)}) copy-start(f32[8,64,32]{1,0,2:T(8,128)} %squeeze.14) | copy-start | bytes 196612
  131.8 3.7 %copy-start.14 = (f32[8,64,32]{1,0,2:T(8,128)S(1)}, f32[8,64,32]{1,0,2:T(8,128)}, u32[]{:S(2)}) copy-start(f32[8,64,32]{1,0,2:T(8,128)} %squeeze.15) | copy-start | bytes 196612
  135.5 2.2 copy-start.1
  137.8 1.5 copy-start.9
  137.8 1.8 copy-start.21
  149.0 3.8 %copy-start.19 = (f32[8192]{0:T(1024)S(1)}, f32[8192]{0:T(1024)}, u32[]{:S(2)}) copy-start(f32[8192]{0:T(1024)} %multiply_divide_fusion.1) | copy-start | bytes 98308
  152.8 3.0 copy-start.2
  152.8 3.5 %copy-start.4 = (f32[8192,64]{0,1:T(8,128)S(1)}, f32[8192,64]{0,1:T(8,128)}, u32[]{:S(2)}) copy-start(f32[8192,64]{0,1:T(8,128)} %copy-done.3) | copy-start | bytes 6291460
  152.8 3.5 %copy-start.18 = (f32[8192]{0:T(1024)S(1)}, f32[8192]{0:T(1024)}, u32[]{:S(2)}) copy-start(f32[8192]{0:T(1024)} %get-tuple-element.40) | copy-start | bytes 98308
  157.7 0.8 copy-start.23
  157.7 0.8 copy-start.25
  162.2 6.1 %copy-start.16 = (bf16[256,256]{1,0:T(8,128)(2,1)S(1)}, bf16[256,256]{1,0:T(8,128)(2,1)}, u32[]{:S(2)}) copy-start(bf16[256,256]{1,0:T(8,128)(2,1)} %param.11) | copy-start | bytes 393220
  166.0 4.5 %copy-start.5 = (bf16[8,32,1024]{2,1,0:T(8,128)(2,1)S(1)}, bf16[8,32,1024]{2,1,0:T(8,128)(2,1)}, u32[]{:S(2)}) copy-start(bf16[8,32,1024]{2,1,0:T(8,128)(2,1)} %convolution_convert_fusion.3) | copy-start | bytes 1572868
  166.1 4.5 %copy-start.8 = (bf16[1024,256]{1,0:T(8,128)(2,1)S(1)}, bf16[1024,256]{1,0:T(8,128)(2,1)}, u32[]{:S(2)}) copy-start(bf16[1024,256]{1,0:T(8,128)(2,1)} %param.17) | copy-start | bytes 1572868
  166.1 5.6 %copy-start.11 = (bf16[256,256]{1,0:T(8,128)(2,1)S(1)}, bf16[256,256]{1,0:T(8,128)(2,1)}, u32[]{:S(2)}) copy-start(bf16[256,256]{1,0:T(8,128)(2,1)} %param.16) | copy-start | bytes 393220
  173.5 61.2 %copy-start.13 = (bf16[256,256]{1,0:T(8,128)(2,1)S(1)}, bf16[256,256]{1,0:T(8,128)(2,1)}, u32[]{:S(2)}) copy-start(bf16[256,256]{1,0:T(8,128)(2,1)} %param.12) | copy-start | bytes 393220
  173.9 60.8 %copy-start.7 = (f32[1024,256]{1,0:T(8,128)S(1)}, f32[1024,256]{1,0:T(8,128)}, u32[]{:S(2)}) copy-start(f32[1024,256]{1,0:T(8,128)} %fusion.39) | copy-start | bytes 3145732
  324.9 2.8 copy-start.17
Sparse Core Ops, SparseCore 0:
  30.2 93.6 all-reduce.10
  234.3 90.5 all-reduce.8
where the time goes:
time: 336 us; the launch traced here: 335 us
  waiting for transfers between devices  144 us (43%)
  blocking collectives  93.8 us (28%)
  matrix products  36.2 us (11%)
  local copies, waits for them, and re-layouts  33.8 us (10%)
  between operations  15.1 us (4%)
  other arithmetic  12.6 us (4%)
    psum x1, waiting for transfers between devices, body(): lax.psum((grad_wx, grad_wfx, grad_slice, grad_temp, out_grad), 'dom')  89 us
    psum x1, blocking collectives, body(): lax.psum((grad_wx, grad_wfx, grad_slice, grad_temp, out_grad), 'dom')  58.6 us
    psum x1, waiting for transfers between devices, body(): total_numer, total_denom = lax.psum((flat_numer, flat_denom), 'dom')  54.7 us
    psum x1, blocking collectives, body(): total_numer, total_denom = lax.psum((flat_numer, flat_denom), 'dom')  35.1 us
    dot_general x6, matrix products, matrix_product(): return jnp.einsum(form, left, right, preferred_element_type=jnp.float32)  11.9 us
    unnamed x57, local copies, waits for them, and re-layouts  6.96 us
  transfers between devices with their start and end apart: 2, of which 2 were waited for; matrix products, arithmetic and copies ran while one was open for 2% of the time, Pallas kernels for 0%

commit v1 on v0

v1 whole, which is shorter than its diff:
```python
import functools
import math

import jax
import jax.numpy as jnp
from jax import lax
from jax.experimental import pallas as pl
from jax.experimental.pallas import tpu as pltpu
from jax.sharding import PartitionSpec as P

F32 = jnp.float32
BF16 = jnp.bfloat16
HIGHEST = lax.Precision.HIGHEST
HEADS = 8
SLICES = 64
HEAD = 32
WIDTH = HEADS * HEAD
ROWS1 = 144
LOG2E = math.log2(math.e)
CHUNK = 256


def nn(a, b, precision=None):
    return lax.dot_general(
        a, b, (((1,), (0,)), ((), ())), precision=precision, preferred_element_type=F32
    )


def nt(a, b, precision=None):
    return lax.dot_general(
        a, b, (((1,), (1,)), ((), ())), precision=precision, preferred_element_type=F32
    )


def iota(shape, dim):
    return lax.broadcasted_iota(jnp.int32, shape, dim)


def slice_blocks(w_slice):
    tall = jnp.concatenate([w_slice] * 4, axis=0)
    pick = (iota((SLICES, 256), 1) % SLICES == iota((SLICES, 256), 0)).astype(BF16)
    wide = nn(tall, pick)
    same = iota((128, 256), 0) // HEAD == iota((128, 256), 1) // SLICES
    return jnp.where(same, wide, 0.0)


def temp_blocks(w_temp):
    pick = (iota((HEAD, WIDTH), 1) % HEAD == iota((HEAD, WIDTH), 0)).astype(BF16)
    wide = nn(jnp.broadcast_to(w_temp, (HEADS, HEAD)), pick)
    same = iota((HEADS, WIDTH), 0) == iota((HEADS, WIDTH), 1) // HEAD
    return jnp.where(same, wide, 0.0).astype(BF16)


def forward_kernel(
    counts, cells, cot, w_x, w_fx, w_slice, w_temp, w_out,
    weights, proj, fd, stats, keep, send,
    wxt, wft, wsb,
):
    core = lax.rem(lax.axis_index("dom"), 2)
    rows = cells.shape[0]
    wxt[...] = w_x[...].T
    wft[...] = w_fx[...].T
    wsb[...] = slice_blocks(w_slice[...]).T.astype(BF16)
    wtb = temp_blocks(w_temp[...])
    count = counts[0]

    def chunk(j, carry):
        at = pl.ds(pl.multiple_of(j * CHUNK, CHUNK), CHUNK)
        c = cells[at, :]
        projected = nt(wxt[...], c).astype(BF16)
        proj[:, at] = projected
        feat = nt(wft[...], c).astype(BF16)
        dhid = nt(w_out[...], cot[at, :]).astype(BF16)
        for h in range(HEADS):
            mine = slice(HEAD * h, HEAD * h + HEAD)
            fd[2 * HEAD * h : 2 * HEAD * h + HEAD, at] = feat[mine]
            fd[2 * HEAD * h + HEAD : 2 * HEAD * h + 2 * HEAD, at] = dhid[mine]
        lin = nn(wtb, projected)
        e = jnp.exp(-jnp.abs(lin))
        soft = jnp.maximum(lin, 0.0) + jnp.log(1.0 + e)
        inv = 1.0 / (0.5 + soft)
        sig = jnp.where(lin >= 0, 1.0, e) / (1.0 + e)
        a = inv * (10.0 * LOG2E)
        live = jnp.where(j * CHUNK + iota((1, CHUNK), 1) < count, 1.0, 0.0)
        norms = []
        for g in range(2):
            x = nn(wsb[...], projected[128 * g : 128 * g + 128])
            for k in range(4):
                h = 4 * g + k
                t = jnp.tanh(x[SLICES * k : SLICES * k + SLICES] * 0.1)
                p = jnp.exp2(t * a[h : h + 1])
                r = live / jnp.sum(p, axis=0, keepdims=True)
                weights[SLICES * h : SLICES * h + SLICES, at] = (p * r).astype(BF16)
                norms.append(r)
        stats[0:8, at] = a
        stats[8:16, at] = inv
        stats[16:24, at] = inv * inv * sig * (-10.0)
        stats[24:32, at] = jnp.concatenate(norms, axis=0)
        return carry

    lax.fori_loop(0, rows // CHUNK, chunk, 0)
    ones = jnp.ones((16, rows), BF16)
    first = iota((64, 128), 1) < SLICES
    blocks, sums = [], []
    for q in range(4):
        mine = slice(128 * q, 128 * q + 128)
        out = nt(jnp.concatenate([fd[mine, :], ones], axis=0), weights[mine, :])
        blocks.append(jnp.where(first, out[0:64], out[64:128]))
        sums.append(out[128:129])
    zero = jnp.zeros((14, 128), F32)
    halves = [
        jnp.concatenate([blocks[2 * s], blocks[2 * s + 1], sums[2 * s], sums[2 * s + 1], zero], 0)
        for s in range(2)
    ]
    keep[...] = jnp.where(core == 0, halves[0], halves[1])
    send[...] = jnp.where(core == 0, halves[1], halves[0])


def spread_kernel(mine, other, out):
    total = (mine[...] + other[...]).astype(BF16)
    n = mine.shape[0]
    for k in range(out.shape[0] // n):
        out[n * k : n * k + n, :] = total


def sum_blocks(ref, n):
    total = ref[0:n, :].astype(F32)
    for k in range(1, ref.shape[0] // n):
        total = total + ref[n * k : n * k + n, :].astype(F32)
    return total


def mix_kernel(parts, w_qkv, out):
    total = sum_blocks(parts, ROWS1)
    numer = jnp.concatenate([total[0:32], total[64:96]], axis=1)
    d_mixed = jnp.concatenate([total[32:64], total[96:128]], axis=1)
    denom = jnp.concatenate([total[128:129], total[129:130]], axis=1) + 1e-05
    inverse = 1.0 / denom
    tokens = numer * inverse
    maps = [w_qkv[k].astype(F32) for k in range(3)]
    q, key, val = [nn(m.T, tokens, HIGHEST) for m in maps]
    key_rows, val_rows = key.T, val.T
    scores = nn(key_rows, q, HIGHEST) * (1.0 / math.sqrt(HEAD))
    same = iota((256, 256), 0) // SLICES == iota((256, 256), 1) // SLICES
    t = jnp.tanh(scores * 0.1)
    powers = jnp.where(same, jnp.exp2(t * (10.0 * LOG2E)), 0.0)
    att = powers * (1.0 / jnp.sum(powers, axis=0, keepdims=True))
    mixed = nn(val, att, HIGHEST)
    d_att = nn(val_rows, d_mixed, HIGHEST)
    d_val = nt(d_mixed, att, HIGHEST)
    inner = jnp.sum(att * d_att, axis=0, keepdims=True)
    d_scores = att * (d_att - inner) * ((1.0 - t * t) * (1.0 / math.sqrt(HEAD)))
    d_q = nn(key, d_scores, HIGHEST)
    d_key = nt(q, d_scores, HIGHEST)
    grads = (d_q, d_key, d_val)
    d_tokens = sum(nn(m, g, HIGHEST) for m, g in zip(maps, grads))
    d_numer = d_tokens * inverse
    d_denom = -jnp.sum(d_numer * tokens, axis=0, keepdims=True)
    out[0:32, :] = d_numer.astype(BF16).astype(F32)
    out[32:64, :] = mixed.astype(BF16).astype(F32)
    out[64:72, :] = jnp.broadcast_to(d_denom, (8, 256))
    for k in range(3):
        out[72 + 32 * k : 104 + 32 * k, 0:32] = nt(tokens, grads[k], HIGHEST)
        out[72 + 32 * k : 104 + 32 * k, 32:256] = jnp.zeros((32, 224), F32)


def backward_kernel(
    scale,
    cells, cot, weights, proj, fd, stats, mine, other, w_x, w_fx, w_slice, w_temp, w_out,
    result, grad_cells, keep, send, grad_qkv,
    hid, dpf, dlog, dtemp, lhs_h, lhs_w, dden, wsb, wsd, wxf, wot,
):
    core = lax.rem(lax.axis_index("dom"), 2)
    rows = cells.shape[0]
    lower = core == 0
    blocks = slice_blocks(w_slice[...])
    wsd[...] = blocks.astype(BF16)
    wsb[...] = blocks.T.astype(BF16)
    wtb = temp_blocks(w_temp[...]).astype(F32).T
    wxf[:, 0:WIDTH] = w_x[...]
    wxf[:, WIDTH : 2 * WIDTH] = w_fx[...]
    wot[...] = w_out[...].T
    diag64 = iota((256, 256), 0) // 64 == iota((256, 256), 1) // 64
    diag32 = iota((128, 256), 0) // 32 == iota((128, 256), 1) // 64
    for g in range(2):
        e = jnp.where(lower == (g == 0), mine[0:72, :], other[0:72, :])
        both = jnp.where(diag64, jnp.concatenate([e[0:64]] * 4, axis=0), 0.0)
        lhs_w[g] = both.T.astype(BF16)
        lhs_h[g, 0:128, :] = jnp.where(
            diag32, jnp.concatenate([e[32:64]] * 4, axis=0), 0.0
        ).astype(BF16)
        lhs_h[g, 128:256, :] = jnp.where(
            diag32, jnp.concatenate([e[0:32]] * 4, axis=0), 0.0
        ).astype(BF16)
        column = e[64:72].T[:, 0:1]
        dden[256 * g : 256 * g + 256, :] = jnp.broadcast_to(column, (256, CHUNK))
    for k in range(3):
        block = slice(72 + 32 * k, 104 + 32 * k)
        grad_qkv[k] = (mine[block, 0:32] + other[block, 0:32]) * scale

    def chunk(j, carry):
        at = pl.ds(pl.multiple_of(j * CHUNK, CHUNK), CHUNK)
        a = stats[0:8, at]
        inv = stats[8:16, at]
        slope = stats[16:24, at]
        norm = stats[24:32, at]
        for g in range(2):
            half = slice(128 * g, 128 * g + 128)
            wide = slice(256 * g, 256 * g + 256)
            hf = nn(lhs_h[g], weights[wide, at])
            hid[half, at] = hf[0:128].astype(BF16)
            dpf[WIDTH + 128 * g : WIDTH + 128 * g + 128, at] = hf[128:256].astype(BF16)
            dw = nn(lhs_w[g], fd[wide, at])
            x = nn(wsb[...], proj[half, at])
            outer = []
            for k in range(4):
                h = 4 * g + k
                sub = slice(SLICES * k, SLICES * k + SLICES)
                rng = slice(SLICES * h, SLICES * h + SLICES)
                one = slice(h, h + 1)
                t = jnp.tanh(x[sub] * 0.1)
                soft = jnp.exp2(t * a[one]) * norm[one]
                d = dw[sub] + dden[rng, :]
                inner = jnp.sum(soft * d, axis=0, keepdims=True)
                ds = soft * (d - inner)
                dlog[rng, at] = (ds * ((1.0 - t * t) * inv[one])).astype(BF16)
                dt = jnp.sum(ds * t, axis=0, keepdims=True) * slope[one]
                dt = dt.astype(BF16).astype(F32)
                dtemp[one, at] = dt
                outer.append(wtb[HEAD * h : HEAD * h + HEAD, h : h + 1] * dt)
            dp = nn(wsd[...], dlog[wide, at]) + jnp.concatenate(outer, axis=0)
            dpf[half, at] = dp.astype(BF16)
        gct = nn(wxf[...], dpf[:, at])
        grad_cells[at, :] = gct.T.astype(BF16)
        rst = nn(wot[...], hid[:, at])
        result[at, :] = rst.T.astype(BF16)
        return carry

    lax.fori_loop(0, rows // CHUNK, chunk, 0)
    d_out = nn(hid[...], cot[...])
    d_in = nn(dpf[...], cells[...])
    d_x = d_in[0:WIDTH].T
    d_fx = d_in[WIDTH : 2 * WIDTH].T
    even = jnp.zeros((HEAD, 128), F32)
    odd = jnp.zeros((HEAD, 128), F32)
    for q in range(4):
        pair = dlog[128 * q : 128 * q + 128, :]
        even = even + nt(proj[64 * q : 64 * q + 32, :], pair)
        odd = odd + nt(proj[64 * q + 32 : 64 * q + 64, :], pair)
    d_slice = jnp.where(iota((HEAD, 128), 1) < SLICES, even, odd)
    d_slice = jnp.concatenate([d_slice[0:16], d_slice[16:32]], axis=1)
    d_temp = nt(dtemp[...].astype(BF16), proj[...])
    own = iota((HEADS, WIDTH), 0) == iota((HEADS, WIDTH), 1) // HEAD
    d_temp = jnp.where(own, d_temp, 0.0)
    d_temp = jnp.broadcast_to(jnp.sum(d_temp, axis=0, keepdims=True), (HEADS, WIDTH))
    for ref, first in ((keep, lower), (send, jnp.logical_not(lower))):
        for i, grad in enumerate((d_out, d_x, d_fx)):
            ref[128 * i : 128 * i + 128, :] = jnp.where(first, grad[0:128], grad[128:256]).astype(
                BF16
            )
        ref[384:400, :] = jnp.concatenate(
            [jnp.where(first, d_slice[0:8], d_slice[8:16]), d_temp], axis=0
        ).astype(BF16)
        ref[400:, :] = jnp.zeros((ref.shape[0] - 400, WIDTH), BF16)


def add_kernel(mine, other, out):
    out[...] = (mine[...].astype(F32) + other[...].astype(F32)).astype(BF16)


def place_kernel(mine, other, d_x, d_fx, d_slice, d_temp, d_out):
    core = lax.rem(lax.axis_index("dom"), 2)
    lower = core == 0
    small = []
    for s in range(2):
        src = jnp.where(lower == (s == 0), mine[0:400, :], other[0:400, :]).astype(F32)
        for i, ref in enumerate((d_out, d_x, d_fx)):
            ref[128 * s : 128 * s + 128, :] = src[128 * i : 128 * i + 128]
        small.append(src[384:392])
        if s == 0:
            v = src[392:400]
            v = v[:, 0:128] + v[:, 128:256]
            v = v + pltpu.roll(v, 64, 1)
            v = v + pltpu.roll(v, 32, 1)
            d_temp[...] = v[0:1, 0:32]
    rows = jnp.concatenate(
        [small[0][:, 0:128], small[1][:, 0:128], small[0][:, 128:256], small[1][:, 128:256]], axis=0
    )
    rows = rows + pltpu.roll(rows, 64, 1)
    d_slice[...] = rows[:, 0:SLICES]


VMEM = pl.BlockSpec(memory_space=pltpu.VMEM)
SMEM = pl.BlockSpec(memory_space=pltpu.SMEM)


def call(kernel, shapes, args, scratch=(), scalars=0, name=None):
    return pl.pallas_call(
        kernel,
        out_shape=[jax.ShapeDtypeStruct(s, d) for s, d in shapes],
        in_specs=[SMEM] * scalars + [VMEM] * (len(args) - scalars),
        out_specs=[VMEM] * len(shapes),
        scratch_shapes=[pltpu.VMEM(s, d) for s, d in scratch],
        name=name,
    )(*args)


def body(devices, cells, counts, w_x, w_fx, w_slice, w_temp, w_qkv, w_out, cotangent):
    rows = cells.shape[0]
    peers = devices // 2
    pairs = [(i, i ^ 1) for i in range(devices)]
    groups = [list(range(c, devices, 2)) for c in range(2)]
    scale = 1.0 / math.sqrt(rows * devices)
    temp = w_temp.reshape(1, HEAD)
    hm = HEADS * SLICES

    def exchange(x):
        return lax.all_to_all(x, "dom", 0, 0, axis_index_groups=groups, tiled=True)

    weights, proj, fd, stats, keep, send = call(
        forward_kernel,
        [
            ((hm, rows), BF16),
            ((WIDTH, rows), BF16),
            ((2 * WIDTH, rows), BF16),
            ((32, rows), F32),
            ((ROWS1, 128), F32),
            ((ROWS1, 128), F32),
        ],
        (counts, cells, cotangent, w_x, w_fx, w_slice, temp, w_out),
        scratch=[((256, 256), BF16), ((256, 256), BF16), ((256, 128), BF16)],
        scalars=1,
        name="forward",
    )
    other = lax.ppermute(send, "dom", pairs)
    (spread,) = call(
        spread_kernel, [((peers * ROWS1, 128), BF16)], (keep, other), name="spread"
    )
    parts = exchange(spread)
    (mine,) = call(mix_kernel, [((168, 256), F32)], (parts, w_qkv), name="mix")
    other = lax.ppermute(mine, "dom", pairs)
    chunk = -(-400 // peers)
    chunk = -(-chunk // 8) * 8
    half = chunk * peers
    result, grad_cells, keep, send, grad_qkv = call(
        functools.partial(backward_kernel, scale),
        [
            ((rows, WIDTH), BF16),
            ((rows, WIDTH), BF16),
            ((half, WIDTH), BF16),
            ((half, WIDTH), BF16),
            ((3, HEAD, HEAD), F32),
        ],
        (cells, cotangent, weights, proj, fd, stats, mine, other)
        + (w_x, w_fx, w_slice, temp, w_out),
        scratch=[
            ((WIDTH, rows), BF16),
            ((2 * WIDTH, rows), BF16),
            ((hm, rows), BF16),
            ((8, rows), F32),
            ((2, 256, 256), BF16),
            ((2, 256, 256), BF16),
            ((hm, CHUNK), F32),
            ((256, 128), BF16),
            ((128, 256), BF16),
            ((256, 512), BF16),
            ((256, 256), BF16),
        ],
        name="backward",
    )
    other = lax.ppermute(send, "dom", pairs)
    (summed,) = call(add_kernel, [((half, WIDTH), BF16)], (keep, other), name="pair_add")
    parts = exchange(summed)

    def gather(parts_ref, out):
        total = (sum_blocks(parts_ref, chunk) * scale).astype(BF16)
        for k in range(peers):
            out[chunk * k : chunk * k + chunk, :] = total

    (spread,) = call(gather, [((half, WIDTH), BF16)], (parts,), name="gather")
    mine = exchange(spread)
    other = lax.ppermute(mine, "dom", pairs)
    d_x, d_fx, d_slice, d_temp, d_out = call(
        place_kernel,
        [
            ((WIDTH, WIDTH), F32),
            ((WIDTH, WIDTH), F32),
            ((HEAD, SLICES), F32),
            ((1, HEAD), F32),
            ((WIDTH, WIDTH), F32),
        ],
        (mine, other),
        name="place",
    )
    return result, grad_cells, d_x, d_fx, d_slice, d_temp.reshape(HEAD), grad_qkv, d_out


def solution(mesh):
    cell = P(("groups", "dom"), None)
    return jax.shard_map(
        functools.partial(body, mesh.shape["dom"]),
        mesh=mesh,
        in_specs=(cell, P(("groups", "dom")), P(), P(), P(), P(), P(), P(), cell),
        out_specs=(
            cell,
            cell,
            P("groups", None),
            P("groups", None),
            P("groups", None),
            P("groups"),
            P("groups", None, None),
            P("groups", None),
        ),
        check_vma=False,
    )
```

time: 336 us -> 80.7 us (0.24)
  waiting for transfers between devices: 144 us -> 5.79 us
  blocking collectives: 93.8 us -> 42.8 us
  matrix products: 36.2 us -> 0 us
  local copies, waits for them, and re-layouts: 33.8 us -> 2.68 us
  Pallas kernels: 0 us -> 26.9 us
  between operations: 15.1 us -> 1.29 us
  other arithmetic: 12.6 us -> 0 us
    psum x2 -> x0, waiting for transfers between devices: 144 us -> none  [the longest x1 89 us: body(): lax.psum((grad_wx, grad_wfx, grad_slice, grad_temp, out_grad), 'dom')]
    psum x2 -> x0, blocking collectives: 93.8 us -> none  [the longest x1 58.6 us: body(): lax.psum((grad_wx, grad_wfx, grad_slice, grad_temp, out_grad), 'dom')]
    all_to_all x0 -> x3, blocking collectives: none -> 42.8 us  [exchange(): return lax.all_to_all(x, 'dom', 0, 0, axis_index_groups=groups, tiled=True)]
    dot_general x28 -> x0, matrix products: 35.2 us -> none  [the longest x6 11.9 us: matrix_product(): return jnp.einsum(form, left, right, preferred_element_type=jnp.float32)]
    pallas_call x0 -> x7, Pallas kernels: none -> 26.9 us  [call(): pl.pallas_call(kernel, out_shape=[jax.ShapeDtypeStruct(s, d) for s, d in...]
    convert_element_type x5 -> x0, local copies, waits for them, and re-layouts: 9.38 us -> none  [the longest x2 6.51 us: cell_backward(): d_proj = d_head.reshape(count_of_rows, -1).astype(jnp.bfloat16)]
    reshape x6 -> x0, local copies, waits for them, and re-layouts: 9.08 us -> none  [the longest x1 3.83 us: cell_backward(): weight_gradient.reshape(count_of_rows * count_of_heads, slice_count)]
    reduce_sum x3 -> x0, other arithmetic: 7.03 us -> none  [the longest x1 2.99 us: slice_softmax(): return powers / jnp.sum(powers, axis=-1, keepdims=True)]
  transfers between devices with their start and end apart: 2 -> 4, of which waited for: 2 -> 4; matrix products, arithmetic and copies ran while one was open for 2% -> 0% of each run, Pallas kernels for 0% -> 0%
where the time goes in v1:
time: 80.7 us; the launch traced here: 80.1 us
  blocking collectives  42.8 us (53%)
  Pallas kernels  26.9 us (33%)
  waiting for transfers between devices  5.79 us (7%)
  local copies, waits for them, and re-layouts  2.68 us (3%)
  between operations  1.29 us (2%)
    all_to_all x3, blocking collectives, exchange(): return lax.all_to_all(x, 'dom', 0, 0, axis_index_groups=groups, tiled=True)  42.8 us
    pallas_call x7, Pallas kernels, call(): pl.pallas_call(kernel, out_shape=[jax.ShapeDtypeStruct(s, d) for s, d in...  26.9 us
    ppermute x2, waiting for transfers between devices, body(): other = lax.ppermute(mine, 'dom', pairs)  3.1 us
    ppermute x2, waiting for transfers between devices, body(): other = lax.ppermute(send, 'dom', pairs)  2.69 us
    unnamed x10, local copies, waits for them, and re-layouts  2.68 us
  transfers between devices with their start and end apart: 4, of which 4 were waited for; matrix products, arithmetic and copies ran while one was open for 0% of the time, Pallas kernels for 0%

profile of v1, /device:TPU:0, one launch (start us, length us, event | category | flops | bytes accessed | tf_op | source)
XLA Modules:
  0.0 80.1 jit_solution(4529373803044197980)
XLA Ops:
  1.3 5.4 %forward.1 = (bf16[512,1024]{1,0:T(8,128)(2,1)}, bf16[256,1024]{1,0:T(8,128)(2,1)}, bf16[512,1024]{1,0:T(8,128)(2,1)}, f32[32,1024]{1,0:T(8,128)}, f32[144,128]{1,0:T(8,128)}, /*index=5*/f32[144,128]{1,0:T(8,128)}) custom-call(s32[1]{0:T(128)S(6)} %copy.17.counts, bf16[1024,256]{1,0:T(8,128)(2,1)} %cells.3, bf16[1024,256]{1,0:T(8,128)(2,1)} %cot.3, ...), custom_call_target="tpu_custom_call" | custom-call | tf_op jit(solution)/shard_map/forward/pallas_call | solution.py:298
  6.7 0.5 collective-permute-start
  7.2 1.1 %collective-permute-done.other = f32[144,128]{1,0:T(8,128)S(1)} collective-permute-done((f32[144,128]{1,0:T(8,128)}, f32[144,128]{1,0:T(8,128)S(1)}, u32[]{:S(2)}, u32[]{:S(2)}) %collective-permute-start) | collective-permute-done | bytes 73760 | tf_op jit(solution)/shard_map/ppermute | solution.py:335
  8.3 0.0 copy-start.4
  8.3 0.6 copy-done.4
  9.0 1.7 %spread.1 = bf16[1152,128]{1,0:T(8,128)(2,1)} custom-call(f32[144,128]{1,0:T(8,128)} %get-tuple-element.28.mine, f32[144,128]{1,0:T(8,128)} %copy-done.4), custom_call_target="tpu_custom_call" | custom-call | tf_op jit(solution)/shard_map/spread/pallas_call | solution.py:298
  10.6 17.9 %all_to_all.33 = bf16[8,144,128]{2,1,0:T(8,128)(2,1)} all-to-all(bf16[8,144,128]{2,1,0:T(8,128)(2,1)} %bitcast.8), channel_id=1, replica_groups={{0,2,4,6,8,10,12,14},{1,3,5,7,9,11,13,15},{16,18,20,22,24,26,28,30},{17..., dimensions={0} | all-to-all | bytes 589824 | tf_op jit(solution)/shard_map/all_to_all | solution.py:318
  28.6 4.3 %mix.1.mine = f32[168,256]{1,0:T(8,128)} custom-call(bf16[1152,128]{1,0:T(8,128)(2,1)} %bitcast.9, bf16[3,32,32]{2,1,0:T(8,128)(2,1)} %w_qkv.1), custom_call_target="tpu_custom_call" | custom-call | tf_op jit(solution)/shard_map/mix/pallas_call | solution.py:298
  32.9 0.0 collective-permute-start.1
  32.9 1.6 %collective-permute-done.1.other = f32[168,256]{1,0:T(8,128)S(1)} collective-permute-done((f32[168,256]{1,0:T(8,128)}, f32[168,256]{1,0:T(8,128)S(1)}, u32[]{:S(2)}, u32[]{:S(2)}) %collective-permute-start.1) | collective-permute-done | bytes 172064 | tf_op jit(solution)/shard_map/ppermute | solution.py:341
  34.5 0.0 copy-start.3
  34.5 0.7 copy-done.3
  35.2 10.0 %backward.1 = (bf16[1024,256]{1,0:T(8,128)(2,1)}, bf16[1024,256]{1,0:T(8,128)(2,1)}, bf16[448,256]{1,0:T(8,128)(2,1)}, bf16[448,256]{1,0:T(8,128)(2,1)}, f32[3,32,32]{2,1,0:T(8,128)}) custom-call(bf16[1024,256]{1,0:T(8,128)(2,1)} %cells.3, bf16[1024,256]{1,0:T(8,128)(2,1)} %cot.3, bf16[512,1024]{1,0:T(8,128)(2,1)} %get-tuple-element.24.weights, ...), custom_call_target="tpu_custom_call" | custom-call | tf_op jit(solution)/shard_map/backward/pallas_call | solution.py:298
  45.2 0.1 collective-permute-start.2
  45.3 1.6 %collective-permute-done.2.other = bf16[448,256]{1,0:T(8,128)(2,1)S(1)} collective-permute-done((bf16[448,256]{1,0:T(8,128)(2,1)}, bf16[448,256]{1,0:T(8,128)(2,1)S(1)}, u32[]{:S(2)}, u32[]{:S(2)}) %collective-permute-start.2) | collective-permute-done | bytes 229408 | tf_op jit(solution)/shard_map/ppermute | solution.py:371
  46.9 0.0 copy-start.2
  46.9 0.7 copy-done.2
  47.6 1.8 %pair_add.1 = bf16[448,256]{1,0:T(8,128)(2,1)} custom-call(bf16[448,256]{1,0:T(8,128)(2,1)} %get-tuple-element.32.mine, bf16[448,256]{1,0:T(8,128)(2,1)} %copy-done.2), custom_call_target="tpu_custom_call" | custom-call | tf_op jit(solution)/shard_map/pair_add/pallas_call | solution.py:298
  49.4 13.0 %all_to_all.34 = bf16[8,56,256]{2,1,0:T(8,128)(2,1)} all-to-all(bf16[8,56,256]{2,1,0:T(8,128)(2,1)} %bitcast.14), channel_id=1, replica_groups={{0,2,4,6,8,10,12,14},{1,3,5,7,9,11,13,15},{16,18,20,22,24,26,28,30},{17..., dimensions={0} | all-to-all | bytes 458752 | tf_op jit(solution)/shard_map/all_to_all | solution.py:318
  62.4 1.7 %gather.1 = bf16[448,256]{1,0:T(8,128)(2,1)} custom-call(bf16[448,256]{1,0:T(8,128)(2,1)} %bitcast.12), custom_call_target="tpu_custom_call" | custom-call | tf_op jit(solution)/shard_map/gather/pallas_call | solution.py:298
  64.1 11.8 %all_to_all.35 = bf16[8,56,256]{2,1,0:T(8,128)(2,1)S(1)} all-to-all(bf16[8,56,256]{2,1,0:T(8,128)(2,1)} %bitcast.13), channel_id=1, replica_groups={{0,2,4,6,8,10,12,14},{1,3,5,7,9,11,13,15},{16,18,20,22,24,26,28,30},{17..., dimensions={0} | all-to-all | bytes 458752 | tf_op jit(solution)/shard_map/all_to_all | solution.py:318
  75.9 0.0 copy-start
  75.9 0.0 collective-permute-start.3
  75.9 1.5 %collective-permute-done.3.other = bf16[448,256]{1,0:T(8,128)(2,1)S(1)} collective-permute-done((bf16[448,256]{1,0:T(8,128)(2,1)S(1)}, bf16[448,256]{1,0:T(8,128)(2,1)S(1)}, u32[]{:S(2)}, u32[]{:S(2)}) %collective-permute-start.3) | collective-permute-done | bytes 229408 | tf_op jit(solution)/shard_map/ppermute | solution.py:382
  77.4 0.0 copy-done
  77.4 0.0 copy-start.1
  77.4 0.7 copy-done.1
  78.1 2.0 %place.1 = (f32[256,256]{1,0:T(8,128)}, f32[256,256]{1,0:T(8,128)}, f32[32,64]{1,0:T(8,128)}, f32[1,32]{1,0:T(1,128)}, f32[256,256]{1,0:T(8,128)}) custom-call(bf16[448,256]{1,0:T(8,128)(2,1)} %bitcast.11, bf16[448,256]{1,0:T(8,128)(2,1)} %copy-done.1), custom_call_target="tpu_custom_call" | custom-call | tf_op jit(solution)/shard_map/place/pallas_call | solution.py:298
Async XLA Ops:
  6.7 1.6 %collective-permute-start = (f32[144,128]{1,0:T(8,128)}, f32[144,128]{1,0:T(8,128)S(1)}, u32[]{:S(2)}, u32[]{:S(2)}) collective-permute-start(f32[144,128]{1,0:T(8,128)} %get-tuple-element.29), channel_id=1, source_target_pairs={{0,1},{1,0},{2,3},{3,2},{4,5},{5,4},{6,7},{7,6},{8,9},{9,8},{10,11... | collective-permute-start | bytes 221192 | tf_op jit(solution)/shard_map/ppermute | solution.py:335
  8.3 0.6 copy-start.4
  32.9 1.6 %collective-permute-start.1 = (f32[168,256]{1,0:T(8,128)}, f32[168,256]{1,0:T(8,128)S(1)}, u32[]{:S(2)}, u32[]{:S(2)}) collective-permute-start(f32[168,256]{1,0:T(8,128)} %mix.1.mine), channel_id=1, source_target_pairs={{0,1},{1,0},{2,3},{3,2},{4,5},{5,4},{6,7},{7,6},{8,9},{9,8},{10,11... | collective-permute-start | bytes 516104 | tf_op jit(solution)/shard_map/ppermute | solution.py:341
  34.5 0.7 copy-start.3
  45.2 1.7 %collective-permute-start.2 = (bf16[448,256]{1,0:T(8,128)(2,1)}, bf16[448,256]{1,0:T(8,128)(2,1)S(1)}, u32[]{:S(2)}, u32[]{:S(2)}) collective-permute-start(bf16[448,256]{1,0:T(8,128)(2,1)} %get-tuple-element.33), channel_id=1, source_target_pairs={{0,1},{1,0},{2,3},{3,2},{4,5},{5,4},{6,7},{7,6},{8,9},{9,8},{10,11... | collective-permute-start | bytes 688136 | tf_op jit(solution)/shard_map/ppermute | solution.py:371
  46.9 0.7 copy-start.2
  75.9 1.5 %copy-start = (bf16[8,56,256]{2,1,0:T(8,128)(2,1)}, bf16[8,56,256]{2,1,0:T(8,128)(2,1)S(1)}, u32[]{:S(2)}) copy-start(bf16[8,56,256]{2,1,0:T(8,128)(2,1)S(1)} %all_to_all.35) | copy-start | bytes 688132
  75.9 1.5 %collective-permute-start.3 = (bf16[448,256]{1,0:T(8,128)(2,1)S(1)}, bf16[448,256]{1,0:T(8,128)(2,1)S(1)}, u32[]{:S(2)}, u32[]{:S(2)}) collective-permute-start(bf16[448,256]{1,0:T(8,128)(2,1)S(1)} %bitcast.10), channel_id=1, source_target_pairs={{0,1},{1,0},{2,3},{3,2},{4,5},{5,4},{6,7},{7,6},{8,9},{9,8},{10,11... | collective-permute-start | bytes 688136 | tf_op jit(solution)/shard_map/ppermute | solution.py:382
  77.4 0.7 copy-start.1

commit v2 on v1

--- a/solution.py
+++ b/solution.py
@@ -52,20 +52,40 @@
 
 
 def forward_kernel(
-    counts, cells, cot, w_x, w_fx, w_slice, w_temp, w_out,
-    weights, proj, fd, stats, keep, send,
-    wxt, wft, wsb,
+    counts, cells_hbm, cot_hbm, *refs,
 ):
+    hbm, refs = refs[:5], refs[5:]
+    (weights, proj, fd, stats, keep, send), refs = refs[:6], refs[6:]
+    cells, cot, w_x, w_fx, w_slice, w_temp, w_out, small, big, wxt, wft, wsb = refs
     core = lax.rem(lax.axis_index("dom"), 2)
     rows = cells.shape[0]
+    steps = rows // CHUNK
+
+    def load(source, target, slot, j):
+        at = pl.ds(pl.multiple_of(j * CHUNK, CHUNK), CHUNK)
+        return pltpu.make_async_copy(source.at[at, :], target.at[at, :], big.at[slot, j])
+
+    tables = [
+        pltpu.make_async_copy(source, target, small.at[i])
+        for i, (source, target) in enumerate(zip(hbm, (w_x, w_fx, w_slice, w_temp, w_out)))
+    ]
+    for table in tables:
+        table.start()
+    for j in range(steps):
+        load(cells_hbm, cells, 0, j).start()
+        load(cot_hbm, cot, 1, j).start()
+    for table in tables:
+        table.wait()
+    wtb = temp_blocks(w_temp[...])
     wxt[...] = w_x[...].T
     wft[...] = w_fx[...].T
     wsb[...] = slice_blocks(w_slice[...]).T.astype(BF16)
-    wtb = temp_blocks(w_temp[...])
     count = counts[0]
 
     def chunk(j, carry):
         at = pl.ds(pl.multiple_of(j * CHUNK, CHUNK), CHUNK)
+        load(cells_hbm, cells, 0, j).wait()
+        load(cot_hbm, cot, 1, j).wait()
         c = cells[at, :]
         projected = nt(wxt[...], c).astype(BF16)
         proj[:, at] = projected
@@ -166,9 +186,9 @@
 
 def backward_kernel(
     scale,
-    cells, cot, weights, proj, fd, stats, mine, other, w_x, w_fx, w_slice, w_temp, w_out,
-    result, grad_cells, keep, send, grad_qkv,
-    hid, dpf, dlog, dtemp, lhs_h, lhs_w, dden, wsb, wsd, wxf, wot,
+    cells, cot, weights, proj, fd, stats, mine, other, w_slice, w_temp,
+    hid, dpf, keep, send, grad_qkv,
+    dlog, dtemp, lhs_h, lhs_w, dden, wsb, wsd,
 ):
     core = lax.rem(lax.axis_index("dom"), 2)
     rows = cells.shape[0]
@@ -177,9 +197,6 @@
     wsd[...] = blocks.astype(BF16)
     wsb[...] = blocks.T.astype(BF16)
     wtb = temp_blocks(w_temp[...]).astype(F32).T
-    wxf[:, 0:WIDTH] = w_x[...]
-    wxf[:, WIDTH : 2 * WIDTH] = w_fx[...]
-    wot[...] = w_out[...].T
     diag64 = iota((256, 256), 0) // 64 == iota((256, 256), 1) // 64
     diag32 = iota((128, 256), 0) // 32 == iota((128, 256), 1) // 64
     for g in range(2):
@@ -230,10 +247,6 @@
                 outer.append(wtb[HEAD * h : HEAD * h + HEAD, h : h + 1] * dt)
             dp = nn(wsd[...], dlog[wide, at]) + jnp.concatenate(outer, axis=0)
             dpf[half, at] = dp.astype(BF16)
-        gct = nn(wxf[...], dpf[:, at])
-        grad_cells[at, :] = gct.T.astype(BF16)
-        rst = nn(wot[...], hid[:, at])
-        result[at, :] = rst.T.astype(BF16)
         return carry
 
     lax.fori_loop(0, rows // CHUNK, chunk, 0)
@@ -264,6 +277,31 @@
         ref[400:, :] = jnp.zeros((ref.shape[0] - 400, WIDTH), BF16)
 
 
+def write_rows(out, stage, sems, product):
+    copies = []
+    for j in range(out.shape[0] // CHUNK):
+        at = pl.ds(j * CHUNK, CHUNK)
+        stage[at, :] = product(at).T.astype(BF16)
+        copies.append(pltpu.make_async_copy(stage.at[at, :], out.at[at, :], sems.at[j]))
+        copies[-1].start()
+    for copy in copies:
+        copy.wait()
+
+
+def result_kernel(hid, w_out, out, stage, sems):
+    table = w_out[...].T
+    write_rows(out, stage, sems, lambda at: nn(table, hid[:, at]))
+
+
+def grad_cells_kernel(dpf, w_x, w_fx, out, stage, sems):
+    write_rows(
+        out,
+        stage,
+        sems,
+        lambda at: nn(w_x[...], dpf[0:WIDTH, at]) + nn(w_fx[...], dpf[WIDTH : 2 * WIDTH, at]),
+    )
+
+
 def add_kernel(mine, other, out):
     out[...] = (mine[...].astype(F32) + other[...].astype(F32)).astype(BF16)
 
@@ -292,16 +330,21 @@
 
 VMEM = pl.BlockSpec(memory_space=pltpu.VMEM)
 SMEM = pl.BlockSpec(memory_space=pltpu.SMEM)
-
-
-def call(kernel, shapes, args, scratch=(), scalars=0, name=None):
+HBM = pl.BlockSpec(memory_space=pltpu.HBM)
+
+
+def call(kernel, shapes, args, scratch=(), name=None, ins=None, outs=None, flops=0):
+    scratch = [pltpu.VMEM(*s) if isinstance(s, tuple) else s for s in scratch]
+    estimate = pl.CostEstimate(flops=flops, bytes_accessed=0, transcendentals=0)
     return pl.pallas_call(
         kernel,
         out_shape=[jax.ShapeDtypeStruct(s, d) for s, d in shapes],
-        in_specs=[SMEM] * scalars + [VMEM] * (len(args) - scalars),
-        out_specs=[VMEM] * len(shapes),
-        scratch_shapes=[pltpu.VMEM(s, d) for s, d in scratch],
+        in_specs=ins or [VMEM] * len(args),
+        out_specs=outs or [VMEM] * len(shapes),
+        scratch_shapes=scratch,
         name=name,
+        cost_estimate=estimate if flops else None,
+        compiler_params=pltpu.CompilerParams(vmem_limit_bytes=24 << 20),
     )(*args)
 
 
@@ -327,9 +370,26 @@
             ((ROWS1, 128), F32),
             ((ROWS1, 128), F32),
         ],
-        (counts, cells, cotangent, w_x, w_fx, w_slice, temp, w_out),
-        scratch=[((256, 256), BF16), ((256, 256), BF16), ((256, 128), BF16)],
-        scalars=1,
+        (counts,)
+        + tuple(
+            pltpu.with_memory_space_constraint(x, pltpu.HBM)
+            for x in (cells, cotangent, w_x, w_fx, w_slice, temp, w_out)
+        ),
+        scratch=[
+            ((rows, WIDTH), BF16),
+            ((rows, WIDTH), BF16),
+            ((WIDTH, WIDTH), BF16),
+            ((WIDTH, WIDTH), BF16),
+            ((HEAD, SLICES), BF16),
+            ((1, HEAD), BF16),
+            ((WIDTH, WIDTH), BF16),
+            pltpu.SemaphoreType.DMA((5,)),
+            pltpu.SemaphoreType.DMA((2, rows // CHUNK)),
+            ((256, 256), BF16),
+            ((256, 256), BF16),
+            ((256, 128), BF16),
+        ],
+        ins=[SMEM] + [HBM] * 7,
         name="forward",
     )
     other = lax.ppermute(send, "dom", pairs)
@@ -342,20 +402,17 @@
     chunk = -(-400 // peers)
     chunk = -(-chunk // 8) * 8
     half = chunk * peers
-    result, grad_cells, keep, send, grad_qkv = call(
+    hid, dpf, keep, send, grad_qkv = call(
         functools.partial(backward_kernel, scale),
         [
-            ((rows, WIDTH), BF16),
-            ((rows, WIDTH), BF16),
+            ((WIDTH, rows), BF16),
+            ((2 * WIDTH, rows), BF16),
             ((half, WIDTH), BF16),
             ((half, WIDTH), BF16),
             ((3, HEAD, HEAD), F32),
         ],
-        (cells, cotangent, weights, proj, fd, stats, mine, other)
-        + (w_x, w_fx, w_slice, temp, w_out),
+        (cells, cotangent, weights, proj, fd, stats, mine, other, w_slice, temp),
         scratch=[
-            ((WIDTH, rows), BF16),
-            ((2 * WIDTH, rows), BF16),
             ((hm, rows), BF16),
             ((8, rows), F32),
             ((2, 256, 256), BF16),
@@ -363,12 +420,30 @@
             ((hm, CHUNK), F32),
             ((256, 128), BF16),
             ((128, 256), BF16),
-            ((256, 512), BF16),
-            ((256, 256), BF16),
         ],
         name="backward",
     )
     other = lax.ppermute(send, "dom", pairs)
+    staging = [((rows, WIDTH), BF16), pltpu.SemaphoreType.DMA((rows // CHUNK,))]
+    (result,) = call(
+        result_kernel,
+        [((rows, WIDTH), BF16)],
+        (hid, w_out),
+        scratch=staging,
+        outs=[HBM],
+        name="result",
+        flops=2 * rows * WIDTH * WIDTH,
+    )
+    other, result = lax.optimization_barrier((other, result))
+    (grad_cells,) = call(
+        grad_cells_kernel,
+        [((rows, WIDTH), BF16)],
+        (dpf, w_x, w_fx),
+        scratch=staging,
+        outs=[HBM],
+        name="grad_cells",
+        flops=4 * rows * WIDTH * WIDTH,
+    )
     (summed,) = call(add_kernel, [((half, WIDTH), BF16)], (keep, other), name="pair_add")
     parts = exchange(summed)
 

time: 80.7 us -> 62.9 us (0.78)
  Pallas kernels: 26.9 us -> 16.4 us
  waiting for transfers between devices: 5.79 us -> 2.71 us
  blocking collectives: 42.8 us -> 40.7 us
  local copies, waits for them, and re-layouts: 2.68 us -> 0.68 us
    pallas_call x7 -> x9, Pallas kernels: 26.9 us -> 16.4 us  [call(): pl.pallas_call(kernel, out_shape=[jax.ShapeDtypeStruct(s, d) for s, d in...]
    all_to_all x3, blocking collectives: 42.8 us -> 40.7 us  [exchange(): return lax.all_to_all(x, 'dom', 0, 0, axis_index_groups=groups, tiled=True)]
    unnamed x10 -> x16, local copies, waits for them, and re-layouts: 2.68 us -> 0.68 us
    ppermute x2, waiting for transfers between devices: 2.69 us -> 1.1 us  [body(): other = lax.ppermute(send, 'dom', pairs)]
    ppermute x2, waiting for transfers between devices: 3.1 us -> 1.61 us  [body(): other = lax.ppermute(mine, 'dom', pairs)]
  transfers between devices with their start and end apart: 4 -> 4, of which waited for: 4 -> 4; matrix products, arithmetic and copies ran while one was open for 0% -> 0% of each run, Pallas kernels for 0% -> 4%
where the time goes in v2:
time: 62.9 us; the launch traced here: 62.6 us
  blocking collectives  40.7 us (65%)
  Pallas kernels  16.4 us (26%)
  waiting for transfers between devices  2.71 us (4%)
  between operations  1.37 us (2%)
  starting transfers between devices  0.8 us (1%)
  local copies, waits for them, and re-layouts  0.68 us (1%)
    all_to_all x3, blocking collectives, exchange(): return lax.all_to_all(x, 'dom', 0, 0, axis_index_groups=groups, tiled=True)  40.7 us
    pallas_call x9, Pallas kernels, call(): pl.pallas_call(kernel, out_shape=[jax.ShapeDtypeStruct(s, d) for s, d in...  16.4 us
    ppermute x2, waiting for transfers between devices, body(): other = lax.ppermute(mine, 'dom', pairs)  1.61 us
  transfers between devices with their start and end apart: 4, of which 4 were waited for; matrix products, arithmetic and copies ran while one was open for 0% of the time, Pallas kernels for 4%

profile of v2, /device:TPU:0, one launch (start us, length us, event | category | flops | bytes accessed | tf_op | source)
XLA Modules:
  0.0 62.6 jit_solution(1527711785676345002)
XLA Ops:
  1.3 4.7 %forward.1 = (bf16[512,1024]{1,0:T(8,128)(2,1)S(1)}, bf16[256,1024]{1,0:T(8,128)(2,1)S(1)}, bf16[512,1024]{1,0:T(8,128)(2,1)S(1)}, f32[32,1024]{1,0:T(8,128)S(1)...) custom-call(s32[1]{0:T(128)S(6)} %copy.17.counts, bf16[1024,256]{1,0:T(8,128)(2,1)} %cells.1, bf16[1024,256]{1,0:T(8,128)(2,1)} %cot.1, ...), custom_call_target="tpu_custom_call" | custom-call | tf_op jit(solution)/shard_map/forward/pallas_call | solution.py:339
  6.0 0.6 collective-permute-start
  6.5 0.9 %collective-permute-done.other = f32[144,128]{1,0:T(8,128)S(1)} collective-permute-done((f32[144,128]{1,0:T(8,128)S(1)}, f32[144,128]{1,0:T(8,128)S(1)}, u32[]{:S(2)}, u32[]{:S(2)}) %collective-permute-start) | collective-permute-done | bytes 73760 | tf_op jit(solution)/shard_map/ppermute | solution.py:395
  7.4 0.0 copy-start.6
  7.5 0.0 copy-start
  7.5 0.0 copy-start.1
  7.5 17.8 %all_to_all.33 = bf16[8,144,128]{2,1,0:T(8,128)(2,1)S(1)} all-to-all(bf16[8,144,128]{2,1,0:T(8,128)(2,1)S(1)} %bitcast.8), channel_id=1, replica_groups={{0,2,4,6,8,10,12,14},{1,3,5,7,9,11,13,15},{16,18,20,22,24,26,28,30},{17..., dimensions={0} | all-to-all | bytes 589824 | tf_op jit(solution)/shard_map/all_to_all | solution.py:361
  25.2 0.0 copy-done.6
  25.3 0.0 copy-start.5
  25.3 2.7 %mix.1.mine = f32[168,256]{1,0:T(8,128)S(1)} custom-call(bf16[1152,128]{1,0:T(8,128)(2,1)S(1)} %bitcast.9, bf16[3,32,32]{2,1,0:T(8,128)(2,1)S(1)} %copy-done.6), custom_call_target="tpu_custom_call" | custom-call | tf_op jit(solution)/shard_map/mix/pallas_call | solution.py:339
  27.9 0.0 collective-permute-start.1
  28.0 1.4 %collective-permute-done.1.other = f32[168,256]{1,0:T(8,128)S(1)} collective-permute-done((f32[168,256]{1,0:T(8,128)S(1)}, f32[168,256]{1,0:T(8,128)S(1)}, u32[]{:S(2)}, u32[]{:S(2)}) %collective-permute-start.1) | collective-permute-done | bytes 172064 | tf_op jit(solution)/shard_map/ppermute | solution.py:401
  29.4 0.0 copy-done
  29.4 0.0 copy-done.1
  29.4 0.0 copy-done.5
  29.4 0.6 %copy-done.7 = bf16[32]{0:T(256)(128)(2,1)S(1)} copy-done((bf16[32]{0:T(256)(128)(2,1)S(1)}, bf16[32]{0:T(256)(128)(2,1)}, u32[]{:S(2)}) %copy-start.7) | copy-done | bytes 88
  30.0 5.5 %backward.1 = (bf16[256,1024]{1,0:T(8,128)(2,1)S(1)}, bf16[512,1024]{1,0:T(8,128)(2,1)S(1)}, bf16[448,256]{1,0:T(8,128)(2,1)S(1)}, bf16[448,256]{1,0:T(8,128)(2,1)S(1)}, f32[3,32,32]{2,1,0:T(8,128)}) custom-call(bf16[1024,256]{1,0:T(8,128)(2,1)S(1)} %copy-done, bf16[1024,256]{1,0:T(8,128)(2,1)S(1)} %copy-done.1, ...), custom_call_target="tpu_custom_call" | custom-call | tf_op jit(solution)/shard_map/backward/pallas_call | solution.py:339
  35.6 0.2 collective-permute-start.2
  35.8 0.0 copy-done.4
  35.8 1.1 %result.1 = bf16[1024,256]{1,0:T(8,128)(2,1)} custom-call(bf16[256,1024]{1,0:T(8,128)(2,1)S(1)} %get-tuple-element.33.hid, bf16[256,256]{1,0:T(8,128)(2,1)S(1)} %copy-done.4), custom_call_target="tpu_custom_call" | custom-call | flops 134217728 | tf_op jit(solution)/shard_map/result/pallas_call | solution.py:339
  36.9 0.2 collective-permute-done.2.other
  37.1 0.1 pair_add.1
  37.2 11.5 %all_to_all.34 = bf16[8,56,256]{2,1,0:T(8,128)(2,1)S(1)} all-to-all(bf16[8,56,256]{2,1,0:T(8,128)(2,1)S(1)} %bitcast.14), channel_id=1, replica_groups={{0,2,4,6,8,10,12,14},{1,3,5,7,9,11,13,15},{16,18,20,22,24,26,28,30},{17..., dimensions={0} | all-to-all | bytes 458752 | tf_op jit(solution)/shard_map/all_to_all | solution.py:361
  48.7 0.0 copy-start.2
  48.7 0.0 copy-start.3
  48.7 11.4 %all_to_all.35 = bf16[8,56,256]{2,1,0:T(8,128)(2,1)S(1)} all-to-all(bf16[8,56,256]{2,1,0:T(8,128)(2,1)S(1)} %bitcast.13), channel_id=1, replica_groups={{0,2,4,6,8,10,12,14},{1,3,5,7,9,11,13,15},{16,18,20,22,24,26,28,30},{17..., dimensions={0} | all-to-all | bytes 458752 | tf_op jit(solution)/shard_map/all_to_all | solution.py:361
  60.2 0.0 collective-permute-start.3
  60.2 0.0 copy-done.2
  60.2 0.0 copy-done.3
  60.2 1.3 %grad_cells.1 = bf16[1024,256]{1,0:T(8,128)(2,1)} custom-call(bf16[512,1024]{1,0:T(8,128)(2,1)S(1)} %get-tuple-element.35.dpf, bf16[256,256]{1,0:T(8,128)(2,1)S(1)} %copy-done.2, bf16[256,256]{1,0:T(8,128)(2,1)S(1)} %copy-done.3), custom_call_target="tpu_custom_call" | custom-call | flops 268435456 | tf_op jit(solution)/shard_map/grad_cells/pallas_call | solution.py:339
  61.4 0.2 collective-permute-done.3.other
  61.6 1.0 %place.1 = (f32[256,256]{1,0:T(8,128)}, f32[256,256]{1,0:T(8,128)}, f32[32,64]{1,0:T(8,128)}, f32[1,32]{1,0:T(1,128)}, f32[256,256]{1,0:T(8,128)}) custom-call(bf16[448,256]{1,0:T(8,128)(2,1)S(1)} %bitcast.11, bf16[448,256]{1,0:T(8,128)(2,1)S(1)} %collective-permute-done.3.other), custom_call_target="tpu_custom_call" | custom-call | tf_op jit(solution)/shard_map/place/pallas_call | solution.py:339
  (4 shorter events, 0.1 us)
Async XLA Ops:
  6.0 1.5 %collective-permute-start = (f32[144,128]{1,0:T(8,128)S(1)}, f32[144,128]{1,0:T(8,128)S(1)}, u32[]{:S(2)}, u32[]{:S(2)}) collective-permute-start(f32[144,128]{1,0:T(8,128)S(1)} %get-tuple-element.31), channel_id=1, source_target_pairs={{0,1},{1,0},{2,3},{3,2},{4,5},{5,4},{6,7},{7,6},{8,9},{9,8},{10,11... | collective-permute-start | bytes 221192 | tf_op jit(solution)/shard_map/ppermute | solution.py:395
  7.4 17.8 %copy-start.6 = (bf16[3,32,32]{2,1,0:T(8,128)(2,1)S(1)}, bf16[3,32,32]{2,1,0:T(8,128)(2,1)}, u32[]{:S(2)}) copy-start(bf16[3,32,32]{2,1,0:T(8,128)(2,1)} %w_qkv.1) | copy-start | bytes 18436
  7.5 21.9 %copy-start = (bf16[1024,256]{1,0:T(8,128)(2,1)S(1)}, bf16[1024,256]{1,0:T(8,128)(2,1)}, u32[]{:S(2)}) copy-start(bf16[1024,256]{1,0:T(8,128)(2,1)} %cells.1) | copy-start | bytes 1572868
  7.5 21.9 %copy-start.1 = (bf16[1024,256]{1,0:T(8,128)(2,1)S(1)}, bf16[1024,256]{1,0:T(8,128)(2,1)}, u32[]{:S(2)}) copy-start(bf16[1024,256]{1,0:T(8,128)(2,1)} %cot.1) | copy-start | bytes 1572868
  25.3 4.1 %copy-start.5 = (bf16[32,64]{1,0:T(8,128)(2,1)S(1)}, bf16[32,64]{1,0:T(8,128)(2,1)}, u32[]{:S(2)}) copy-start(bf16[32,64]{1,0:T(8,128)(2,1)} %w_slice.1) | copy-start | bytes 12292
  27.9 1.4 %collective-permute-start.1 = (f32[168,256]{1,0:T(8,128)S(1)}, f32[168,256]{1,0:T(8,128)S(1)}, u32[]{:S(2)}, u32[]{:S(2)}) collective-permute-start(f32[168,256]{1,0:T(8,128)S(1)} %mix.1.mine), channel_id=1, source_target_pairs={{0,1},{1,0},{2,3},{3,2},{4,5},{5,4},{6,7},{7,6},{8,9},{9,8},{10,11... | collective-permute-start | bytes 516104 | tf_op jit(solution)/shard_map/ppermute | solution.py:401
  29.4 0.7 %copy-start.7 = (bf16[32]{0:T(256)(128)(2,1)S(1)}, bf16[32]{0:T(256)(128)(2,1)}, u32[]{:S(2)}) copy-start(bf16[32]{0:T(256)(128)(2,1)} %param.14) | copy-start | bytes 196
  30.0 5.7 %copy-start.4 = (bf16[256,256]{1,0:T(8,128)(2,1)S(1)}, bf16[256,256]{1,0:T(8,128)(2,1)}, u32[]{:S(2)}) copy-start(bf16[256,256]{1,0:T(8,128)(2,1)} %w_out.1) | copy-start | bytes 393220
  35.6 1.5 %collective-permute-start.2 = (bf16[448,256]{1,0:T(8,128)(2,1)S(1)}, bf16[448,256]{1,0:T(8,128)(2,1)S(1)}, u32[]{:S(2)}, u32[]{:S(2)}) collective-permute-start(bf16[448,256]{1,0:T(8,128)(2,1)S(1)} %get-tuple-element.32), channel_id=1, source_target_pairs={{0,1},{1,0},{2,3},{3,2},{4,5},{5,4},{6,7},{7,6},{8,9},{9,8},{10,11... | collective-permute-start | bytes 688136 | tf_op jit(solution)/shard_map/ppermute | solution.py:426
  48.7 11.5 %copy-start.2 = (bf16[256,256]{1,0:T(8,128)(2,1)S(1)}, bf16[256,256]{1,0:T(8,128)(2,1)}, u32[]{:S(2)}) copy-start(bf16[256,256]{1,0:T(8,128)(2,1)} %w_x.1) | copy-start | bytes 393220
  48.7 11.5 %copy-start.3 = (bf16[256,256]{1,0:T(8,128)(2,1)S(1)}, bf16[256,256]{1,0:T(8,128)(2,1)}, u32[]{:S(2)}) copy-start(bf16[256,256]{1,0:T(8,128)(2,1)} %w_fx.1) | copy-start | bytes 393220
  60.2 1.5 %collective-permute-start.3 = (bf16[448,256]{1,0:T(8,128)(2,1)S(1)}, bf16[448,256]{1,0:T(8,128)(2,1)S(1)}, u32[]{:S(2)}, u32[]{:S(2)}) collective-permute-start(bf16[448,256]{1,0:T(8,128)(2,1)S(1)} %bitcast.10), channel_id=1, source_target_pairs={{0,1},{1,0},{2,3},{3,2},{4,5},{5,4},{6,7},{7,6},{8,9},{9,8},{10,11... | collective-permute-start | bytes 688136 | tf_op jit(solution)/shard_map/ppermute | solution.py:457

commit v3 on v2

--- a/solution.py
+++ b/solution.py
@@ -17,7 +17,7 @@
 WIDTH = HEADS * HEAD
 ROWS1 = 144
 LOG2E = math.log2(math.e)
-CHUNK = 256
+CHUNK = 512
 
 
 def nn(a, b, precision=None):
@@ -55,8 +55,8 @@
     counts, cells_hbm, cot_hbm, *refs,
 ):
     hbm, refs = refs[:5], refs[5:]
-    (weights, proj, fd, stats, keep, send), refs = refs[:6], refs[6:]
-    cells, cot, w_x, w_fx, w_slice, w_temp, w_out, small, big, wxt, wft, wsb = refs
+    (weights, proj, fd, stats, keep, send, wsb, wsd, wtc), refs = refs[:9], refs[9:]
+    cells, cot, w_x, w_fx, w_out, w_slice, w_temp, small, big, wxt, wft = refs
     core = lax.rem(lax.axis_index("dom"), 2)
     rows = cells.shape[0]
     steps = rows // CHUNK
@@ -79,7 +79,10 @@
     wtb = temp_blocks(w_temp[...])
     wxt[...] = w_x[...].T
     wft[...] = w_fx[...].T
-    wsb[...] = slice_blocks(w_slice[...]).T.astype(BF16)
+    slices = slice_blocks(w_slice[...])
+    wsd[...] = slices.astype(BF16)
+    wsb[...] = slices.T.astype(BF16)
+    wtc[...] = wtb.astype(F32).T
     count = counts[0]
 
     def chunk(j, carry):
@@ -136,11 +139,26 @@
     send[...] = jnp.where(core == 0, halves[1], halves[0])
 
 
-def spread_kernel(mine, other, out):
-    total = (mine[...] + other[...]).astype(BF16)
-    n = mine.shape[0]
-    for k in range(out.shape[0] // n):
-        out[n * k : n * k + n, :] = total
+def narrow_add_kernel(mine, other, out):
+    out[...] = (mine[...].astype(F32) + other[...].astype(F32)).astype(BF16)
+
+
+def softmax_kernel(proj, stats, wsb, tanhs, soft):
+    def chunk(j, carry):
+        at = pl.ds(pl.multiple_of(j * CHUNK, CHUNK), CHUNK)
+        a = stats[0:8, at]
+        norm = stats[24:32, at]
+        for g in range(2):
+            x = nn(wsb[...], proj[128 * g : 128 * g + 128, at])
+            for k in range(4):
+                h = 4 * g + k
+                rng = slice(SLICES * h, SLICES * h + SLICES)
+                t = jnp.tanh(x[SLICES * k : SLICES * k + SLICES] * 0.1)
+                tanhs[rng, at] = t
+                soft[rng, at] = jnp.exp2(t * a[h : h + 1]) * norm[h : h + 1]
+        return carry
+
+    lax.fori_loop(0, proj.shape[1] // CHUNK, chunk, 0)
 
 
 def sum_blocks(ref, n):
@@ -150,8 +168,9 @@
     return total
 
 
-def mix_kernel(parts, w_qkv, out):
-    total = sum_blocks(parts, ROWS1)
+def mix_kernel(w_qkv, *refs):
+    parts, out = refs[:-1], refs[-1]
+    total = sum(part[...].astype(F32) for part in parts)
     numer = jnp.concatenate([total[0:32], total[64:96]], axis=1)
     d_mixed = jnp.concatenate([total[32:64], total[96:128]], axis=1)
     denom = jnp.concatenate([total[128:129], total[129:130]], axis=1) + 1e-05
@@ -180,23 +199,19 @@
     out[32:64, :] = mixed.astype(BF16).astype(F32)
     out[64:72, :] = jnp.broadcast_to(d_denom, (8, 256))
     for k in range(3):
-        out[72 + 32 * k : 104 + 32 * k, 0:32] = nt(tokens, grads[k], HIGHEST)
-        out[72 + 32 * k : 104 + 32 * k, 32:256] = jnp.zeros((32, 224), F32)
+        out[72:104, 32 * k : 32 * k + 32] = nt(tokens, grads[k], HIGHEST)
+    out[72:104, 96:256] = jnp.zeros((32, 160), F32)
 
 
 def backward_kernel(
     scale,
-    cells, cot, weights, proj, fd, stats, mine, other, w_slice, w_temp,
+    cells, cot, weights, proj, fd, stats, tanhs, softs, mine, other, wsd, wtc,
     hid, dpf, keep, send, grad_qkv,
-    dlog, dtemp, lhs_h, lhs_w, dden, wsb, wsd,
+    dlog, dtemp, lhs_h, lhs_w, dden,
 ):
     core = lax.rem(lax.axis_index("dom"), 2)
     rows = cells.shape[0]
     lower = core == 0
-    blocks = slice_blocks(w_slice[...])
-    wsd[...] = blocks.astype(BF16)
-    wsb[...] = blocks.T.astype(BF16)
-    wtb = temp_blocks(w_temp[...]).astype(F32).T
     diag64 = iota((256, 256), 0) // 64 == iota((256, 256), 1) // 64
     diag32 = iota((128, 256), 0) // 32 == iota((128, 256), 1) // 64
     for g in range(2):
@@ -212,15 +227,13 @@
         column = e[64:72].T[:, 0:1]
         dden[256 * g : 256 * g + 256, :] = jnp.broadcast_to(column, (256, CHUNK))
     for k in range(3):
-        block = slice(72 + 32 * k, 104 + 32 * k)
-        grad_qkv[k] = (mine[block, 0:32] + other[block, 0:32]) * scale
+        block = slice(32 * k, 32 * k + 32)
+        grad_qkv[k] = (mine[72:104, block] + other[72:104, block]) * scale
 
     def chunk(j, carry):
         at = pl.ds(pl.multiple_of(j * CHUNK, CHUNK), CHUNK)
-        a = stats[0:8, at]
         inv = stats[8:16, at]
         slope = stats[16:24, at]
-        norm = stats[24:32, at]
         for g in range(2):
             half = slice(128 * g, 128 * g + 128)
             wide = slice(256 * g, 256 * g + 256)
@@ -228,15 +241,14 @@
             hid[half, at] = hf[0:128].astype(BF16)
             dpf[WIDTH + 128 * g : WIDTH + 128 * g + 128, at] = hf[128:256].astype(BF16)
             dw = nn(lhs_w[g], fd[wide, at])
-            x = nn(wsb[...], proj[half, at])
             outer = []
             for k in range(4):
                 h = 4 * g + k
                 sub = slice(SLICES * k, SLICES * k + SLICES)
                 rng = slice(SLICES * h, SLICES * h + SLICES)
                 one = slice(h, h + 1)
-                t = jnp.tanh(x[sub] * 0.1)
-                soft = jnp.exp2(t * a[one]) * norm[one]
+                t = tanhs[rng, at]
+                soft = softs[rng, at]
                 d = dw[sub] + dden[rng, :]
                 inner = jnp.sum(soft * d, axis=0, keepdims=True)
                 ds = soft * (d - inner)
@@ -244,7 +256,7 @@
                 dt = jnp.sum(ds * t, axis=0, keepdims=True) * slope[one]
                 dt = dt.astype(BF16).astype(F32)
                 dtemp[one, at] = dt
-                outer.append(wtb[HEAD * h : HEAD * h + HEAD, h : h + 1] * dt)
+                outer.append(wtc[HEAD * h : HEAD * h + HEAD, h : h + 1] * dt)
             dp = nn(wsd[...], dlog[wide, at]) + jnp.concatenate(outer, axis=0)
             dpf[half, at] = dp.astype(BF16)
         return carry
@@ -302,10 +314,6 @@
     )
 
 
-def add_kernel(mine, other, out):
-    out[...] = (mine[...].astype(F32) + other[...].astype(F32)).astype(BF16)
-
-
 def place_kernel(mine, other, d_x, d_fx, d_slice, d_temp, d_out):
     core = lax.rem(lax.axis_index("dom"), 2)
     lower = core == 0
@@ -351,16 +359,18 @@
 def body(devices, cells, counts, w_x, w_fx, w_slice, w_temp, w_qkv, w_out, cotangent):
     rows = cells.shape[0]
     peers = devices // 2
-    pairs = [(i, i ^ 1) for i in range(devices)]
     groups = [list(range(c, devices, 2)) for c in range(2)]
     scale = 1.0 / math.sqrt(rows * devices)
     temp = w_temp.reshape(1, HEAD)
     hm = HEADS * SLICES
 
+    def swap(x, mask):
+        return lax.ppermute(x, "dom", [(i, i ^ mask) for i in range(devices)])
+
     def exchange(x):
         return lax.all_to_all(x, "dom", 0, 0, axis_index_groups=groups, tiled=True)
 
-    weights, proj, fd, stats, keep, send = call(
+    local = call(
         forward_kernel,
         [
             ((hm, rows), BF16),
@@ -369,6 +379,14 @@
             ((32, rows), F32),
             ((ROWS1, 128), F32),
             ((ROWS1, 128), F32),
+            ((256, 128), BF16),
+            ((128, 256), BF16),
+            ((WIDTH, HEADS), F32),
+            ((rows, WIDTH), BF16),
+            ((rows, WIDTH), BF16),
+            ((WIDTH, WIDTH), BF16),
+            ((WIDTH, WIDTH), BF16),
+            ((WIDTH, WIDTH), BF16),
         ],
         (counts,)
         + tuple(
@@ -376,29 +394,39 @@
             for x in (cells, cotangent, w_x, w_fx, w_slice, temp, w_out)
         ),
         scratch=[
-            ((rows, WIDTH), BF16),
-            ((rows, WIDTH), BF16),
-            ((WIDTH, WIDTH), BF16),
-            ((WIDTH, WIDTH), BF16),
             ((HEAD, SLICES), BF16),
             ((1, HEAD), BF16),
-            ((WIDTH, WIDTH), BF16),
             pltpu.SemaphoreType.DMA((5,)),
             pltpu.SemaphoreType.DMA((2, rows // CHUNK)),
             ((256, 256), BF16),
             ((256, 256), BF16),
-            ((256, 128), BF16),
         ],
         ins=[SMEM] + [HBM] * 7,
         name="forward",
     )
-    other = lax.ppermute(send, "dom", pairs)
-    (spread,) = call(
-        spread_kernel, [((peers * ROWS1, 128), BF16)], (keep, other), name="spread"
-    )
-    parts = exchange(spread)
-    (mine,) = call(mix_kernel, [((168, 256), F32)], (parts, w_qkv), name="mix")
-    other = lax.ppermute(mine, "dom", pairs)
+    weights, proj, fd, stats, keep, send, wsb, wsd, wtc = local[:9]
+    cells, cotangent, w_x, w_fx, w_out = local[9:]
+    other = swap(send, 1)
+    part = ((ROWS1, 128), BF16)
+    (total,) = call(narrow_add_kernel, [part], (keep, other), name="narrow")
+    near = [2**b for b in range(1, devices.bit_length() - 3)]
+    far = [devices // 4 * k for k in (1, 2, 3)]
+    tanhs = softs = None
+    for mask in near:
+        other = swap(total, mask)
+        if tanhs is None:
+            tanhs, softs = call(
+                softmax_kernel,
+                [((hm, rows), F32)] * 2,
+                (proj, stats, wsb),
+                name="softmax",
+                flops=2 * rows * hm * 128,
+            )
+            other, tanhs, softs = lax.optimization_barrier((other, tanhs, softs))
+        (total,) = call(narrow_add_kernel, [part], (total, other), name="near")
+    parts = [total] + [swap(total, mask) for mask in far]
+    (mine,) = call(mix_kernel, [((104, 256), F32)], (w_qkv, *parts), name="mix")
+    other = swap(mine, 1)
     chunk = -(-400 // peers)
     chunk = -(-chunk // 8) * 8
     half = chunk * peers
@@ -411,19 +439,17 @@
             ((half, WIDTH), BF16),
             ((3, HEAD, HEAD), F32),
         ],
-        (cells, cotangent, weights, proj, fd, stats, mine, other, w_slice, temp),
+        (cells, cotangent, weights, proj, fd, stats, tanhs, softs, mine, other, wsd, wtc),
         scratch=[
             ((hm, rows), BF16),
             ((8, rows), F32),
             ((2, 256, 256), BF16),
             ((2, 256, 256), BF16),
             ((hm, CHUNK), F32),
-            ((256, 128), BF16),
-            ((128, 256), BF16),
         ],
         name="backward",
     )
-    other = lax.ppermute(send, "dom", pairs)
+    other = swap(send, 1)
     staging = [((rows, WIDTH), BF16), pltpu.SemaphoreType.DMA((rows // CHUNK,))]
     (result,) = call(
         result_kernel,
@@ -444,7 +470,7 @@
         name="grad_cells",
         flops=4 * rows * WIDTH * WIDTH,
     )
-    (summed,) = call(add_kernel, [((half, WIDTH), BF16)], (keep, other), name="pair_add")
+    (summed,) = call(narrow_add_kernel, [((half, WIDTH), BF16)], (keep, other), name="pair_add")
     parts = exchange(summed)
 
     def gather(parts_ref, out):
@@ -454,7 +480,7 @@
 
     (spread,) = call(gather, [((half, WIDTH), BF16)], (parts,), name="gather")
     mine = exchange(spread)
-    other = lax.ppermute(mine, "dom", pairs)
+    other = swap(mine, 1)
     d_x, d_fx, d_slice, d_temp, d_out = call(
         place_kernel,
         [

time: 62.9 us -> 56.9 us (0.905)
  blocking collectives: 40.7 us -> 24.1 us
  starting transfers between devices: 0.8 us -> 8.54 us
  waiting for transfers between devices: 2.71 us -> 7.93 us
  Pallas kernels: 16.4 us -> 14.7 us
  local copies, waits for them, and re-layouts: 0.68 us -> 0.01 us
    all_to_all x3 -> x2, blocking collectives: 40.7 us -> 24.1 us  [exchange(): return lax.all_to_all(x, 'dom', 0, 0, axis_index_groups=groups, tiled=True)]
    ppermute x4 -> x8, starting transfers between devices: 0.8 us -> 8.54 us  [swap(): return lax.ppermute(x, 'dom', [(i, i ^ mask) for i in range(devices)])]
    ppermute x4 -> x8, waiting for transfers between devices: 2.71 us -> 7.93 us  [swap(): return lax.ppermute(x, 'dom', [(i, i ^ mask) for i in range(devices)])]
    pallas_call x9 -> x11, Pallas kernels: 16.4 us -> 14.7 us  [call(): pl.pallas_call(kernel, out_shape=[jax.ShapeDtypeStruct(s, d) for s, d in...]
    unnamed x16 -> x2, local copies, waits for them, and re-layouts: 0.68 us -> 0.01 us
  transfers between devices with their start and end apart: 4 -> 8, of which waited for: 4 -> 7; matrix products, arithmetic and copies ran while one was open for 0% -> 0% of each run, Pallas kernels for 4% -> 6%
where the time goes in v3:
time: 56.9 us; the launch traced here: 56.7 us
  blocking collectives  24.1 us (42%)
  Pallas kernels  14.7 us (26%)
  starting transfers between devices  8.54 us (15%)
  waiting for transfers between devices  7.93 us (14%)
  between operations  1.35 us (2%)
    all_to_all x2, blocking collectives, exchange(): return lax.all_to_all(x, 'dom', 0, 0, axis_index_groups=groups, tiled=True)  24.1 us
    pallas_call x11, Pallas kernels, call(): pl.pallas_call(kernel, out_shape=[jax.ShapeDtypeStruct(s, d) for s, d in...  14.7 us
    ppermute x8, starting transfers between devices, swap(): return lax.ppermute(x, 'dom', [(i, i ^ mask) for i in range(devices)])  8.54 us
    ppermute x8, waiting for transfers between devices, swap(): return lax.ppermute(x, 'dom', [(i, i ^ mask) for i in range(devices)])  7.93 us
  transfers between devices with their start and end apart: 8, of which 7 were waited for; matrix products, arithmetic and copies ran while one was open for 0% of the time, Pallas kernels for 6%

profile of v3, /device:TPU:0, one launch (start us, length us, event | category | flops | bytes accessed | tf_op | source)
XLA Modules:
  0.0 56.7 jit_solution(1490007248480230841)
XLA Ops:
  0.6 0.0 copy-start
  1.3 3.8 %forward.1 = (bf16[512,1024]{1,0:T(8,128)(2,1)S(1)}, bf16[256,1024]{1,0:T(8,128)(2,1)S(1)}, bf16[512,1024]{1,0:T(8,128)(2,1)S(1)}, f32[32,1024]{1,0:T(8,128)S(1)...) custom-call(s32[1]{0:T(128)S(6)} %copy.17.counts, ...), custom_call_target="tpu_custom_call" | custom-call | tf_op jit(solution)/shard_map/forward/pallas_call | solution.py:347
  5.1 0.6 collective-permute-start
  5.6 0.9 %collective-permute-done.other = f32[144,128]{1,0:T(8,128)S(1)} collective-permute-done((f32[144,128]{1,0:T(8,128)S(1)}, f32[144,128]{1,0:T(8,128)S(1)}, u32[]{:S(2)}, u32[]{:S(2)}) %collective-permute-start) | collective-permute-done | bytes 73760 | tf_op jit(solution)/shard_map/ppermute | solution.py:368
  6.6 2.9 %collective-permute-start.1 = (bf16[144,128]{1,0:T(8,128)(2,1)S(1)}, bf16[144,128]{1,0:T(8,128)(2,1)S(1)}, u32[]{:S(2)}, u32[]{:S(2)}) collective-permute-start(bf16[144,128]{1,0:T(8,128)(2,1)S(1)} %narrow.1.mine), channel_id=1, source_target_pairs={{0,2},{1,3},{2,0},{3,1},{4,6},{5,7},{6,4},{7,5},{8,10},{9,11},{10,... | collective-permute-start | bytes 110600 | tf_op jit(solution)/shard_map/ppermute | solution.py:368
  9.5 0.9 %softmax.1 = (f32[512,1024]{1,0:T(8,128)S(1)}, f32[512,1024]{1,0:T(8,128)S(1)}) custom-call(bf16[256,1024]{1,0:T(8,128)(2,1)S(1)} %get-tuple-element.42.proj, f32[32,1024]{1,0:T(8,128)S(1)} %get-tuple-element.44.stats, bf16[256,128]{1,0:T(8,128)(2,1)S(1)} %get-tuple-element.47.wsb), custom_call_target="tpu_custom_call" | custom-call | flops 134217728 | tf_op jit(solution)/shard_map/softmax/pallas_call | solution.py:347
  10.4 1.1 %collective-permute-done.1.other = bf16[144,128]{1,0:T(8,128)(2,1)S(1)} collective-permute-done((bf16[144,128]{1,0:T(8,128)(2,1)S(1)}, bf16[144,128]{1,0:T(8,128)(2,1)S(1)}, u32[]{:S(2)}, u32[]{:S(2)}) %collective-permute-start.1) | collective-permute-done | bytes 36896 | tf_op jit(solution)/shard_map/ppermute | solution.py:368
  11.4 4.2 %collective-permute-start.4 = (bf16[144,128]{1,0:T(8,128)(2,1)S(1)}, bf16[144,128]{1,0:T(8,128)(2,1)S(1)}, u32[]{:S(2)}, u32[]{:S(2)}) collective-permute-start(bf16[144,128]{1,0:T(8,128)(2,1)S(1)} %near.1.refs_0_), channel_id=1, source_target_pairs={{0,12},{1,13},{2,14},{3,15},{4,8},{5,9},{6,10},{7,11},{8,4},{9,5},... | collective-permute-start | bytes 110600 | tf_op jit(solution)/shard_map/ppermute | solution.py:368
  15.6 0.0 collective-permute-start.3
  15.6 0.6 %collective-permute-start.2 = (bf16[144,128]{1,0:T(8,128)(2,1)S(1)}, bf16[144,128]{1,0:T(8,128)(2,1)S(1)}, u32[]{:S(2)}, u32[]{:S(2)}) collective-permute-start(bf16[144,128]{1,0:T(8,128)(2,1)S(1)} %near.1.refs_0_), channel_id=1, source_target_pairs={{0,4},{1,5},{2,6},{3,7},{4,0},{5,1},{6,2},{7,3},{8,12},{9,13},{10,... | collective-permute-start | bytes 110600 | tf_op jit(solution)/shard_map/ppermute | solution.py:368
  16.2 1.5 %collective-permute-done.4.refs_3_ = bf16[144,128]{1,0:T(8,128)(2,1)S(1)} collective-permute-done((bf16[144,128]{1,0:T(8,128)(2,1)S(1)}, bf16[144,128]{1,0:T(8,128)(2,1)S(1)}, u32[]{:S(2)}, u32[]{:S(2)}) %collective-permute-start.4) | collective-permute-done | bytes 36896 | tf_op jit(solution)/shard_map/ppermute | solution.py:368
  17.7 2.7 %collective-permute-done.3.refs_2_ = bf16[144,128]{1,0:T(8,128)(2,1)S(1)} collective-permute-done((bf16[144,128]{1,0:T(8,128)(2,1)S(1)}, bf16[144,128]{1,0:T(8,128)(2,1)S(1)}, u32[]{:S(2)}, u32[]{:S(2)}) %collective-permute-start.3) | collective-permute-done | bytes 36896 | tf_op jit(solution)/shard_map/ppermute | solution.py:368
  20.5 0.0 collective-permute-done.2.refs_1_
  20.5 0.0 copy-done
  20.5 2.8 %mix.1.mine = f32[104,256]{1,0:T(8,128)S(1)} custom-call(bf16[3,32,32]{2,1,0:T(8,128)(2,1)S(1)} %copy-done, bf16[144,128]{1,0:T(8,128)(2,1)S(1)} %near.1.refs_0_, bf16[144,128]{1,0:T(8,128)(2,1)S(1)} %collective-permute-done.2.refs_1_, bf16[144,128]{1,0:T(8,128)(2,1)S(1)} %collective-permute-done.3.refs_2_, bf16[144,128]{1,0:T(8,128)(2,1)S(1)} %collective-permute-done.4.refs_3_), custom_call_target="tpu_custom_call" | custom-call | tf_op jit(solution)/shard_map/mix/pallas_call | solution.py:347
  23.2 0.0 collective-permute-start.5
  23.3 1.3 %collective-permute-done.5.other = f32[104,256]{1,0:T(8,128)S(1)} collective-permute-done((f32[104,256]{1,0:T(8,128)S(1)}, f32[104,256]{1,0:T(8,128)S(1)}, u32[]{:S(2)}, u32[]{:S(2)}) %collective-permute-start.5) | collective-permute-done | bytes 106528 | tf_op jit(solution)/shard_map/ppermute | solution.py:368
  24.6 3.9 %backward.1 = (bf16[256,1024]{1,0:T(8,128)(2,1)S(1)}, bf16[512,1024]{1,0:T(8,128)(2,1)S(1)}, bf16[448,256]{1,0:T(8,128)(2,1)S(1)}, bf16[448,256]{1,0:T(8,128)(2,1)S(1)}, f32[3,32,32]{2,1,0:T(8,128)}) custom-call(bf16[1024,256]{1,0:T(8,128)(2,1)S(1)} %get-tuple-element.39.cells, bf16[1024,256]{1,0:T(8,128)(2,1)S(1)} %get-tuple-element.40.cot, ...), custom_call_target="tpu_custom_call" | custom-call | tf_op jit(solution)/shard_map/backward/pallas_call | solution.py:347
  28.4 0.2 collective-permute-start.6
  28.6 1.1 %result.1 = bf16[1024,256]{1,0:T(8,128)(2,1)} custom-call(bf16[256,1024]{1,0:T(8,128)(2,1)S(1)} %get-tuple-element.56.hid, bf16[256,256]{1,0:T(8,128)(2,1)S(1)} %get-tuple-element.57.w_out), custom_call_target="tpu_custom_call" | custom-call | flops 134217728 | tf_op jit(solution)/shard_map/result/pallas_call | solution.py:347
  29.8 0.2 collective-permute-done.6.other
  30.0 0.1 pair_add.1
  30.0 12.8 %all_to_all.22 = bf16[8,56,256]{2,1,0:T(8,128)(2,1)S(1)} all-to-all(bf16[8,56,256]{2,1,0:T(8,128)(2,1)S(1)} %bitcast.10), channel_id=1, replica_groups={{0,2,4,6,8,10,12,14},{1,3,5,7,9,11,13,15},{16,18,20,22,24,26,28,30},{17..., dimensions={0} | all-to-all | bytes 458752 | tf_op jit(solution)/shard_map/all_to_all | solution.py:371
  42.9 11.3 %all_to_all.23 = bf16[8,56,256]{2,1,0:T(8,128)(2,1)S(1)} all-to-all(bf16[8,56,256]{2,1,0:T(8,128)(2,1)S(1)} %bitcast.9), channel_id=1, replica_groups={{0,2,4,6,8,10,12,14},{1,3,5,7,9,11,13,15},{16,18,20,22,24,26,28,30},{17..., dimensions={0} | all-to-all | bytes 458752 | tf_op jit(solution)/shard_map/all_to_all | solution.py:371
  54.2 0.0 collective-permute-start.7
  54.2 1.2 %grad_cells.1 = bf16[1024,256]{1,0:T(8,128)(2,1)} custom-call(bf16[512,1024]{1,0:T(8,128)(2,1)S(1)} %get-tuple-element.59.dpf, bf16[256,256]{1,0:T(8,128)(2,1)S(1)} %get-tuple-element.60.w_x, bf16[256,256]{1,0:T(8,128)(2,1)S(1)} %get-tuple-element.61.w_fx), custom_call_target="tpu_custom_call" | custom-call | flops 268435456 | tf_op jit(solution)/shard_map/grad_cells/pallas_call | solution.py:347
  55.4 0.2 collective-permute-done.7.other
  55.7 1.0 %place.1 = (f32[256,256]{1,0:T(8,128)}, f32[256,256]{1,0:T(8,128)}, f32[32,64]{1,0:T(8,128)}, f32[1,32]{1,0:T(1,128)}, f32[256,256]{1,0:T(8,128)}) custom-call(bf16[448,256]{1,0:T(8,128)(2,1)S(1)} %bitcast.7, bf16[448,256]{1,0:T(8,128)(2,1)S(1)} %collective-permute-done.7.other), custom_call_target="tpu_custom_call" | custom-call | tf_op jit(solution)/shard_map/place/pallas_call | solution.py:347
  (3 shorter events, 0.1 us)
Async XLA Ops:
  0.6 19.8 %copy-start = (bf16[3,32,32]{2,1,0:T(8,128)(2,1)S(1)}, bf16[3,32,32]{2,1,0:T(8,128)(2,1)}, u32[]{:S(2)}) copy-start(bf16[3,32,32]{2,1,0:T(8,128)(2,1)} %w_qkv.1) | copy-start | bytes 18436
  5.1 1.5 %collective-permute-start = (f32[144,128]{1,0:T(8,128)S(1)}, f32[144,128]{1,0:T(8,128)S(1)}, u32[]{:S(2)}, u32[]{:S(2)}) collective-permute-start(f32[144,128]{1,0:T(8,128)S(1)} %get-tuple-element.46), channel_id=1, source_target_pairs={{0,1},{1,0},{2,3},{3,2},{4,5},{5,4},{6,7},{7,6},{8,9},{9,8},{10,11... | collective-permute-start | bytes 221192 | tf_op jit(solution)/shard_map/ppermute | solution.py:368
  6.6 4.9 %collective-permute-start.1 = (bf16[144,128]{1,0:T(8,128)(2,1)S(1)}, bf16[144,128]{1,0:T(8,128)(2,1)S(1)}, u32[]{:S(2)}, u32[]{:S(2)}) collective-permute-start(bf16[144,128]{1,0:T(8,128)(2,1)S(1)} %narrow.1.mine), channel_id=1, source_target_pairs={{0,2},{1,3},{2,0},{3,1},{4,6},{5,7},{6,4},{7,5},{8,10},{9,11},{10,... | collective-permute-start | bytes 110600 | tf_op jit(solution)/shard_map/ppermute | solution.py:368
  11.4 6.3 %collective-permute-start.4 = (bf16[144,128]{1,0:T(8,128)(2,1)S(1)}, bf16[144,128]{1,0:T(8,128)(2,1)S(1)}, u32[]{:S(2)}, u32[]{:S(2)}) collective-permute-start(bf16[144,128]{1,0:T(8,128)(2,1)S(1)} %near.1.refs_0_), channel_id=1, source_target_pairs={{0,12},{1,13},{2,14},{3,15},{4,8},{5,9},{6,10},{7,11},{8,4},{9,5},... | collective-permute-start | bytes 110600 | tf_op jit(solution)/shard_map/ppermute | solution.py:368
  15.6 4.9 %collective-permute-start.3 = (bf16[144,128]{1,0:T(8,128)(2,1)S(1)}, bf16[144,128]{1,0:T(8,128)(2,1)S(1)}, u32[]{:S(2)}, u32[]{:S(2)}) collective-permute-start(bf16[144,128]{1,0:T(8,128)(2,1)S(1)} %near.1.refs_0_), channel_id=1, source_target_pairs={{0,8},{1,9},{2,10},{3,11},{4,12},{5,13},{6,14},{7,15},{8,0},{9,1},... | collective-permute-start | bytes 110600 | tf_op jit(solution)/shard_map/ppermute | solution.py:368
  15.6 4.9 %collective-permute-start.2 = (bf16[144,128]{1,0:T(8,128)(2,1)S(1)}, bf16[144,128]{1,0:T(8,128)(2,1)S(1)}, u32[]{:S(2)}, u32[]{:S(2)}) collective-permute-start(bf16[144,128]{1,0:T(8,128)(2,1)S(1)} %near.1.refs_0_), channel_id=1, source_target_pairs={{0,4},{1,5},{2,6},{3,7},{4,0},{5,1},{6,2},{7,3},{8,12},{9,13},{10,... | collective-permute-start | bytes 110600 | tf_op jit(solution)/shard_map/ppermute | solution.py:368
  23.2 1.4 %collective-permute-start.5 = (f32[104,256]{1,0:T(8,128)S(1)}, f32[104,256]{1,0:T(8,128)S(1)}, u32[]{:S(2)}, u32[]{:S(2)}) collective-permute-start(f32[104,256]{1,0:T(8,128)S(1)} %mix.1.mine), channel_id=1, source_target_pairs={{0,1},{1,0},{2,3},{3,2},{4,5},{5,4},{6,7},{7,6},{8,9},{9,8},{10,11... | collective-permute-start | bytes 319496 | tf_op jit(solution)/shard_map/ppermute | solution.py:368
  28.4 1.5 %collective-permute-start.6 = (bf16[448,256]{1,0:T(8,128)(2,1)S(1)}, bf16[448,256]{1,0:T(8,128)(2,1)S(1)}, u32[]{:S(2)}, u32[]{:S(2)}) collective-permute-start(bf16[448,256]{1,0:T(8,128)(2,1)S(1)} %get-tuple-element.55), channel_id=1, source_target_pairs={{0,1},{1,0},{2,3},{3,2},{4,5},{5,4},{6,7},{7,6},{8,9},{9,8},{10,11... | collective-permute-start | bytes 688136 | tf_op jit(solution)/shard_map/ppermute | solution.py:368
  54.2 1.5 %collective-permute-start.7 = (bf16[448,256]{1,0:T(8,128)(2,1)S(1)}, bf16[448,256]{1,0:T(8,128)(2,1)S(1)}, u32[]{:S(2)}, u32[]{:S(2)}) collective-permute-start(bf16[448,256]{1,0:T(8,128)(2,1)S(1)} %bitcast.6), channel_id=1, source_target_pairs={{0,1},{1,0},{2,3},{3,2},{4,5},{5,4},{6,7},{7,6},{8,9},{9,8},{10,11... | collective-permute-start | bytes 688136 | tf_op jit(solution)/shard_map/ppermute | solution.py:368

commit v4 on v3

v4 whole, which is shorter than its diff:
```python
import functools
import math

import jax
import jax.numpy as jnp
from jax import lax
from jax.experimental import pallas as pl
from jax.experimental.pallas import tpu as pltpu
from jax.sharding import PartitionSpec as P

F32 = jnp.float32
BF16 = jnp.bfloat16
FINE = lax.Precision.HIGH
HEADS = 8
SLICES = 64
HEAD = 32
WIDTH = HEADS * HEAD
ROWS1 = 136
ROWS2 = 408
LOG2E = math.log2(math.e)
CHUNK = 1024
WRITE = 256


def nn(a, b, precision=None):
    return lax.dot_general(
        a, b, (((1,), (0,)), ((), ())), precision=precision, preferred_element_type=F32
    )


def nt(a, b, precision=None):
    return lax.dot_general(
        a, b, (((1,), (1,)), ((), ())), precision=precision, preferred_element_type=F32
    )


def iota(shape, dim):
    return lax.broadcasted_iota(jnp.int32, shape, dim)


def slice_blocks(w_slice):
    tall = jnp.concatenate([w_slice] * 4, axis=0)
    pick = (iota((SLICES, 256), 1) % SLICES == iota((SLICES, 256), 0)).astype(BF16)
    wide = nn(tall, pick)
    same = iota((128, 256), 0) // HEAD == iota((128, 256), 1) // SLICES
    return jnp.where(same, wide, 0.0)


def temp_blocks(w_temp):
    pick = (iota((HEAD, 128), 1) % HEAD == iota((HEAD, 128), 0)).astype(BF16)
    wide = nn(jnp.broadcast_to(w_temp, (HEADS, HEAD)), pick)
    same = iota((HEADS, 128), 0) == iota((HEADS, 128), 1) // HEAD
    return jnp.where(same, wide, 0.0).astype(BF16)


def group_rows(group):
    return pl.ds(pl.multiple_of(group * 128, 128), 128)


def chunk_of(j):
    return pl.ds(pl.multiple_of(j * CHUNK, CHUNK), CHUNK)


def forward_group(count, operands, outs, tab, group, wait):
    cells, cot, w_out, wxt, wft, wsb, wtb = operands
    weights, proj, fd, stats, payload = outs
    rows = cells.shape[0]
    mine = group_rows(group)
    tab[0:128, :] = wxt[mine, :]
    tab[128:256, :] = wft[mine, :]

    def chunk(j, carry):
        at = chunk_of(j)
        wait(j)
        both = nt(tab[...], cells[at, :]).astype(BF16)
        projected = both[0:128]
        proj[:, at] = projected
        dhid = nt(w_out[mine, :], cot[at, :]).astype(BF16)
        for k in range(4):
            fd[64 * k : 64 * k + 32, at] = both[128 + 32 * k : 160 + 32 * k]
            fd[64 * k + 32 : 64 * k + 64, at] = dhid[32 * k : 32 * k + 32]
        lin = nn(wtb[...], projected)
        e = jnp.exp(-jnp.abs(lin))
        soft = jnp.maximum(lin, 0.0) + jnp.log(1.0 + e)
        inv = 1.0 / (0.5 + soft)
        sig = jnp.where(lin >= 0, 1.0, e) / (1.0 + e)
        a = inv * (10.0 * LOG2E)
        live = jnp.where(j * CHUNK + iota((1, CHUNK), 1) < count, 1.0, 0.0)
        norms = []
        x = nn(wsb[...], projected)
        for k in range(4):
            t = jnp.tanh(x[SLICES * k : SLICES * k + SLICES] * 0.1)
            p = jnp.exp2(t * a[k : k + 1])
            r = live / jnp.sum(p, axis=0, keepdims=True)
            weights[SLICES * k : SLICES * k + SLICES, at] = (p * r).astype(BF16)
            norms.append(r)
        stats[0:8, at] = a
        stats[8:16, at] = inv
        stats[16:24, at] = inv * inv * sig * (-10.0)
        stats[24:32, at] = jnp.concatenate(norms + norms, axis=0)
        return carry

    lax.fori_loop(0, rows // CHUNK, chunk, 0)
    ones = jnp.ones((16, rows), BF16)
    first = iota((64, 128), 1) < SLICES
    for q in range(2):
        pair = slice(128 * q, 128 * q + 128)
        out = nt(jnp.concatenate([fd[pair, :], ones], axis=0), weights[pair, :])
        payload[64 * q : 64 * q + 64, :] = jnp.where(first, out[0:64], out[64:128])
        payload[128 + q : 129 + q, :] = out[128:129]
    payload[130:136, :] = jnp.zeros((6, 128), F32)


def forward_far_kernel(counts, cells_hbm, cot_hbm, *refs):
    hbm, refs = refs[:5], refs[5:]
    outs, refs = refs[:5], refs[5:]
    (wxt, wft, wsb, wsd, wtb, wtc, cells, cot, w_x, w_fx, w_out), refs = refs[:11], refs[11:]
    w_slice, w_temp, small, big, tab = refs
    core = lax.rem(lax.axis_index("dom"), 2)

    def load(source, target, slot, j):
        at = chunk_of(j)
        return pltpu.make_async_copy(source.at[at, :], target.at[at, :], big.at[slot, j])

    tables = [
        pltpu.make_async_copy(source, target, small.at[i])
        for i, (source, target) in enumerate(zip(hbm, (w_x, w_fx, w_slice, w_temp, w_out)))
    ]
    for table in tables:
        table.start()
    for j in range(cells.shape[0] // CHUNK):
        load(cells_hbm, cells, 0, j).start()
        load(cot_hbm, cot, 1, j).start()
    for table in tables:
        table.wait()
    blocks = temp_blocks(w_temp[...])
    wtb[...] = blocks
    wtc[...] = blocks.astype(F32).T
    wxt[...] = w_x[...].T
    wft[...] = w_fx[...].T
    slices = slice_blocks(w_slice[...])
    wsd[...] = slices.astype(BF16)
    wsb[...] = slices.T.astype(BF16)

    def wait(j):
        load(cells_hbm, cells, 0, j).wait()
        load(cot_hbm, cot, 1, j).wait()

    operands = (cells, cot, w_out, wxt, wft, wsb, wtb)
    forward_group(counts[0], operands, outs, tab, 1 - core, wait)


def forward_own_kernel(counts, *refs):
    core = lax.rem(lax.axis_index("dom"), 2)
    forward_group(counts[0], refs[:7], refs[7:12], refs[12], core, lambda j: None)


def narrow_add_kernel(mine, other, out):
    out[...] = (mine[...].astype(F32) + other[...].astype(F32)).astype(BF16)


def softmax_kernel(wsb, *refs):
    def chunk(j, carry):
        at = chunk_of(j)
        for g in range(2):
            proj, stats = refs[2 * g : 2 * g + 2]
            tanhs, soft = refs[4 + 2 * g : 6 + 2 * g]
            x = nn(wsb[...], proj[:, at])
            for k in range(4):
                rng = slice(SLICES * k, SLICES * k + SLICES)
                t = jnp.tanh(x[rng] * 0.1)
                tanhs[rng, at] = t
                soft[rng, at] = jnp.exp2(t * stats[k : k + 1, at]) * stats[24 + k : 25 + k, at]
        return carry

    lax.fori_loop(0, refs[0].shape[1] // CHUNK, chunk, 0)


def sum_blocks(ref, n):
    total = ref[0:n, :].astype(F32)
    for k in range(1, ref.shape[0] // n):
        total = total + ref[n * k : n * k + n, :].astype(F32)
    return total


def mix_kernel(w_qkv, *refs):
    parts, out = refs[:-1], refs[-1]
    total = sum(part[...].astype(F32) for part in parts)
    numer = jnp.concatenate([total[0:32], total[64:96]], axis=1)
    d_mixed = jnp.concatenate([total[32:64], total[96:128]], axis=1)
    denom = jnp.concatenate([total[128:129], total[129:130]], axis=1) + 1e-05
    inverse = 1.0 / denom
    tokens = numer * inverse
    maps = [w_qkv[k].astype(F32) for k in range(3)]
    q, key, val = [nn(m.T, tokens, FINE) for m in maps]
    key_rows, val_rows = key.T, val.T
    scores = nn(key_rows, q, FINE) * (1.0 / math.sqrt(HEAD))
    same = iota((256, 256), 0) // SLICES == iota((256, 256), 1) // SLICES
    t = jnp.tanh(scores * 0.1)
    powers = jnp.where(same, jnp.exp2(t * (10.0 * LOG2E)), 0.0)
    att = powers * (1.0 / jnp.sum(powers, axis=0, keepdims=True))
    mixed = nn(val, att, FINE)
    d_att = nn(val_rows, d_mixed, FINE)
    d_val = nt(d_mixed, att, FINE)
    inner = jnp.sum(att * d_att, axis=0, keepdims=True)
    d_scores = att * (d_att - inner) * ((1.0 - t * t) * (1.0 / math.sqrt(HEAD)))
    d_q = nn(key, d_scores, FINE)
    d_key = nt(q, d_scores, FINE)
    grads = (d_q, d_key, d_val)
    d_tokens = sum(nn(m, g, FINE) for m, g in zip(maps, grads))
    d_numer = d_tokens * inverse
    d_denom = -jnp.sum(d_numer * tokens, axis=0, keepdims=True)
    out[0:32, :] = d_numer.astype(BF16).astype(F32)
    out[32:64, :] = mixed.astype(BF16).astype(F32)
    out[64:72, :] = jnp.broadcast_to(d_denom, (8, 256))
    for k in range(3):
        out[72:104, 32 * k : 32 * k + 32] = nt(tokens, grads[k], FINE)
    out[72:104, 96:256] = jnp.zeros((32, 160), F32)


def backward_kernel(scale, cells, cot, wsd, wtc, weights, proj, fd, stats, tanhs, softs, *refs):
    if scale is None:
        (e,), refs = refs[:1], refs[1:]
    else:
        (own, e, grad_qkv), refs = (*refs[:2], refs[5]), (*refs[2:5], *refs[6:])
        for k in range(3):
            block = slice(32 * k, 32 * k + 32)
            grad_qkv[k] = (own[72:104, block] + e[72:104, block]) * scale
    hid, dpf, payload, dlog, dtemp, lhs_h, lhs_w, dden = refs
    rows = cells.shape[0]
    diag64 = iota((256, 256), 0) // 64 == iota((256, 256), 1) // 64
    diag32 = iota((128, 256), 0) // 32 == iota((128, 256), 1) // 64
    both = jnp.where(diag64, jnp.concatenate([e[0:64, :]] * 4, axis=0), 0.0)
    lhs_w[...] = both.T.astype(BF16)
    for i in range(2):
        part = jnp.concatenate([e[32 - 32 * i : 64 - 32 * i, :]] * 4, axis=0)
        lhs_h[128 * i : 128 * i + 128, :] = jnp.where(diag32, part, 0.0).astype(BF16)
    dden[...] = jnp.broadcast_to(e[64:72, :].T[:, 0:1], (256, CHUNK))
    dtemp[...] = jnp.zeros(dtemp.shape, F32)

    def chunk(j, carry):
        at = chunk_of(j)
        hf = nn(lhs_h[...], weights[:, at])
        hid[:, at] = hf[0:128].astype(BF16)
        dpf[128:256, at] = hf[128:256].astype(BF16)
        dw = nn(lhs_w[...], fd[:, at])
        outer = []
        for k in range(4):
            rng = slice(SLICES * k, SLICES * k + SLICES)
            t = tanhs[rng, at]
            soft = softs[rng, at]
            d = dw[rng] + dden[rng, :]
            inner = jnp.sum(soft * d, axis=0, keepdims=True)
            ds = soft * (d - inner)
            dlog[rng, at] = (ds * ((1.0 - t * t) * stats[8 + k : 9 + k, at])).astype(BF16)
            dt = jnp.sum(ds * t, axis=0, keepdims=True) * stats[16 + k : 17 + k, at]
            dt = dt.astype(BF16).astype(F32)
            dtemp[k : k + 1, at] = dt
            outer.append(wtc[HEAD * k : HEAD * k + HEAD, k : k + 1] * dt)
        dp = nn(wsd[...], dlog[:, at]) + jnp.concatenate(outer, axis=0)
        dpf[0:128, at] = dp.astype(BF16)
        return carry

    lax.fori_loop(0, rows // CHUNK, chunk, 0)
    payload[0:128, :] = nn(hid[...], cot[...]).astype(BF16)
    payload[128:384, :] = nn(dpf[...], cells[...]).astype(BF16)
    even = jnp.zeros((HEAD, 128), F32)
    odd = jnp.zeros((HEAD, 128), F32)
    for q in range(2):
        pair = dlog[128 * q : 128 * q + 128, :]
        even = even + nt(proj[64 * q : 64 * q + 32, :], pair)
        odd = odd + nt(proj[64 * q + 32 : 64 * q + 64, :], pair)
    d_slice = jnp.where(iota((HEAD, 128), 1) < SLICES, even, odd)
    d_slice = jnp.concatenate([d_slice[0:16], d_slice[16:32]], axis=1)
    d_temp = nt(dtemp[...].astype(BF16), proj[...])
    here = iota((HEADS, 128), 0) == iota((HEADS, 128), 1) // HEAD
    d_temp = jnp.sum(jnp.where(here, d_temp, 0.0), axis=0, keepdims=True)
    d_temp = jnp.concatenate(
        [jnp.broadcast_to(d_temp, (8, 128)), jnp.zeros((8, 128), F32)], axis=1
    )
    payload[384:408, :] = jnp.concatenate([d_slice, d_temp], axis=0).astype(BF16)
    payload[ROWS2:, :] = jnp.zeros((payload.shape[0] - ROWS2, WIDTH), BF16)


def write_rows(out, stage, sems, product):
    copies = []
    for j in range(out.shape[0] // WRITE):
        at = pl.ds(j * WRITE, WRITE)
        stage[at, :] = product(at).T.astype(BF16)
        copies.append(pltpu.make_async_copy(stage.at[at, :], out.at[at, :], sems.at[j]))
        copies[-1].start()
    for copy in copies:
        copy.wait()


def result_kernel(own, far, w_out, out, table, stage, sems):
    core = lax.rem(lax.axis_index("dom"), 2)
    order = [w_out[group_rows(g), :] for g in (core, 1 - core)]
    table[...] = jnp.concatenate(order, axis=0).T

    def product(at):
        return nn(table[...], jnp.concatenate([own[:, at], far[:, at]], axis=0))

    write_rows(out, stage, sems, product)


def grad_cells_kernel(own, far, w_x, w_fx, out, table, stage, sems):
    core = lax.rem(lax.axis_index("dom"), 2)
    for i, g in enumerate((core, 1 - core)):
        table[:, 256 * i : 256 * i + 128] = w_x[:, group_rows(g)]
        table[:, 256 * i + 128 : 256 * i + 256] = w_fx[:, group_rows(g)]

    def product(at):
        return nn(table[...], jnp.concatenate([own[:, at], far[:, at]], axis=0))

    write_rows(out, stage, sems, product)


def place_kernel(mine, other, d_x, d_fx, d_slice, d_temp, d_out):
    core = lax.rem(lax.axis_index("dom"), 2)
    for ref, g in ((mine, core), (other, 1 - core)):
        at = group_rows(g)
        d_out[at, :] = ref[0:128, :].astype(F32)
        d_x[:, at] = ref[128:256, :].astype(F32).T
        d_fx[:, at] = ref[256:384, :].astype(F32).T
    small = mine[384:ROWS2, :].astype(F32) + other[384:ROWS2, :].astype(F32)
    rows = jnp.concatenate([small[0:16, 0:128], small[0:16, 128:256]], axis=0)
    rows = rows + pltpu.roll(rows, 64, 1)
    d_slice[...] = rows[:, 0:SLICES]
    v = small[16:24, 0:128]
    v = v + pltpu.roll(v, 64, 1)
    v = v + pltpu.roll(v, 32, 1)
    d_temp[...] = v[0:1, 0:32]


VMEM = pl.BlockSpec(memory_space=pltpu.VMEM)
SMEM = pl.BlockSpec(memory_space=pltpu.SMEM)
HBM = pl.BlockSpec(memory_space=pltpu.HBM)


def call(kernel, shapes, args, scratch=(), name=None, ins=None, outs=None, flops=0):
    scratch = [pltpu.VMEM(*s) if isinstance(s, tuple) else s for s in scratch]
    estimate = pl.CostEstimate(flops=flops, bytes_accessed=0, transcendentals=0)
    return pl.pallas_call(
        kernel,
        out_shape=[jax.ShapeDtypeStruct(s, d) for s, d in shapes],
        in_specs=ins or [VMEM] * len(args),
        out_specs=outs or [VMEM] * len(shapes),
        scratch_shapes=scratch,
        name=name,
        cost_estimate=estimate if flops else None,
        compiler_params=pltpu.CompilerParams(vmem_limit_bytes=24 << 20),
    )(*args)


def body(devices, cells, counts, w_x, w_fx, w_slice, w_temp, w_qkv, w_out, cotangent):
    rows = cells.shape[0]
    peers = devices // 2
    groups = [list(range(c, devices, 2)) for c in range(2)]
    scale = 1.0 / math.sqrt(rows * devices)
    temp = w_temp.reshape(1, HEAD)
    hm = HEADS * SLICES

    def swap(x, mask):
        return lax.ppermute(x, "dom", [(i, i ^ mask) for i in range(devices)])

    def exchange(x):
        return lax.all_to_all(x, "dom", 0, 0, axis_index_groups=groups, tiled=True)

    hgm = hm // 2
    grouped = [
        ((hgm, rows), BF16),
        ((WIDTH // 2, rows), BF16),
        ((WIDTH, rows), BF16),
        ((32, rows), F32),
        ((ROWS1, 128), F32),
    ]
    local = call(
        forward_far_kernel,
        grouped
        + [
            ((WIDTH, WIDTH), BF16),
            ((WIDTH, WIDTH), BF16),
            ((256, 128), BF16),
            ((128, 256), BF16),
            ((HEADS, 128), BF16),
            ((128, HEADS), F32),
            ((rows, WIDTH), BF16),
            ((rows, WIDTH), BF16),
            ((WIDTH, WIDTH), BF16),
            ((WIDTH, WIDTH), BF16),
            ((WIDTH, WIDTH), BF16),
        ],
        (counts,)
        + tuple(
            pltpu.with_memory_space_constraint(x, pltpu.HBM)
            for x in (cells, cotangent, w_x, w_fx, w_slice, temp, w_out)
        ),
        scratch=[
            ((HEAD, SLICES), BF16),
            ((1, HEAD), BF16),
            pltpu.SemaphoreType.DMA((5,)),
            pltpu.SemaphoreType.DMA((2, rows // CHUNK)),
            ((256, 256), BF16),
        ],
        ins=[SMEM] + [HBM] * 7,
        name="forward_far",
    )
    far = local[:4]
    send = local[4]
    wxt, wft, wsb, wsd, wtb, wtc, cells, cotangent, w_x, w_fx, w_out = local[5:]
    other = swap(send, 1)
    *own, keep = call(
        forward_own_kernel,
        grouped,
        (counts, cells, cotangent, w_out, wxt, wft, wsb, wtb),
        scratch=[((256, 256), BF16)],
        ins=[SMEM] + [VMEM] * 7,
        name="forward_own",
        flops=6 * rows * WIDTH * WIDTH,
    )
    other, keep = lax.optimization_barrier((other, keep))
    part = ((ROWS1, 128), BF16)
    (total,) = call(narrow_add_kernel, [part], (keep, other), name="narrow")
    near = [2**b for b in range(1, devices.bit_length() - 3)]
    last = [devices // 4 * k for k in (1, 2, 3)]
    again = None
    for mask in near:
        other = swap(total, mask)
        if again is None:
            again = call(
                softmax_kernel,
                [((hgm, rows), F32)] * 4,
                (wsb, own[1], own[3], far[1], far[3]),
                name="softmax",
                flops=2 * rows * hm * 128,
            )
            other, *again = lax.optimization_barrier((other, *again))
        (total,) = call(narrow_add_kernel, [part], (total, other), name="near")
    parts = [total] + [swap(total, mask) for mask in last]
    (mine,) = call(mix_kernel, [((104, 256), F32)], (w_qkv, *parts), name="mix")
    other = swap(mine, 1)
    chunk = -(-ROWS2 // peers)
    chunk = -(-chunk // 8) * 8
    half = chunk * peers
    grads = [
        ((WIDTH // 2, rows), BF16),
        ((WIDTH, rows), BF16),
        ((half, WIDTH), BF16),
    ]
    scratch = [
        ((hgm, rows), BF16),
        ((8, rows), F32),
        ((256, 256), BF16),
        ((256, 256), BF16),
        ((hgm, CHUNK), F32),
    ]
    hid_own, dpf_own, keep = call(
        functools.partial(backward_kernel, None),
        grads,
        (cells, cotangent, wsd, wtc, *own, *again[:2], mine),
        scratch=scratch,
        name="backward_own",
        flops=8 * rows * WIDTH * WIDTH,
    )
    other, keep = lax.optimization_barrier((other, keep))
    hid_far, dpf_far, send, grad_qkv = call(
        functools.partial(backward_kernel, scale),
        grads + [((3, HEAD, HEAD), F32)],
        (cells, cotangent, wsd, wtc, *far, *again[2:], mine, other),
        scratch=scratch,
        name="backward_far",
    )
    other = swap(send, 1)
    staging = [((rows, WIDTH), BF16), pltpu.SemaphoreType.DMA((rows // WRITE,))]
    (result,) = call(
        result_kernel,
        [((rows, WIDTH), BF16)],
        (hid_own, hid_far, w_out),
        scratch=[((WIDTH, WIDTH), BF16)] + staging,
        outs=[HBM],
        name="result",
        flops=2 * rows * WIDTH * WIDTH,
    )
    other, result = lax.optimization_barrier((other, result))
    (grad_cells,) = call(
        grad_cells_kernel,
        [((rows, WIDTH), BF16)],
        (dpf_own, dpf_far, w_x, w_fx),
        scratch=[((WIDTH, 2 * WIDTH), BF16)] + staging,
        outs=[HBM],
        name="grad_cells",
        flops=4 * rows * WIDTH * WIDTH,
    )
    (summed,) = call(narrow_add_kernel, [((half, WIDTH), BF16)], (keep, other), name="pair_add")
    parts = exchange(summed)

    def gather(parts_ref, out):
        total = (sum_blocks(parts_ref, chunk) * scale).astype(BF16)
        for k in range(peers):
            out[chunk * k : chunk * k + chunk, :] = total

    (spread,) = call(gather, [((half, WIDTH), BF16)], (parts,), name="gather")
    mine = exchange(spread)
    other = swap(mine, 1)
    d_x, d_fx, d_slice, d_temp, d_out = call(
        place_kernel,
        [
            ((WIDTH, WIDTH), F32),
            ((WIDTH, WIDTH), F32),
            ((HEAD, SLICES), F32),
            ((1, HEAD), F32),
            ((WIDTH, WIDTH), F32),
        ],
        (mine, other),
        name="place",
    )
    return result, grad_cells, d_x, d_fx, d_slice, d_temp.reshape(HEAD), grad_qkv, d_out


def solution(mesh):
    cell = P(("groups", "dom"), None)
    return jax.shard_map(
        functools.partial(body, mesh.shape["dom"]),
        mesh=mesh,
        in_specs=(cell, P(("groups", "dom")), P(), P(), P(), P(), P(), P(), cell),
        out_specs=(
            cell,
            cell,
            P("groups", None),
            P("groups", None),
            P("groups", None),
            P("groups"),
            P("groups", None, None),
            P("groups", None),
        ),
        check_vma=False,
    )
```

time: 56.9 us -> 53.6 us (0.942)
  waiting for transfers between devices: 7.93 us -> 5.67 us
  Pallas kernels: 14.7 us -> 13.4 us
    ppermute x8, waiting for transfers between devices: 7.93 us -> 5.67 us  [swap(): return lax.ppermute(x, 'dom', [(i, i ^ mask) for i in range(devices)])]
    pallas_call x11 -> x13, Pallas kernels: 14.7 us -> 13.4 us  [call(): pl.pallas_call(kernel, out_shape=[jax.ShapeDtypeStruct(s, d) for s, d in...]
  transfers between devices with their start and end apart: 8 -> 8, of which waited for: 7 -> 4; matrix products, arithmetic and copies ran while one was open for 0% -> 0% of each run, Pallas kernels for 6% -> 11%
where the time goes in v4:
time: 53.6 us; the launch traced here: 53.3 us
  blocking collectives  24.3 us (45%)
  Pallas kernels  13.4 us (25%)
  starting transfers between devices  8.62 us (16%)
  waiting for transfers between devices  5.67 us (11%)
  between operations  1.38 us (3%)
    all_to_all x2, blocking collectives, exchange(): return lax.all_to_all(x, 'dom', 0, 0, axis_index_groups=groups, tiled=True)  24.3 us
    pallas_call x13, Pallas kernels, call(): pl.pallas_call(kernel, out_shape=[jax.ShapeDtypeStruct(s, d) for s, d in...  13.4 us
    ppermute x8, starting transfers between devices, swap(): return lax.ppermute(x, 'dom', [(i, i ^ mask) for i in range(devices)])  8.62 us
    ppermute x8, waiting for transfers between devices, swap(): return lax.ppermute(x, 'dom', [(i, i ^ mask) for i in range(devices)])  5.67 us
  transfers between devices with their start and end apart: 8, of which 4 were waited for; matrix products, arithmetic and copies ran while one was open for 0% of the time, Pallas kernels for 11%

profile of v4, /device:TPU:0, one launch (start us, length us, event | category | flops | bytes accessed | tf_op | source)
XLA Modules:
  0.0 53.3 jit_solution(8931807840507447781)
XLA Ops:
  1.3 2.6 %forward_far.1 = (bf16[256,1024]{1,0:T(8,128)(2,1)S(1)}, bf16[128,1024]{1,0:T(8,128)(2,1)S(1)}, bf16[256,1024]{1,0:T(8,128)(2,1)S(1)}, f32[32,1024]{1,0:T(8,128)...) custom-call(s32[1]{0:T(128)S(6)} %copy.17.counts, ...), custom_call_target="tpu_custom_call" | custom-call | tf_op jit(solution)/shard_map/forward_far/pallas_call | solution.py:344
  3.9 0.5 %collective-permute-start = (f32[136,128]{1,0:T(8,128)S(1)}, f32[136,128]{1,0:T(8,128)S(1)}, u32[]{:S(2)}, u32[]{:S(2)}) collective-permute-start(f32[136,128]{1,0:T(8,128)S(1)} %get-tuple-element.64), channel_id=1, source_target_pairs={{0,1},{1,0},{2,3},{3,2},{4,5},{5,4},{6,7},{7,6},{8,9},{9,8},{10,11... | collective-permute-start | bytes 208904 | tf_op jit(solution)/shard_map/ppermute | solution.py:365
  4.5 1.1 %forward_own.1 = (bf16[256,1024]{1,0:T(8,128)(2,1)S(1)}, bf16[128,1024]{1,0:T(8,128)(2,1)S(1)}, bf16[256,1024]{1,0:T(8,128)(2,1)S(1)}, f32[32,1024]{1,0:T(8,128)S(1)}, f32[136,128]{1,0:T(8,128)S(1)}) custom-call(s32[1]{0:T(128)S(6)} %copy.17.counts, bf16[1024,256]{1,0:T(8,128)(2,1)S(1)} %get-tuple-element.56.refs_0_.cells, ...), custom_call_target="tpu_custom_call" | custom-call | flops 402653184 | tf_op jit(solution)/shard_map/forward_own/pallas_call | solution.py:344
  5.6 0.0 collective-permute-done.other
  5.6 2.7 %collective-permute-start.1 = (bf16[136,128]{1,0:T(8,128)(2,1)S(1)}, bf16[136,128]{1,0:T(8,128)(2,1)S(1)}, u32[]{:S(2)}, u32[]{:S(2)}) collective-permute-start(bf16[136,128]{1,0:T(8,128)(2,1)S(1)} %narrow.1.mine), channel_id=1, source_target_pairs={{0,2},{1,3},{2,0},{3,1},{4,6},{5,7},{6,4},{7,5},{8,10},{9,11},{10,... | collective-permute-start | bytes 104456 | tf_op jit(solution)/shard_map/ppermute | solution.py:365
  8.3 0.7 %softmax.1 = (f32[256,1024]{1,0:T(8,128)S(1)}, f32[256,1024]{1,0:T(8,128)S(1)}, f32[256,1024]{1,0:T(8,128)S(1)}, f32[256,1024]{1,0:T(8,128)S(1)}) custom-call(bf16[256,128]{1,0:T(8,128)(2,1)S(1)} %get-tuple-element.68.refs_5_.wsb, bf16[128,1024]{1,0:T(8,128)(2,1)S(1)} %get-tuple-element.73.refs_0_.proj, f32[32,1024]{1,0:T(8,128)S(1)} %get-tuple-element.74.refs_1_.stats, ...), custom_call_target="tpu_custom_call" | custom-call | flops 134217728 | tf_op jit(solution)/shard_map/softmax/pallas_call | solution.py:344
  9.0 1.2 %collective-permute-done.1.other = bf16[136,128]{1,0:T(8,128)(2,1)S(1)} collective-permute-done((bf16[136,128]{1,0:T(8,128)(2,1)S(1)}, bf16[136,128]{1,0:T(8,128)(2,1)S(1)}, u32[]{:S(2)}, u32[]{:S(2)}) %collective-permute-start.1) | collective-permute-done | bytes 34848 | tf_op jit(solution)/shard_map/ppermute | solution.py:365
  10.3 0.0 copy-start
  10.3 4.1 %collective-permute-start.4 = (bf16[136,128]{1,0:T(8,128)(2,1)S(1)}, bf16[136,128]{1,0:T(8,128)(2,1)S(1)}, u32[]{:S(2)}, u32[]{:S(2)}) collective-permute-start(bf16[136,128]{1,0:T(8,128)(2,1)S(1)} %near.1.refs_0_), channel_id=1, source_target_pairs={{0,12},{1,13},{2,14},{3,15},{4,8},{5,9},{6,10},{7,11},{8,4},{9,5},... | collective-permute-start | bytes 104456 | tf_op jit(solution)/shard_map/ppermute | solution.py:365
  14.4 0.0 collective-permute-start.3
  14.4 0.6 %collective-permute-start.2 = (bf16[136,128]{1,0:T(8,128)(2,1)S(1)}, bf16[136,128]{1,0:T(8,128)(2,1)S(1)}, u32[]{:S(2)}, u32[]{:S(2)}) collective-permute-start(bf16[136,128]{1,0:T(8,128)(2,1)S(1)} %near.1.refs_0_), channel_id=1, source_target_pairs={{0,4},{1,5},{2,6},{3,7},{4,0},{5,1},{6,2},{7,3},{8,12},{9,13},{10,... | collective-permute-start | bytes 104456 | tf_op jit(solution)/shard_map/ppermute | solution.py:365
  15.1 1.6 %collective-permute-done.4.refs_3_ = bf16[136,128]{1,0:T(8,128)(2,1)S(1)} collective-permute-done((bf16[136,128]{1,0:T(8,128)(2,1)S(1)}, bf16[136,128]{1,0:T(8,128)(2,1)S(1)}, u32[]{:S(2)}, u32[]{:S(2)}) %collective-permute-start.4) | collective-permute-done | bytes 34848 | tf_op jit(solution)/shard_map/ppermute | solution.py:365
  16.7 2.6 %collective-permute-done.3.refs_2_ = bf16[136,128]{1,0:T(8,128)(2,1)S(1)} collective-permute-done((bf16[136,128]{1,0:T(8,128)(2,1)S(1)}, bf16[136,128]{1,0:T(8,128)(2,1)S(1)}, u32[]{:S(2)}, u32[]{:S(2)}) %collective-permute-start.3) | collective-permute-done | bytes 34848 | tf_op jit(solution)/shard_map/ppermute | solution.py:365
  19.3 0.0 collective-permute-done.2.refs_1_
  19.3 0.0 copy-done
  19.3 1.8 %mix.1.refs_0_ = f32[104,256]{1,0:T(8,128)S(1)} custom-call(bf16[3,32,32]{2,1,0:T(8,128)(2,1)S(1)} %copy-done, bf16[136,128]{1,0:T(8,128)(2,1)S(1)} %near.1.refs_0_, bf16[136,128]{1,0:T(8,128)(2,1)S(1)} %collective-permute-done.2.refs_1_, bf16[136,128]{1,0:T(8,128)(2,1)S(1)} %collective-permute-done.3.refs_2_, ...), custom_call_target="tpu_custom_call" | custom-call | tf_op jit(solution)/shard_map/mix/pallas_call | solution.py:344
  21.1 0.1 collective-permute-start.5
  21.1 1.6 %backward_own.1 = (bf16[128,1024]{1,0:T(8,128)(2,1)S(1)}, bf16[256,1024]{1,0:T(8,128)(2,1)S(1)}, bf16[448,256]{1,0:T(8,128)(2,1)S(1)}) custom-call(bf16[1024,256]{1,0:T(8,128)(2,1)S(1)} %get-tuple-element.56.refs_0_.cells, bf16[1024,256]{1,0:T(8,128)(2,1)S(1)} %get-tuple-element.57.refs_1_.cot, bf16[128,256]{1,0:T(8,128)(2,1)S(1)} %get-tuple-element.58.wsd, ...), custom_call_target="tpu_custom_call" | custom-call | flops 536870912 | tf_op jit(solution)/shard_map/backward_own/pallas_call | solution.py:344
  22.7 0.0 collective-permute-done.5.refs_1_
  22.7 2.1 %backward_far.1 = (bf16[128,1024]{1,0:T(8,128)(2,1)S(1)}, bf16[256,1024]{1,0:T(8,128)(2,1)S(1)}, bf16[448,256]{1,0:T(8,128)(2,1)S(1)}, f32[3,32,32]{2,1,0:T(8,128)}) custom-call(bf16[1024,256]{1,0:T(8,128)(2,1)S(1)} %get-tuple-element.56.refs_0_.cells, bf16[1024,256]{1,0:T(8,128)(2,1)S(1)} %get-tuple-element.57.refs_1_.cot, ...), custom_call_target="tpu_custom_call" | custom-call | tf_op jit(solution)/shard_map/backward_far/pallas_call | solution.py:344
  24.8 0.5 collective-permute-start.6
  25.3 1.2 %result.1 = bf16[1024,256]{1,0:T(8,128)(2,1)} custom-call(bf16[128,1024]{1,0:T(8,128)(2,1)S(1)} %get-tuple-element.89.own, bf16[128,1024]{1,0:T(8,128)(2,1)S(1)} %get-tuple-element.90.far, bf16[256,256]{1,0:T(8,128)(2,1)S(1)} %get-tuple-element.65.refs_2_.w_out), custom_call_target="tpu_custom_call" | custom-call | flops 134217728 | tf_op jit(solution)/shard_map/result/pallas_call | solution.py:344
  26.5 0.0 collective-permute-done.6.other
  26.5 0.1 pair_add.1
  26.5 13.0 %all_to_all.22 = bf16[8,56,256]{2,1,0:T(8,128)(2,1)S(1)} all-to-all(bf16[8,56,256]{2,1,0:T(8,128)(2,1)S(1)} %bitcast.10), channel_id=1, replica_groups={{0,2,4,6,8,10,12,14},{1,3,5,7,9,11,13,15},{16,18,20,22,24,26,28,30},{17..., dimensions={0} | all-to-all | bytes 458752 | tf_op jit(solution)/shard_map/all_to_all | solution.py:368
  39.5 11.3 %all_to_all.23 = bf16[8,56,256]{2,1,0:T(8,128)(2,1)S(1)} all-to-all(bf16[8,56,256]{2,1,0:T(8,128)(2,1)S(1)} %bitcast.9), channel_id=1, replica_groups={{0,2,4,6,8,10,12,14},{1,3,5,7,9,11,13,15},{16,18,20,22,24,26,28,30},{17..., dimensions={0} | all-to-all | bytes 458752 | tf_op jit(solution)/shard_map/all_to_all | solution.py:368
  50.8 0.0 collective-permute-start.7
  50.8 1.2 %grad_cells.1 = bf16[1024,256]{1,0:T(8,128)(2,1)} custom-call(bf16[256,1024]{1,0:T(8,128)(2,1)S(1)} %get-tuple-element.92.own, bf16[256,1024]{1,0:T(8,128)(2,1)S(1)} %get-tuple-element.93.far, bf16[256,256]{1,0:T(8,128)(2,1)S(1)} %get-tuple-element.94.w_x, bf16[256,256]{1,0:T(8,128)(2,1)S(1)} %get-tuple-element.95.w_fx), custom_call_target="tpu_custom_call" | custom-call | flops 268435456 | tf_op jit(solution)/shard_map/grad_cells/pallas_call | solution.py:344
  52.1 0.2 collective-permute-done.7.other
  52.3 1.0 %place.1 = (f32[256,256]{1,0:T(8,128)}, f32[256,256]{1,0:T(8,128)}, f32[32,64]{1,0:T(8,128)}, f32[1,32]{1,0:T(1,128)}, f32[256,256]{1,0:T(8,128)}) custom-call(bf16[448,256]{1,0:T(8,128)(2,1)S(1)} %bitcast.7, bf16[448,256]{1,0:T(8,128)(2,1)S(1)} %collective-permute-done.7.other), custom_call_target="tpu_custom_call" | custom-call | tf_op jit(solution)/shard_map/place/pallas_call | solution.py:344
  (3 shorter events, 0.1 us)
Async XLA Ops:
  3.9 1.6 %collective-permute-start = (f32[136,128]{1,0:T(8,128)S(1)}, f32[136,128]{1,0:T(8,128)S(1)}, u32[]{:S(2)}, u32[]{:S(2)}) collective-permute-start(f32[136,128]{1,0:T(8,128)S(1)} %get-tuple-element.64), channel_id=1, source_target_pairs={{0,1},{1,0},{2,3},{3,2},{4,5},{5,4},{6,7},{7,6},{8,9},{9,8},{10,11... | collective-permute-start | bytes 208904 | tf_op jit(solution)/shard_map/ppermute | solution.py:365
  5.6 4.7 %collective-permute-start.1 = (bf16[136,128]{1,0:T(8,128)(2,1)S(1)}, bf16[136,128]{1,0:T(8,128)(2,1)S(1)}, u32[]{:S(2)}, u32[]{:S(2)}) collective-permute-start(bf16[136,128]{1,0:T(8,128)(2,1)S(1)} %narrow.1.mine), channel_id=1, source_target_pairs={{0,2},{1,3},{2,0},{3,1},{4,6},{5,7},{6,4},{7,5},{8,10},{9,11},{10,... | collective-permute-start | bytes 104456 | tf_op jit(solution)/shard_map/ppermute | solution.py:365
  10.3 9.0 %copy-start = (bf16[3,32,32]{2,1,0:T(8,128)(2,1)S(1)}, bf16[3,32,32]{2,1,0:T(8,128)(2,1)}, u32[]{:S(2)}) copy-start(bf16[3,32,32]{2,1,0:T(8,128)(2,1)} %w_qkv.1) | copy-start | bytes 18436
  10.3 6.4 %collective-permute-start.4 = (bf16[136,128]{1,0:T(8,128)(2,1)S(1)}, bf16[136,128]{1,0:T(8,128)(2,1)S(1)}, u32[]{:S(2)}, u32[]{:S(2)}) collective-permute-start(bf16[136,128]{1,0:T(8,128)(2,1)S(1)} %near.1.refs_0_), channel_id=1, source_target_pairs={{0,12},{1,13},{2,14},{3,15},{4,8},{5,9},{6,10},{7,11},{8,4},{9,5},... | collective-permute-start | bytes 104456 | tf_op jit(solution)/shard_map/ppermute | solution.py:365
  14.4 4.8 %collective-permute-start.3 = (bf16[136,128]{1,0:T(8,128)(2,1)S(1)}, bf16[136,128]{1,0:T(8,128)(2,1)S(1)}, u32[]{:S(2)}, u32[]{:S(2)}) collective-permute-start(bf16[136,128]{1,0:T(8,128)(2,1)S(1)} %near.1.refs_0_), channel_id=1, source_target_pairs={{0,8},{1,9},{2,10},{3,11},{4,12},{5,13},{6,14},{7,15},{8,0},{9,1},... | collective-permute-start | bytes 104456 | tf_op jit(solution)/shard_map/ppermute | solution.py:365
  14.4 4.8 %collective-permute-start.2 = (bf16[136,128]{1,0:T(8,128)(2,1)S(1)}, bf16[136,128]{1,0:T(8,128)(2,1)S(1)}, u32[]{:S(2)}, u32[]{:S(2)}) collective-permute-start(bf16[136,128]{1,0:T(8,128)(2,1)S(1)} %near.1.refs_0_), channel_id=1, source_target_pairs={{0,4},{1,5},{2,6},{3,7},{4,0},{5,1},{6,2},{7,3},{8,12},{9,13},{10,... | collective-permute-start | bytes 104456 | tf_op jit(solution)/shard_map/ppermute | solution.py:365
  21.1 1.6 %collective-permute-start.5 = (f32[104,256]{1,0:T(8,128)S(1)}, f32[104,256]{1,0:T(8,128)S(1)}, u32[]{:S(2)}, u32[]{:S(2)}) collective-permute-start(f32[104,256]{1,0:T(8,128)S(1)} %mix.1.refs_0_), channel_id=1, source_target_pairs={{0,1},{1,0},{2,3},{3,2},{4,5},{5,4},{6,7},{7,6},{8,9},{9,8},{10,11... | collective-permute-start | bytes 319496 | tf_op jit(solution)/shard_map/ppermute | solution.py:365
  24.8 1.7 %collective-permute-start.6 = (bf16[448,256]{1,0:T(8,128)(2,1)S(1)}, bf16[448,256]{1,0:T(8,128)(2,1)S(1)}, u32[]{:S(2)}, u32[]{:S(2)}) collective-permute-start(bf16[448,256]{1,0:T(8,128)(2,1)S(1)} %get-tuple-element.88), channel_id=1, source_target_pairs={{0,1},{1,0},{2,3},{3,2},{4,5},{5,4},{6,7},{7,6},{8,9},{9,8},{10,11... | collective-permute-start | bytes 688136 | tf_op jit(solution)/shard_map/ppermute | solution.py:365
  50.8 1.5 %collective-permute-start.7 = (bf16[448,256]{1,0:T(8,128)(2,1)S(1)}, bf16[448,256]{1,0:T(8,128)(2,1)S(1)}, u32[]{:S(2)}, u32[]{:S(2)}) collective-permute-start(bf16[448,256]{1,0:T(8,128)(2,1)S(1)} %bitcast.6), channel_id=1, source_target_pairs={{0,1},{1,0},{2,3},{3,2},{4,5},{5,4},{6,7},{7,6},{8,9},{9,8},{10,11... | collective-permute-start | bytes 688136 | tf_op jit(solution)/shard_map/ppermute | solution.py:365

commit v5 on v4

--- a/solution.py
+++ b/solution.py
@@ -16,7 +16,7 @@
 HEAD = 32
 WIDTH = HEADS * HEAD
 ROWS1 = 136
-ROWS2 = 408
+ROWS2 = 808
 LOG2E = math.log2(math.e)
 CHUNK = 1024
 WRITE = 256
@@ -192,7 +192,8 @@
     inverse = 1.0 / denom
     tokens = numer * inverse
     maps = [w_qkv[k].astype(F32) for k in range(3)]
-    q, key, val = [nn(m.T, tokens, FINE) for m in maps]
+    qkv = nn(jnp.concatenate([m.T for m in maps], axis=0), tokens, FINE)
+    q, key, val = qkv[0:32], qkv[32:64], qkv[64:96]
     key_rows, val_rows = key.T, val.T
     scores = nn(key_rows, q, FINE) * (1.0 / math.sqrt(HEAD))
     same = iota((256, 256), 0) // SLICES == iota((256, 256), 1) // SLICES
@@ -213,20 +214,15 @@
     out[0:32, :] = d_numer.astype(BF16).astype(F32)
     out[32:64, :] = mixed.astype(BF16).astype(F32)
     out[64:72, :] = jnp.broadcast_to(d_denom, (8, 256))
-    for k in range(3):
-        out[72:104, 32 * k : 32 * k + 32] = nt(tokens, grads[k], FINE)
+    out[72:104, 0:96] = nt(tokens, jnp.concatenate(grads, axis=0), FINE)
     out[72:104, 96:256] = jnp.zeros((32, 160), F32)
 
 
-def backward_kernel(scale, cells, cot, wsd, wtc, weights, proj, fd, stats, tanhs, softs, *refs):
-    if scale is None:
-        (e,), refs = refs[:1], refs[1:]
-    else:
-        (own, e, grad_qkv), refs = (*refs[:2], refs[5]), (*refs[2:5], *refs[6:])
-        for k in range(3):
-            block = slice(32 * k, 32 * k + 32)
-            grad_qkv[k] = (own[72:104, block] + e[72:104, block]) * scale
-    hid, dpf, payload, dlog, dtemp, lhs_h, lhs_w, dden = refs
+def backward_kernel(
+    cells, cot, wsd, wtc, weights, proj, fd, stats, tanhs, softs, e,
+    hid, dpf, payload,
+    dlog, dtemp, lhs_h, lhs_w, dden,
+):
     rows = cells.shape[0]
     diag64 = iota((256, 256), 0) // 64 == iota((256, 256), 1) // 64
     diag32 = iota((128, 256), 0) // 32 == iota((128, 256), 1) // 64
@@ -262,8 +258,11 @@
         return carry
 
     lax.fori_loop(0, rows // CHUNK, chunk, 0)
-    payload[0:128, :] = nn(hid[...], cot[...]).astype(BF16)
-    payload[128:384, :] = nn(dpf[...], cells[...]).astype(BF16)
+    d_out = nn(hid[...], cot[...]).astype(BF16)
+    d_in = nn(dpf[...], cells[...]).astype(BF16)
+    for i, grad in enumerate((d_out, d_in[0:128], d_in[128:256])):
+        payload[256 * i : 256 * i + 128, :] = grad[:, 0:128]
+        payload[256 * i + 128 : 256 * i + 256, :] = grad[:, 128:256]
     even = jnp.zeros((HEAD, 128), F32)
     odd = jnp.zeros((HEAD, 128), F32)
     for q in range(2):
@@ -271,19 +270,16 @@
         even = even + nt(proj[64 * q : 64 * q + 32, :], pair)
         odd = odd + nt(proj[64 * q + 32 : 64 * q + 64, :], pair)
     d_slice = jnp.where(iota((HEAD, 128), 1) < SLICES, even, odd)
-    d_slice = jnp.concatenate([d_slice[0:16], d_slice[16:32]], axis=1)
     d_temp = nt(dtemp[...].astype(BF16), proj[...])
     here = iota((HEADS, 128), 0) == iota((HEADS, 128), 1) // HEAD
     d_temp = jnp.sum(jnp.where(here, d_temp, 0.0), axis=0, keepdims=True)
-    d_temp = jnp.concatenate(
-        [jnp.broadcast_to(d_temp, (8, 128)), jnp.zeros((8, 128), F32)], axis=1
-    )
-    payload[384:408, :] = jnp.concatenate([d_slice, d_temp], axis=0).astype(BF16)
-    payload[ROWS2:, :] = jnp.zeros((payload.shape[0] - ROWS2, WIDTH), BF16)
-
-
-def write_rows(out, stage, sems, product):
-    copies = []
+    d_temp = jnp.broadcast_to(d_temp, (8, 128))
+    payload[768:ROWS2, :] = jnp.concatenate([d_slice, d_temp], axis=0).astype(BF16)
+    payload[ROWS2:, :] = jnp.zeros((payload.shape[0] - ROWS2, 128), BF16)
+
+
+def write_rows(out, stage, sems, product, copies=()):
+    copies = list(copies)
     for j in range(out.shape[0] // WRITE):
         at = pl.ds(j * WRITE, WRITE)
         stage[at, :] = product(at).T.astype(BF16)
@@ -293,15 +289,22 @@
         copy.wait()
 
 
-def result_kernel(own, far, w_out, out, table, stage, sems):
+def result_kernel(
+    scale, own, far, w_out, e_own, e_far, out, grad_qkv, qkv, sem, table, stage, sems,
+):
     core = lax.rem(lax.axis_index("dom"), 2)
+    for k in range(3):
+        block = slice(32 * k, 32 * k + 32)
+        qkv[k] = (e_own[72:104, block] + e_far[72:104, block]) * scale
+    copy = pltpu.make_async_copy(qkv, grad_qkv, sem.at[0])
+    copy.start()
     order = [w_out[group_rows(g), :] for g in (core, 1 - core)]
     table[...] = jnp.concatenate(order, axis=0).T
 
     def product(at):
         return nn(table[...], jnp.concatenate([own[:, at], far[:, at]], axis=0))
 
-    write_rows(out, stage, sems, product)
+    write_rows(out, stage, sems, product, [copy])
 
 
 def grad_cells_kernel(own, far, w_x, w_fx, out, table, stage, sems):
@@ -316,21 +319,37 @@
     write_rows(out, stage, sems, product)
 
 
-def place_kernel(mine, other, d_x, d_fx, d_slice, d_temp, d_out):
+def place_kernel(mine, other, *refs):
+    outs, (d_x, d_fx, d_slice, d_temp, d_out), sems = refs[:5], refs[5:10], refs[10]
     core = lax.rem(lax.axis_index("dom"), 2)
-    for ref, g in ((mine, core), (other, 1 - core)):
-        at = group_rows(g)
-        d_out[at, :] = ref[0:128, :].astype(F32)
-        d_x[:, at] = ref[128:256, :].astype(F32).T
-        d_fx[:, at] = ref[256:384, :].astype(F32).T
-    small = mine[384:ROWS2, :].astype(F32) + other[384:ROWS2, :].astype(F32)
-    rows = jnp.concatenate([small[0:16, 0:128], small[0:16, 128:256]], axis=0)
-    rows = rows + pltpu.roll(rows, 64, 1)
+    copies = []
+
+    def copy_out(i):
+        copies.append(pltpu.make_async_copy(refs[5 + i], outs[i], sems.at[i]))
+        copies[-1].start()
+
+    parts = ((mine, group_rows(core)), (other, group_rows(1 - core)))
+    for ref, at in parts:
+        d_out[at, 0:128] = ref[0:128, :].astype(F32)
+        d_out[at, 128:256] = ref[128:256, :].astype(F32)
+    copy_out(4)
+    for i, grad in enumerate((d_x, d_fx)):
+        first = 256 * i + 256
+        for ref, at in parts:
+            grad[0:128, at] = ref[first : first + 128, :].astype(F32).T
+            grad[128:256, at] = ref[first + 128 : first + 256, :].astype(F32).T
+        copy_out(i)
+    small = mine[768:ROWS2, :].astype(F32) + other[768:ROWS2, :].astype(F32)
+    rows = small[0:32] + pltpu.roll(small[0:32], 64, 1)
     d_slice[...] = rows[:, 0:SLICES]
-    v = small[16:24, 0:128]
+    copy_out(2)
+    v = small[32:40]
     v = v + pltpu.roll(v, 64, 1)
     v = v + pltpu.roll(v, 32, 1)
-    d_temp[...] = v[0:1, 0:32]
+    d_temp[...] = v[0:1, 0:HEAD]
+    copy_out(3)
+    for copy in copies:
+        copy.wait()
 
 
 VMEM = pl.BlockSpec(memory_space=pltpu.VMEM)
@@ -446,7 +465,7 @@
     grads = [
         ((WIDTH // 2, rows), BF16),
         ((WIDTH, rows), BF16),
-        ((half, WIDTH), BF16),
+        ((half, 128), BF16),
     ]
     scratch = [
         ((hgm, rows), BF16),
@@ -456,7 +475,7 @@
         ((hgm, CHUNK), F32),
     ]
     hid_own, dpf_own, keep = call(
-        functools.partial(backward_kernel, None),
+        backward_kernel,
         grads,
         (cells, cotangent, wsd, wtc, *own, *again[:2], mine),
         scratch=scratch,
@@ -464,21 +483,23 @@
         flops=8 * rows * WIDTH * WIDTH,
     )
     other, keep = lax.optimization_barrier((other, keep))
-    hid_far, dpf_far, send, grad_qkv = call(
-        functools.partial(backward_kernel, scale),
-        grads + [((3, HEAD, HEAD), F32)],
-        (cells, cotangent, wsd, wtc, *far, *again[2:], mine, other),
+    maps = other
+    hid_far, dpf_far, send = call(
+        backward_kernel,
+        grads,
+        (cells, cotangent, wsd, wtc, *far, *again[2:], maps),
         scratch=scratch,
         name="backward_far",
     )
     other = swap(send, 1)
     staging = [((rows, WIDTH), BF16), pltpu.SemaphoreType.DMA((rows // WRITE,))]
-    (result,) = call(
-        result_kernel,
-        [((rows, WIDTH), BF16)],
-        (hid_own, hid_far, w_out),
-        scratch=[((WIDTH, WIDTH), BF16)] + staging,
-        outs=[HBM],
+    result, grad_qkv = call(
+        functools.partial(result_kernel, scale),
+        [((rows, WIDTH), BF16), ((3, HEAD, HEAD), F32)],
+        (hid_own, hid_far, w_out, mine, maps),
+        scratch=[((3, HEAD, HEAD), F32), pltpu.SemaphoreType.DMA((1,)), ((WIDTH, WIDTH), BF16)]
+        + staging,
+        outs=[HBM, HBM],
         name="result",
         flops=2 * rows * WIDTH * WIDTH,
     )
@@ -492,7 +513,7 @@
         name="grad_cells",
         flops=4 * rows * WIDTH * WIDTH,
     )
-    (summed,) = call(narrow_add_kernel, [((half, WIDTH), BF16)], (keep, other), name="pair_add")
+    (summed,) = call(narrow_add_kernel, [((half, 128), BF16)], (keep, other), name="pair_add")
     parts = exchange(summed)
 
     def gather(parts_ref, out):
@@ -500,19 +521,22 @@
         for k in range(peers):
             out[chunk * k : chunk * k + chunk, :] = total
 
-    (spread,) = call(gather, [((half, WIDTH), BF16)], (parts,), name="gather")
+    (spread,) = call(gather, [((half, 128), BF16)], (parts,), name="gather")
     mine = exchange(spread)
     other = swap(mine, 1)
+    shapes = [
+        ((WIDTH, WIDTH), F32),
+        ((WIDTH, WIDTH), F32),
+        ((HEAD, SLICES), F32),
+        ((1, HEAD), F32),
+        ((WIDTH, WIDTH), F32),
+    ]
     d_x, d_fx, d_slice, d_temp, d_out = call(
         place_kernel,
-        [
-            ((WIDTH, WIDTH), F32),
-            ((WIDTH, WIDTH), F32),
-            ((HEAD, SLICES), F32),
-            ((1, HEAD), F32),
-            ((WIDTH, WIDTH), F32),
-        ],
+        shapes,
         (mine, other),
+        scratch=[*shapes, pltpu.SemaphoreType.DMA((5,))],
+        outs=[HBM] * 5,
         name="place",
     )
     return result, grad_cells, d_x, d_fx, d_slice, d_temp.reshape(HEAD), grad_qkv, d_out

time: 53.6 us -> 52.5 us (0.979)
  blocking collectives: 24.3 us -> 23.6 us
    all_to_all x2, blocking collectives: 24.3 us -> 23.6 us  [exchange(): return lax.all_to_all(x, 'dom', 0, 0, axis_index_groups=groups, tiled=True)]
where the time goes in v5:
time: 52.5 us; the launch traced here: 52.3 us
  blocking collectives  23.6 us (45%)
  Pallas kernels  13 us (25%)
  starting transfers between devices  8.59 us (16%)
  waiting for transfers between devices  5.64 us (11%)
  between operations  1.38 us (3%)
    all_to_all x2, blocking collectives, exchange(): return lax.all_to_all(x, 'dom', 0, 0, axis_index_groups=groups, tiled=True)  23.6 us
    pallas_call x13, Pallas kernels, call(): pl.pallas_call(kernel, out_shape=[jax.ShapeDtypeStruct(s, d) for s, d in...  13 us
    ppermute x8, starting transfers between devices, swap(): return lax.ppermute(x, 'dom', [(i, i ^ mask) for i in range(devices)])  8.59 us
    ppermute x8, waiting for transfers between devices, swap(): return lax.ppermute(x, 'dom', [(i, i ^ mask) for i in range(devices)])  5.64 us
  transfers between devices with their start and end apart: 8, of which 4 were waited for; matrix products, arithmetic and copies ran while one was open for 0% of the time, Pallas kernels for 11%

profile of v5, /device:TPU:0, one launch (start us, length us, event | category | flops | bytes accessed | tf_op | source)
XLA Modules:
  0.0 52.3 jit_solution(6131281675895886571)
XLA Ops:
  1.3 2.6 %forward_far.1 = (bf16[256,1024]{1,0:T(8,128)(2,1)S(1)}, bf16[128,1024]{1,0:T(8,128)(2,1)S(1)}, bf16[256,1024]{1,0:T(8,128)(2,1)S(1)}, f32[32,1024]{1,0:T(8,128)...) custom-call(s32[1]{0:T(128)S(6)} %copy.17.counts, ...), custom_call_target="tpu_custom_call" | custom-call | tf_op jit(solution)/shard_map/forward_far/pallas_call | solution.py:363
  3.9 0.5 %collective-permute-start = (f32[136,128]{1,0:T(8,128)S(1)}, f32[136,128]{1,0:T(8,128)S(1)}, u32[]{:S(2)}, u32[]{:S(2)}) collective-permute-start(f32[136,128]{1,0:T(8,128)S(1)} %get-tuple-element.65), channel_id=1, source_target_pairs={{0,1},{1,0},{2,3},{3,2},{4,5},{5,4},{6,7},{7,6},{8,9},{9,8},{10,11... | collective-permute-start | bytes 208904 | tf_op jit(solution)/shard_map/ppermute | solution.py:384
  4.5 1.1 %forward_own.1 = (bf16[256,1024]{1,0:T(8,128)(2,1)S(1)}, bf16[128,1024]{1,0:T(8,128)(2,1)S(1)}, bf16[256,1024]{1,0:T(8,128)(2,1)S(1)}, f32[32,1024]{1,0:T(8,128)S(1)}, f32[136,128]{1,0:T(8,128)S(1)}) custom-call(s32[1]{0:T(128)S(6)} %copy.17.counts, bf16[1024,256]{1,0:T(8,128)(2,1)S(1)} %get-tuple-element.57.refs_0_.cells, ...), custom_call_target="tpu_custom_call" | custom-call | flops 402653184 | tf_op jit(solution)/shard_map/forward_own/pallas_call | solution.py:363
  5.6 0.0 collective-permute-done.other
  5.6 2.7 %collective-permute-start.1 = (bf16[136,128]{1,0:T(8,128)(2,1)S(1)}, bf16[136,128]{1,0:T(8,128)(2,1)S(1)}, u32[]{:S(2)}, u32[]{:S(2)}) collective-permute-start(bf16[136,128]{1,0:T(8,128)(2,1)S(1)} %narrow.1.mine), channel_id=1, source_target_pairs={{0,2},{1,3},{2,0},{3,1},{4,6},{5,7},{6,4},{7,5},{8,10},{9,11},{10,... | collective-permute-start | bytes 104456 | tf_op jit(solution)/shard_map/ppermute | solution.py:384
  8.3 0.7 %softmax.1 = (f32[256,1024]{1,0:T(8,128)S(1)}, f32[256,1024]{1,0:T(8,128)S(1)}, f32[256,1024]{1,0:T(8,128)S(1)}, f32[256,1024]{1,0:T(8,128)S(1)}) custom-call(bf16[256,128]{1,0:T(8,128)(2,1)S(1)} %get-tuple-element.69.refs_5_.wsb, bf16[128,1024]{1,0:T(8,128)(2,1)S(1)} %get-tuple-element.74.refs_0_.proj, f32[32,1024]{1,0:T(8,128)S(1)} %get-tuple-element.75.refs_1_.stats, ...), custom_call_target="tpu_custom_call" | custom-call | flops 134217728 | tf_op jit(solution)/shard_map/softmax/pallas_call | solution.py:363
  9.0 1.2 %collective-permute-done.1.other = bf16[136,128]{1,0:T(8,128)(2,1)S(1)} collective-permute-done((bf16[136,128]{1,0:T(8,128)(2,1)S(1)}, bf16[136,128]{1,0:T(8,128)(2,1)S(1)}, u32[]{:S(2)}, u32[]{:S(2)}) %collective-permute-start.1) | collective-permute-done | bytes 34848 | tf_op jit(solution)/shard_map/ppermute | solution.py:384
  10.3 0.0 copy-start
  10.3 4.1 %collective-permute-start.4 = (bf16[136,128]{1,0:T(8,128)(2,1)S(1)}, bf16[136,128]{1,0:T(8,128)(2,1)S(1)}, u32[]{:S(2)}, u32[]{:S(2)}) collective-permute-start(bf16[136,128]{1,0:T(8,128)(2,1)S(1)} %near.1.refs_0_), channel_id=1, source_target_pairs={{0,12},{1,13},{2,14},{3,15},{4,8},{5,9},{6,10},{7,11},{8,4},{9,5},... | collective-permute-start | bytes 104456 | tf_op jit(solution)/shard_map/ppermute | solution.py:384
  14.4 0.0 collective-permute-start.3
  14.4 0.6 %collective-permute-start.2 = (bf16[136,128]{1,0:T(8,128)(2,1)S(1)}, bf16[136,128]{1,0:T(8,128)(2,1)S(1)}, u32[]{:S(2)}, u32[]{:S(2)}) collective-permute-start(bf16[136,128]{1,0:T(8,128)(2,1)S(1)} %near.1.refs_0_), channel_id=1, source_target_pairs={{0,4},{1,5},{2,6},{3,7},{4,0},{5,1},{6,2},{7,3},{8,12},{9,13},{10,... | collective-permute-start | bytes 104456 | tf_op jit(solution)/shard_map/ppermute | solution.py:384
  15.1 1.6 %collective-permute-done.4.refs_3_ = bf16[136,128]{1,0:T(8,128)(2,1)S(1)} collective-permute-done((bf16[136,128]{1,0:T(8,128)(2,1)S(1)}, bf16[136,128]{1,0:T(8,128)(2,1)S(1)}, u32[]{:S(2)}, u32[]{:S(2)}) %collective-permute-start.4) | collective-permute-done | bytes 34848 | tf_op jit(solution)/shard_map/ppermute | solution.py:384
  16.7 2.6 %collective-permute-done.3.refs_2_ = bf16[136,128]{1,0:T(8,128)(2,1)S(1)} collective-permute-done((bf16[136,128]{1,0:T(8,128)(2,1)S(1)}, bf16[136,128]{1,0:T(8,128)(2,1)S(1)}, u32[]{:S(2)}, u32[]{:S(2)}) %collective-permute-start.3) | collective-permute-done | bytes 34848 | tf_op jit(solution)/shard_map/ppermute | solution.py:384
  19.3 0.0 collective-permute-done.2.refs_1_
  19.3 0.0 copy-done
  19.3 1.7 %mix.1.e.e_own = f32[104,256]{1,0:T(8,128)S(1)} custom-call(bf16[3,32,32]{2,1,0:T(8,128)(2,1)S(1)} %copy-done, bf16[136,128]{1,0:T(8,128)(2,1)S(1)} %near.1.refs_0_, bf16[136,128]{1,0:T(8,128)(2,1)S(1)} %collective-permute-done.2.refs_1_, bf16[136,128]{1,0:T(8,128)(2,1)S(1)} %collective-permute-done.3.refs_2_, ...), custom_call_target="tpu_custom_call" | custom-call | tf_op jit(solution)/shard_map/mix/pallas_call | solution.py:363
  21.0 0.0 collective-permute-start.5
  21.0 1.6 %backward_own.1 = (bf16[128,1024]{1,0:T(8,128)(2,1)S(1)}, bf16[256,1024]{1,0:T(8,128)(2,1)S(1)}, bf16[832,128]{1,0:T(8,128)(2,1)S(1)}) custom-call(bf16[1024,256]{1,0:T(8,128)(2,1)S(1)} %get-tuple-element.57.refs_0_.cells, bf16[1024,256]{1,0:T(8,128)(2,1)S(1)} %get-tuple-element.58.refs_1_.cot, bf16[128,256]{1,0:T(8,128)(2,1)S(1)} %get-tuple-element.59.wsd, ...), custom_call_target="tpu_custom_call" | custom-call | flops 536870912 | tf_op jit(solution)/shard_map/backward_own/pallas_call | solution.py:363
  22.7 0.0 collective-permute-done.5.e.e_far
  22.7 1.7 %backward_far.1 = (bf16[128,1024]{1,0:T(8,128)(2,1)S(1)}, bf16[256,1024]{1,0:T(8,128)(2,1)S(1)}, bf16[832,128]{1,0:T(8,128)(2,1)S(1)}) custom-call(bf16[1024,256]{1,0:T(8,128)(2,1)S(1)} %get-tuple-element.57.refs_0_.cells, bf16[1024,256]{1,0:T(8,128)(2,1)S(1)} %get-tuple-element.58.refs_1_.cot, bf16[128,256]{1,0:T(8,128)(2,1)S(1)} %get-tuple-element.59.wsd, ...), custom_call_target="tpu_custom_call" | custom-call | tf_op jit(solution)/shard_map/backward_far/pallas_call | solution.py:363
  24.3 0.5 collective-permute-start.6
  24.8 1.2 %result.1 = (bf16[1024,256]{1,0:T(8,128)(2,1)}, f32[3,32,32]{2,1,0:T(8,128)}) custom-call(bf16[128,1024]{1,0:T(8,128)(2,1)S(1)} %get-tuple-element.90.own, bf16[128,1024]{1,0:T(8,128)(2,1)S(1)} %get-tuple-element.91.far, bf16[256,256]{1,0:T(8,128)(2,1)S(1)} %get-tuple-element.66.refs_2_.w_out, f32[104,256]{1,0:T(8,128)S(1)} %mix.1.e.e_own, ...), custom_call_target="tpu_custom_call" | custom-call | flops 134217728 | tf_op jit(solution)/shard_map/result/pallas_call | solution.py:363
  26.1 0.0 collective-permute-done.6.other
  26.1 0.1 pair_add.1
  26.1 12.7 %all_to_all.22 = bf16[8,104,128]{2,1,0:T(8,128)(2,1)S(1)} all-to-all(bf16[8,104,128]{2,1,0:T(8,128)(2,1)S(1)} %bitcast.6), channel_id=1, replica_groups={{0,2,4,6,8,10,12,14},{1,3,5,7,9,11,13,15},{16,18,20,22,24,26,28,30},{17..., dimensions={0} | all-to-all | bytes 425984 | tf_op jit(solution)/shard_map/all_to_all | solution.py:387
  38.8 11.0 %all_to_all.23 = bf16[8,104,128]{2,1,0:T(8,128)(2,1)S(1)} all-to-all(bf16[8,104,128]{2,1,0:T(8,128)(2,1)S(1)} %bitcast.10), channel_id=1, replica_groups={{0,2,4,6,8,10,12,14},{1,3,5,7,9,11,13,15},{16,18,20,22,24,26,28,30},{17..., dimensions={0} | all-to-all | bytes 425984 | tf_op jit(solution)/shard_map/all_to_all | solution.py:387
  49.8 0.0 collective-permute-start.7
  49.8 1.2 %grad_cells.1 = bf16[1024,256]{1,0:T(8,128)(2,1)} custom-call(bf16[256,1024]{1,0:T(8,128)(2,1)S(1)} %get-tuple-element.94.own, bf16[256,1024]{1,0:T(8,128)(2,1)S(1)} %get-tuple-element.95.far, bf16[256,256]{1,0:T(8,128)(2,1)S(1)} %get-tuple-element.96.w_x, bf16[256,256]{1,0:T(8,128)(2,1)S(1)} %get-tuple-element.97.w_fx), custom_call_target="tpu_custom_call" | custom-call | flops 268435456 | tf_op jit(solution)/shard_map/grad_cells/pallas_call | solution.py:363
  51.1 0.2 collective-permute-done.7.other
  51.3 1.0 %place.1 = (f32[256,256]{1,0:T(8,128)}, f32[256,256]{1,0:T(8,128)}, f32[32,64]{1,0:T(8,128)}, f32[1,32]{1,0:T(1,128)}, f32[256,256]{1,0:T(8,128)}) custom-call(bf16[832,128]{1,0:T(8,128)(2,1)S(1)} %bitcast.8, bf16[832,128]{1,0:T(8,128)(2,1)S(1)} %collective-permute-done.7.other), custom_call_target="tpu_custom_call" | custom-call | tf_op jit(solution)/shard_map/place/pallas_call | solution.py:363
  (3 shorter events, 0.1 us)
Async XLA Ops:
  3.9 1.6 %collective-permute-start = (f32[136,128]{1,0:T(8,128)S(1)}, f32[136,128]{1,0:T(8,128)S(1)}, u32[]{:S(2)}, u32[]{:S(2)}) collective-permute-start(f32[136,128]{1,0:T(8,128)S(1)} %get-tuple-element.65), channel_id=1, source_target_pairs={{0,1},{1,0},{2,3},{3,2},{4,5},{5,4},{6,7},{7,6},{8,9},{9,8},{10,11... | collective-permute-start | bytes 208904 | tf_op jit(solution)/shard_map/ppermute | solution.py:384
  5.6 4.7 %collective-permute-start.1 = (bf16[136,128]{1,0:T(8,128)(2,1)S(1)}, bf16[136,128]{1,0:T(8,128)(2,1)S(1)}, u32[]{:S(2)}, u32[]{:S(2)}) collective-permute-start(bf16[136,128]{1,0:T(8,128)(2,1)S(1)} %narrow.1.mine), channel_id=1, source_target_pairs={{0,2},{1,3},{2,0},{3,1},{4,6},{5,7},{6,4},{7,5},{8,10},{9,11},{10,... | collective-permute-start | bytes 104456 | tf_op jit(solution)/shard_map/ppermute | solution.py:384
  10.3 9.0 %copy-start = (bf16[3,32,32]{2,1,0:T(8,128)(2,1)S(1)}, bf16[3,32,32]{2,1,0:T(8,128)(2,1)}, u32[]{:S(2)}) copy-start(bf16[3,32,32]{2,1,0:T(8,128)(2,1)} %w_qkv.1) | copy-start | bytes 18436
  10.3 6.4 %collective-permute-start.4 = (bf16[136,128]{1,0:T(8,128)(2,1)S(1)}, bf16[136,128]{1,0:T(8,128)(2,1)S(1)}, u32[]{:S(2)}, u32[]{:S(2)}) collective-permute-start(bf16[136,128]{1,0:T(8,128)(2,1)S(1)} %near.1.refs_0_), channel_id=1, source_target_pairs={{0,12},{1,13},{2,14},{3,15},{4,8},{5,9},{6,10},{7,11},{8,4},{9,5},... | collective-permute-start | bytes 104456 | tf_op jit(solution)/shard_map/ppermute | solution.py:384
  14.4 4.8 %collective-permute-start.3 = (bf16[136,128]{1,0:T(8,128)(2,1)S(1)}, bf16[136,128]{1,0:T(8,128)(2,1)S(1)}, u32[]{:S(2)}, u32[]{:S(2)}) collective-permute-start(bf16[136,128]{1,0:T(8,128)(2,1)S(1)} %near.1.refs_0_), channel_id=1, source_target_pairs={{0,8},{1,9},{2,10},{3,11},{4,12},{5,13},{6,14},{7,15},{8,0},{9,1},... | collective-permute-start | bytes 104456 | tf_op jit(solution)/shard_map/ppermute | solution.py:384
  14.4 4.8 %collective-permute-start.2 = (bf16[136,128]{1,0:T(8,128)(2,1)S(1)}, bf16[136,128]{1,0:T(8,128)(2,1)S(1)}, u32[]{:S(2)}, u32[]{:S(2)}) collective-permute-start(bf16[136,128]{1,0:T(8,128)(2,1)S(1)} %near.1.refs_0_), channel_id=1, source_target_pairs={{0,4},{1,5},{2,6},{3,7},{4,0},{5,1},{6,2},{7,3},{8,12},{9,13},{10,... | collective-permute-start | bytes 104456 | tf_op jit(solution)/shard_map/ppermute | solution.py:384
  21.0 1.7 %collective-permute-start.5 = (f32[104,256]{1,0:T(8,128)S(1)}, f32[104,256]{1,0:T(8,128)S(1)}, u32[]{:S(2)}, u32[]{:S(2)}) collective-permute-start(f32[104,256]{1,0:T(8,128)S(1)} %mix.1.e.e_own), channel_id=1, source_target_pairs={{0,1},{1,0},{2,3},{3,2},{4,5},{5,4},{6,7},{7,6},{8,9},{9,8},{10,11... | collective-permute-start | bytes 319496 | tf_op jit(solution)/shard_map/ppermute | solution.py:384
  24.3 1.7 %collective-permute-start.6 = (bf16[832,128]{1,0:T(8,128)(2,1)S(1)}, bf16[832,128]{1,0:T(8,128)(2,1)S(1)}, u32[]{:S(2)}, u32[]{:S(2)}) collective-permute-start(bf16[832,128]{1,0:T(8,128)(2,1)S(1)} %get-tuple-element.89), channel_id=1, source_target_pairs={{0,1},{1,0},{2,3},{3,2},{4,5},{5,4},{6,7},{7,6},{8,9},{9,8},{10,11... | collective-permute-start | bytes 638984 | tf_op jit(solution)/shard_map/ppermute | solution.py:384
  49.8 1.5 %collective-permute-start.7 = (bf16[832,128]{1,0:T(8,128)(2,1)S(1)}, bf16[832,128]{1,0:T(8,128)(2,1)S(1)}, u32[]{:S(2)}, u32[]{:S(2)}) collective-permute-start(bf16[832,128]{1,0:T(8,128)(2,1)S(1)} %bitcast.7), channel_id=1, source_target_pairs={{0,1},{1,0},{2,3},{3,2},{4,5},{5,4},{6,7},{7,6},{8,9},{9,8},{10,11... | collective-permute-start | bytes 638984 | tf_op jit(solution)/shard_map/ppermute | solution.py:384

commit v6 on v5

--- a/solution.py
+++ b/solution.py
@@ -159,17 +159,21 @@
     out[...] = (mine[...].astype(F32) + other[...].astype(F32)).astype(BF16)
 
 
-def softmax_kernel(wsb, *refs):
+def softmax_kernel(wsb, w_qkv, *refs):
+    for k in range(3):
+        refs[10][HEAD * k : HEAD * k + HEAD, :] = w_qkv[k].astype(F32).T
+
     def chunk(j, carry):
         at = chunk_of(j)
         for g in range(2):
             proj, stats = refs[2 * g : 2 * g + 2]
-            tanhs, soft = refs[4 + 2 * g : 6 + 2 * g]
+            tanhs, soft, slope = refs[4 + 3 * g : 7 + 3 * g]
             x = nn(wsb[...], proj[:, at])
             for k in range(4):
                 rng = slice(SLICES * k, SLICES * k + SLICES)
                 t = jnp.tanh(x[rng] * 0.1)
                 tanhs[rng, at] = t
+                slope[rng, at] = (1.0 - t * t) * stats[8 + k : 9 + k, at]
                 soft[rng, at] = jnp.exp2(t * stats[k : k + 1, at]) * stats[24 + k : 25 + k, at]
         return carry
 
@@ -183,7 +187,7 @@
     return total
 
 
-def mix_kernel(w_qkv, *refs):
+def mix_kernel(w_qkv, turned, *refs):
     parts, out = refs[:-1], refs[-1]
     total = sum(part[...].astype(F32) for part in parts)
     numer = jnp.concatenate([total[0:32], total[64:96]], axis=1)
@@ -192,7 +196,7 @@
     inverse = 1.0 / denom
     tokens = numer * inverse
     maps = [w_qkv[k].astype(F32) for k in range(3)]
-    qkv = nn(jnp.concatenate([m.T for m in maps], axis=0), tokens, FINE)
+    qkv = nn(turned[...], tokens, FINE)
     q, key, val = qkv[0:32], qkv[32:64], qkv[64:96]
     key_rows, val_rows = key.T, val.T
     scores = nn(key_rows, q, FINE) * (1.0 / math.sqrt(HEAD))
@@ -219,7 +223,7 @@
 
 
 def backward_kernel(
-    cells, cot, wsd, wtc, weights, proj, fd, stats, tanhs, softs, e,
+    cells, cot, wsd, wtc, weights, proj, fd, stats, tanhs, softs, slopes, e,
     hid, dpf, payload,
     dlog, dtemp, lhs_h, lhs_w, dden,
 ):
@@ -231,7 +235,7 @@
     for i in range(2):
         part = jnp.concatenate([e[32 - 32 * i : 64 - 32 * i, :]] * 4, axis=0)
         lhs_h[128 * i : 128 * i + 128, :] = jnp.where(diag32, part, 0.0).astype(BF16)
-    dden[...] = jnp.broadcast_to(e[64:72, :].T[:, 0:1], (256, CHUNK))
+    dden[...] = jnp.broadcast_to(e[64:72, :].T[:, 0:1], (256, 128))
     dtemp[...] = jnp.zeros(dtemp.shape, F32)
 
     def chunk(j, carry):
@@ -245,10 +249,10 @@
             rng = slice(SLICES * k, SLICES * k + SLICES)
             t = tanhs[rng, at]
             soft = softs[rng, at]
-            d = dw[rng] + dden[rng, :]
+            d = dw[rng] + jnp.concatenate([dden[rng, :]] * (CHUNK // 128), axis=1)
             inner = jnp.sum(soft * d, axis=0, keepdims=True)
             ds = soft * (d - inner)
-            dlog[rng, at] = (ds * ((1.0 - t * t) * stats[8 + k : 9 + k, at])).astype(BF16)
+            dlog[rng, at] = (ds * slopes[rng, at]).astype(BF16)
             dt = jnp.sum(ds * t, axis=0, keepdims=True) * stats[16 + k : 17 + k, at]
             dt = dt.astype(BF16).astype(F32)
             dtemp[k : k + 1, at] = dt
@@ -263,12 +267,9 @@
     for i, grad in enumerate((d_out, d_in[0:128], d_in[128:256])):
         payload[256 * i : 256 * i + 128, :] = grad[:, 0:128]
         payload[256 * i + 128 : 256 * i + 256, :] = grad[:, 128:256]
-    even = jnp.zeros((HEAD, 128), F32)
-    odd = jnp.zeros((HEAD, 128), F32)
-    for q in range(2):
-        pair = dlog[128 * q : 128 * q + 128, :]
-        even = even + nt(proj[64 * q : 64 * q + 32, :], pair)
-        odd = odd + nt(proj[64 * q + 32 : 64 * q + 64, :], pair)
+    every = nt(proj[...], dlog[...])
+    even = every[0:32, 0:128] + every[64:96, 128:256]
+    odd = every[32:64, 0:128] + every[96:128, 128:256]
     d_slice = jnp.where(iota((HEAD, 128), 1) < SLICES, even, odd)
     d_temp = nt(dtemp[...].astype(BF16), proj[...])
     here = iota((HEADS, 128), 0) == iota((HEADS, 128), 1) // HEAD
@@ -449,15 +450,15 @@
         if again is None:
             again = call(
                 softmax_kernel,
-                [((hgm, rows), F32)] * 4,
-                (wsb, own[1], own[3], far[1], far[3]),
+                [((hgm, rows), F32)] * 6 + [((3 * HEAD, HEAD), F32)],
+                (wsb, w_qkv, own[1], own[3], far[1], far[3]),
                 name="softmax",
                 flops=2 * rows * hm * 128,
             )
             other, *again = lax.optimization_barrier((other, *again))
         (total,) = call(narrow_add_kernel, [part], (total, other), name="near")
     parts = [total] + [swap(total, mask) for mask in last]
-    (mine,) = call(mix_kernel, [((104, 256), F32)], (w_qkv, *parts), name="mix")
+    (mine,) = call(mix_kernel, [((104, 256), F32)], (w_qkv, again[6], *parts), name="mix")
     other = swap(mine, 1)
     chunk = -(-ROWS2 // peers)
     chunk = -(-chunk // 8) * 8
@@ -472,12 +473,12 @@
         ((8, rows), F32),
         ((256, 256), BF16),
         ((256, 256), BF16),
-        ((hgm, CHUNK), F32),
+        ((hgm, 128), F32),
     ]
     hid_own, dpf_own, keep = call(
         backward_kernel,
         grads,
-        (cells, cotangent, wsd, wtc, *own, *again[:2], mine),
+        (cells, cotangent, wsd, wtc, *own, *again[:3], mine),
         scratch=scratch,
         name="backward_own",
         flops=8 * rows * WIDTH * WIDTH,
@@ -487,7 +488,7 @@
     hid_far, dpf_far, send = call(
         backward_kernel,
         grads,
-        (cells, cotangent, wsd, wtc, *far, *again[2:], maps),
+        (cells, cotangent, wsd, wtc, *far, *again[3:6], maps),
         scratch=scratch,
         name="backward_far",
     )

time: 52.5 us -> 52.2 us (level)
  no operation moved by 1% of the time
where the time goes in v6:
time: 52.2 us; the launch traced here: 52 us
  blocking collectives  23.6 us (45%)
  Pallas kernels  12.8 us (25%)
  starting transfers between devices  8.63 us (17%)
  waiting for transfers between devices  5.5 us (11%)
  between operations  1.4 us (3%)
    all_to_all x2, blocking collectives, exchange(): return lax.all_to_all(x, 'dom', 0, 0, axis_index_groups=groups, tiled=True)  23.6 us
    pallas_call x13, Pallas kernels, call(): pl.pallas_call(kernel, out_shape=[jax.ShapeDtypeStruct(s, d) for s, d in...  12.8 us
    ppermute x8, starting transfers between devices, swap(): return lax.ppermute(x, 'dom', [(i, i ^ mask) for i in range(devices)])  8.63 us
    ppermute x8, waiting for transfers between devices, swap(): return lax.ppermute(x, 'dom', [(i, i ^ mask) for i in range(devices)])  5.5 us
  transfers between devices with their start and end apart: 8, of which 4 were waited for; matrix products, arithmetic and copies ran while one was open for 0% of the time, Pallas kernels for 11%

profile of v6, /device:TPU:0, one launch (start us, length us, event | category | flops | bytes accessed | tf_op | source)
XLA Modules:
  0.0 52.0 jit_solution(16549871752664990088)
XLA Ops:
  1.3 2.6 %forward_far.1 = (bf16[256,1024]{1,0:T(8,128)(2,1)S(1)}, bf16[128,1024]{1,0:T(8,128)(2,1)S(1)}, bf16[256,1024]{1,0:T(8,128)(2,1)S(1)}, f32[32,1024]{1,0:T(8,128)...) custom-call(s32[1]{0:T(128)S(6)} %copy.17.counts, ...), custom_call_target="tpu_custom_call" | custom-call | tf_op jit(solution)/shard_map/forward_far/pallas_call | solution.py:364
  3.9 0.5 %collective-permute-start = (f32[136,128]{1,0:T(8,128)S(1)}, f32[136,128]{1,0:T(8,128)S(1)}, u32[]{:S(2)}, u32[]{:S(2)}) collective-permute-start(f32[136,128]{1,0:T(8,128)S(1)} %get-tuple-element.71), channel_id=1, source_target_pairs={{0,1},{1,0},{2,3},{3,2},{4,5},{5,4},{6,7},{7,6},{8,9},{9,8},{10,11... | collective-permute-start | bytes 208904 | tf_op jit(solution)/shard_map/ppermute | solution.py:385
  4.5 1.1 %forward_own.1 = (bf16[256,1024]{1,0:T(8,128)(2,1)S(1)}, bf16[128,1024]{1,0:T(8,128)(2,1)S(1)}, bf16[256,1024]{1,0:T(8,128)(2,1)S(1)}, f32[32,1024]{1,0:T(8,128)S(1)}, f32[136,128]{1,0:T(8,128)S(1)}) custom-call(s32[1]{0:T(128)S(6)} %copy.17.counts, bf16[1024,256]{1,0:T(8,128)(2,1)S(1)} %get-tuple-element.63.refs_0_.cells, ...), custom_call_target="tpu_custom_call" | custom-call | flops 402653184 | tf_op jit(solution)/shard_map/forward_own/pallas_call | solution.py:364
  5.6 0.0 collective-permute-done.other
  5.6 0.0 copy-start
  5.6 2.7 %collective-permute-start.1 = (bf16[136,128]{1,0:T(8,128)(2,1)S(1)}, bf16[136,128]{1,0:T(8,128)(2,1)S(1)}, u32[]{:S(2)}, u32[]{:S(2)}) collective-permute-start(bf16[136,128]{1,0:T(8,128)(2,1)S(1)} %narrow.1.mine), channel_id=1, source_target_pairs={{0,2},{1,3},{2,0},{3,1},{4,6},{5,7},{6,4},{7,5},{8,10},{9,11},{10,... | collective-permute-start | bytes 104456 | tf_op jit(solution)/shard_map/ppermute | solution.py:385
  8.3 0.0 copy-done
  8.3 0.8 %softmax.1 = (f32[256,1024]{1,0:T(8,128)S(1)}, f32[256,1024]{1,0:T(8,128)S(1)}, f32[256,1024]{1,0:T(8,128)S(1)}, f32[256,1024]{1,0:T(8,128)S(1)}, f32[256,1024]{...) custom-call(bf16[256,128]{1,0:T(8,128)(2,1)S(1)} %get-tuple-element.75.refs_5_.wsb, ...), custom_call_target="tpu_custom_call" | custom-call | flops 134217728 | tf_op jit(solution)/shard_map/softmax/pallas_call | solution.py:364
  9.2 1.1 %collective-permute-done.1.other = bf16[136,128]{1,0:T(8,128)(2,1)S(1)} collective-permute-done((bf16[136,128]{1,0:T(8,128)(2,1)S(1)}, bf16[136,128]{1,0:T(8,128)(2,1)S(1)}, u32[]{:S(2)}, u32[]{:S(2)}) %collective-permute-start.1) | collective-permute-done | bytes 34848 | tf_op jit(solution)/shard_map/ppermute | solution.py:385
  10.3 4.1 %collective-permute-start.4 = (bf16[136,128]{1,0:T(8,128)(2,1)S(1)}, bf16[136,128]{1,0:T(8,128)(2,1)S(1)}, u32[]{:S(2)}, u32[]{:S(2)}) collective-permute-start(bf16[136,128]{1,0:T(8,128)(2,1)S(1)} %near.1.refs_0_), channel_id=1, source_target_pairs={{0,12},{1,13},{2,14},{3,15},{4,8},{5,9},{6,10},{7,11},{8,4},{9,5},... | collective-permute-start | bytes 104456 | tf_op jit(solution)/shard_map/ppermute | solution.py:385
  14.4 0.0 collective-permute-start.3
  14.4 0.6 %collective-permute-start.2 = (bf16[136,128]{1,0:T(8,128)(2,1)S(1)}, bf16[136,128]{1,0:T(8,128)(2,1)S(1)}, u32[]{:S(2)}, u32[]{:S(2)}) collective-permute-start(bf16[136,128]{1,0:T(8,128)(2,1)S(1)} %near.1.refs_0_), channel_id=1, source_target_pairs={{0,4},{1,5},{2,6},{3,7},{4,0},{5,1},{6,2},{7,3},{8,12},{9,13},{10,... | collective-permute-start | bytes 104456 | tf_op jit(solution)/shard_map/ppermute | solution.py:385
  15.1 1.6 %collective-permute-done.4.refs_3_ = bf16[136,128]{1,0:T(8,128)(2,1)S(1)} collective-permute-done((bf16[136,128]{1,0:T(8,128)(2,1)S(1)}, bf16[136,128]{1,0:T(8,128)(2,1)S(1)}, u32[]{:S(2)}, u32[]{:S(2)}) %collective-permute-start.4) | collective-permute-done | bytes 34848 | tf_op jit(solution)/shard_map/ppermute | solution.py:385
  16.7 2.6 %collective-permute-done.3.refs_2_ = bf16[136,128]{1,0:T(8,128)(2,1)S(1)} collective-permute-done((bf16[136,128]{1,0:T(8,128)(2,1)S(1)}, bf16[136,128]{1,0:T(8,128)(2,1)S(1)}, u32[]{:S(2)}, u32[]{:S(2)}) %collective-permute-start.3) | collective-permute-done | bytes 34848 | tf_op jit(solution)/shard_map/ppermute | solution.py:385
  19.3 0.0 collective-permute-done.2.refs_1_
  19.3 1.7 %mix.1.e.e_own = f32[104,256]{1,0:T(8,128)S(1)} custom-call(bf16[3,32,32]{2,1,0:T(8,128)(2,1)S(1)} %copy-done, f32[96,32]{1,0:T(8,128)S(1)} %get-tuple-element.92.turned, bf16[136,128]{1,0:T(8,128)(2,1)S(1)} %near.1.refs_0_, bf16[136,128]{1,0:T(8,128)(2,1)S(1)} %collective-permute-done.2.refs_1_, bf16[136,128]{1,0:T(8,128)(2,1)S(1)} %collective-permute-done.3.refs_2_, ...), custom_call_target="tpu_custom_call" | custom-call | tf_op jit(solution)/shard_map/mix/pallas_call | solution.py:364
  21.0 0.0 collective-permute-start.5
  21.0 1.5 %backward_own.1 = (bf16[128,1024]{1,0:T(8,128)(2,1)S(1)}, bf16[256,1024]{1,0:T(8,128)(2,1)S(1)}, bf16[832,128]{1,0:T(8,128)(2,1)S(1)}) custom-call(bf16[1024,256]{1,0:T(8,128)(2,1)S(1)} %get-tuple-element.63.refs_0_.cells, bf16[1024,256]{1,0:T(8,128)(2,1)S(1)} %get-tuple-element.64.refs_1_.cot, bf16[128,256]{1,0:T(8,128)(2,1)S(1)} %get-tuple-element.65.wsd, ...), custom_call_target="tpu_custom_call" | custom-call | flops 536870912 | tf_op jit(solution)/shard_map/backward_own/pallas_call | solution.py:364
  22.5 0.0 collective-permute-done.5.e.e_far
  22.5 1.5 %backward_far.1 = (bf16[128,1024]{1,0:T(8,128)(2,1)S(1)}, bf16[256,1024]{1,0:T(8,128)(2,1)S(1)}, bf16[832,128]{1,0:T(8,128)(2,1)S(1)}) custom-call(bf16[1024,256]{1,0:T(8,128)(2,1)S(1)} %get-tuple-element.63.refs_0_.cells, bf16[1024,256]{1,0:T(8,128)(2,1)S(1)} %get-tuple-element.64.refs_1_.cot, bf16[128,256]{1,0:T(8,128)(2,1)S(1)} %get-tuple-element.65.wsd, ...), custom_call_target="tpu_custom_call" | custom-call | tf_op jit(solution)/shard_map/backward_far/pallas_call | solution.py:364
  24.0 0.6 %collective-permute-start.6 = (bf16[832,128]{1,0:T(8,128)(2,1)S(1)}, bf16[832,128]{1,0:T(8,128)(2,1)S(1)}, u32[]{:S(2)}, u32[]{:S(2)}) collective-permute-start(bf16[832,128]{1,0:T(8,128)(2,1)S(1)} %get-tuple-element.101), channel_id=1, source_target_pairs={{0,1},{1,0},{2,3},{3,2},{4,5},{5,4},{6,7},{7,6},{8,9},{9,8},{10,11... | collective-permute-start | bytes 638984 | tf_op jit(solution)/shard_map/ppermute | solution.py:385
  24.5 1.2 %result.1 = (bf16[1024,256]{1,0:T(8,128)(2,1)}, f32[3,32,32]{2,1,0:T(8,128)}) custom-call(bf16[128,1024]{1,0:T(8,128)(2,1)S(1)} %get-tuple-element.102.own, bf16[128,1024]{1,0:T(8,128)(2,1)S(1)} %get-tuple-element.103.far, bf16[256,256]{1,0:T(8,128)(2,1)S(1)} %get-tuple-element.72.refs_2_.w_out, f32[104,256]{1,0:T(8,128)S(1)} %mix.1.e.e_own, ...), custom_call_target="tpu_custom_call" | custom-call | flops 134217728 | tf_op jit(solution)/shard_map/result/pallas_call | solution.py:364
  25.7 0.0 collective-permute-done.6.other
  25.7 0.1 pair_add.1
  25.8 12.7 %all_to_all.22 = bf16[8,104,128]{2,1,0:T(8,128)(2,1)S(1)} all-to-all(bf16[8,104,128]{2,1,0:T(8,128)(2,1)S(1)} %bitcast.6), channel_id=1, replica_groups={{0,2,4,6,8,10,12,14},{1,3,5,7,9,11,13,15},{16,18,20,22,24,26,28,30},{17..., dimensions={0} | all-to-all | bytes 425984 | tf_op jit(solution)/shard_map/all_to_all | solution.py:388
  38.5 11.0 %all_to_all.23 = bf16[8,104,128]{2,1,0:T(8,128)(2,1)S(1)} all-to-all(bf16[8,104,128]{2,1,0:T(8,128)(2,1)S(1)} %bitcast.10), channel_id=1, replica_groups={{0,2,4,6,8,10,12,14},{1,3,5,7,9,11,13,15},{16,18,20,22,24,26,28,30},{17..., dimensions={0} | all-to-all | bytes 425984 | tf_op jit(solution)/shard_map/all_to_all | solution.py:388
  49.5 0.0 collective-permute-start.7
  49.5 1.3 %grad_cells.1 = bf16[1024,256]{1,0:T(8,128)(2,1)} custom-call(bf16[256,1024]{1,0:T(8,128)(2,1)S(1)} %get-tuple-element.106.own, bf16[256,1024]{1,0:T(8,128)(2,1)S(1)} %get-tuple-element.107.far, bf16[256,256]{1,0:T(8,128)(2,1)S(1)} %get-tuple-element.108.w_x, bf16[256,256]{1,0:T(8,128)(2,1)S(1)} %get-tuple-element.109.w_fx), custom_call_target="tpu_custom_call" | custom-call | flops 268435456 | tf_op jit(solution)/shard_map/grad_cells/pallas_call | solution.py:364
  50.7 0.2 collective-permute-done.7.other
  50.9 1.0 %place.1 = (f32[256,256]{1,0:T(8,128)}, f32[256,256]{1,0:T(8,128)}, f32[32,64]{1,0:T(8,128)}, f32[1,32]{1,0:T(1,128)}, f32[256,256]{1,0:T(8,128)}) custom-call(bf16[832,128]{1,0:T(8,128)(2,1)S(1)} %bitcast.8, bf16[832,128]{1,0:T(8,128)(2,1)S(1)} %collective-permute-done.7.other), custom_call_target="tpu_custom_call" | custom-call | tf_op jit(solution)/shard_map/place/pallas_call | solution.py:364
  (3 shorter events, 0.1 us)
Async XLA Ops:
  3.9 1.6 %collective-permute-start = (f32[136,128]{1,0:T(8,128)S(1)}, f32[136,128]{1,0:T(8,128)S(1)}, u32[]{:S(2)}, u32[]{:S(2)}) collective-permute-start(f32[136,128]{1,0:T(8,128)S(1)} %get-tuple-element.71), channel_id=1, source_target_pairs={{0,1},{1,0},{2,3},{3,2},{4,5},{5,4},{6,7},{7,6},{8,9},{9,8},{10,11... | collective-permute-start | bytes 208904 | tf_op jit(solution)/shard_map/ppermute | solution.py:385
  5.6 2.8 %copy-start = (bf16[3,32,32]{2,1,0:T(8,128)(2,1)S(1)}, bf16[3,32,32]{2,1,0:T(8,128)(2,1)}, u32[]{:S(2)}) copy-start(bf16[3,32,32]{2,1,0:T(8,128)(2,1)} %w_qkv.3) | copy-start | bytes 18436
  5.6 4.7 %collective-permute-start.1 = (bf16[136,128]{1,0:T(8,128)(2,1)S(1)}, bf16[136,128]{1,0:T(8,128)(2,1)S(1)}, u32[]{:S(2)}, u32[]{:S(2)}) collective-permute-start(bf16[136,128]{1,0:T(8,128)(2,1)S(1)} %narrow.1.mine), channel_id=1, source_target_pairs={{0,2},{1,3},{2,0},{3,1},{4,6},{5,7},{6,4},{7,5},{8,10},{9,11},{10,... | collective-permute-start | bytes 104456 | tf_op jit(solution)/shard_map/ppermute | solution.py:385
  10.3 6.4 %collective-permute-start.4 = (bf16[136,128]{1,0:T(8,128)(2,1)S(1)}, bf16[136,128]{1,0:T(8,128)(2,1)S(1)}, u32[]{:S(2)}, u32[]{:S(2)}) collective-permute-start(bf16[136,128]{1,0:T(8,128)(2,1)S(1)} %near.1.refs_0_), channel_id=1, source_target_pairs={{0,12},{1,13},{2,14},{3,15},{4,8},{5,9},{6,10},{7,11},{8,4},{9,5},... | collective-permute-start | bytes 104456 | tf_op jit(solution)/shard_map/ppermute | solution.py:385
  14.4 4.8 %collective-permute-start.3 = (bf16[136,128]{1,0:T(8,128)(2,1)S(1)}, bf16[136,128]{1,0:T(8,128)(2,1)S(1)}, u32[]{:S(2)}, u32[]{:S(2)}) collective-permute-start(bf16[136,128]{1,0:T(8,128)(2,1)S(1)} %near.1.refs_0_), channel_id=1, source_target_pairs={{0,8},{1,9},{2,10},{3,11},{4,12},{5,13},{6,14},{7,15},{8,0},{9,1},... | collective-permute-start | bytes 104456 | tf_op jit(solution)/shard_map/ppermute | solution.py:385
  14.4 4.8 %collective-permute-start.2 = (bf16[136,128]{1,0:T(8,128)(2,1)S(1)}, bf16[136,128]{1,0:T(8,128)(2,1)S(1)}, u32[]{:S(2)}, u32[]{:S(2)}) collective-permute-start(bf16[136,128]{1,0:T(8,128)(2,1)S(1)} %near.1.refs_0_), channel_id=1, source_target_pairs={{0,4},{1,5},{2,6},{3,7},{4,0},{5,1},{6,2},{7,3},{8,12},{9,13},{10,... | collective-permute-start | bytes 104456 | tf_op jit(solution)/shard_map/ppermute | solution.py:385
  21.0 1.5 %collective-permute-start.5 = (f32[104,256]{1,0:T(8,128)S(1)}, f32[104,256]{1,0:T(8,128)S(1)}, u32[]{:S(2)}, u32[]{:S(2)}) collective-permute-start(f32[104,256]{1,0:T(8,128)S(1)} %mix.1.e.e_own), channel_id=1, source_target_pairs={{0,1},{1,0},{2,3},{3,2},{4,5},{5,4},{6,7},{7,6},{8,9},{9,8},{10,11... | collective-permute-start | bytes 319496 | tf_op jit(solution)/shard_map/ppermute | solution.py:385
  24.0 1.8 %collective-permute-start.6 = (bf16[832,128]{1,0:T(8,128)(2,1)S(1)}, bf16[832,128]{1,0:T(8,128)(2,1)S(1)}, u32[]{:S(2)}, u32[]{:S(2)}) collective-permute-start(bf16[832,128]{1,0:T(8,128)(2,1)S(1)} %get-tuple-element.101), channel_id=1, source_target_pairs={{0,1},{1,0},{2,3},{3,2},{4,5},{5,4},{6,7},{7,6},{8,9},{9,8},{10,11... | collective-permute-start | bytes 638984 | tf_op jit(solution)/shard_map/ppermute | solution.py:385
  49.5 1.5 %collective-permute-start.7 = (bf16[832,128]{1,0:T(8,128)(2,1)S(1)}, bf16[832,128]{1,0:T(8,128)(2,1)S(1)}, u32[]{:S(2)}, u32[]{:S(2)}) collective-permute-start(bf16[832,128]{1,0:T(8,128)(2,1)S(1)} %bitcast.7), channel_id=1, source_target_pairs={{0,1},{1,0},{2,3},{3,2},{4,5},{5,4},{6,7},{7,6},{8,9},{9,8},{10,11... | collective-permute-start | bytes 638984 | tf_op jit(solution)/shard_map/ppermute | solution.py:385

commit v7 on v6

--- a/solution.py
+++ b/solution.py
@@ -197,21 +197,21 @@
     tokens = numer * inverse
     maps = [w_qkv[k].astype(F32) for k in range(3)]
     qkv = nn(turned[...], tokens, FINE)
-    q, key, val = qkv[0:32], qkv[32:64], qkv[64:96]
-    key_rows, val_rows = key.T, val.T
-    scores = nn(key_rows, q, FINE) * (1.0 / math.sqrt(HEAD))
-    same = iota((256, 256), 0) // SLICES == iota((256, 256), 1) // SLICES
-    t = jnp.tanh(scores * 0.1)
-    powers = jnp.where(same, jnp.exp2(t * (10.0 * LOG2E)), 0.0)
-    att = powers * (1.0 / jnp.sum(powers, axis=0, keepdims=True))
-    mixed = nn(val, att, FINE)
-    d_att = nn(val_rows, d_mixed, FINE)
-    d_val = nt(d_mixed, att, FINE)
-    inner = jnp.sum(att * d_att, axis=0, keepdims=True)
-    d_scores = att * (d_att - inner) * ((1.0 - t * t) * (1.0 / math.sqrt(HEAD)))
-    d_q = nn(key, d_scores, FINE)
-    d_key = nt(q, d_scores, FINE)
-    grads = (d_q, d_key, d_val)
+    same = iota((128, 128), 0) // SLICES == iota((128, 128), 1) // SLICES
+    pairs = []
+    for i in range(2):
+        q, key, val = (qkv[32 * k : 32 * k + 32, 128 * i : 128 * i + 128] for k in range(3))
+        d_mix = d_mixed[:, 128 * i : 128 * i + 128]
+        scores = nn(key.T, q, FINE) * (1.0 / math.sqrt(HEAD))
+        t = jnp.tanh(scores * 0.1)
+        powers = jnp.where(same, jnp.exp2(t * (10.0 * LOG2E)), 0.0)
+        att = powers * (1.0 / jnp.sum(powers, axis=0, keepdims=True))
+        d_att = nn(val.T, d_mix, FINE)
+        inner = jnp.sum(att * d_att, axis=0, keepdims=True)
+        d_scores = att * (d_att - inner) * ((1.0 - t * t) * (1.0 / math.sqrt(HEAD)))
+        d_qkv = (nn(key, d_scores, FINE), nt(q, d_scores, FINE), nt(d_mix, att, FINE))
+        pairs.append((nn(val, att, FINE), *d_qkv))
+    mixed, *grads = (jnp.concatenate(both, axis=1) for both in zip(*pairs))
     d_tokens = sum(nn(m, g, FINE) for m, g in zip(maps, grads))
     d_numer = d_tokens * inverse
     d_denom = -jnp.sum(d_numer * tokens, axis=0, keepdims=True)

time: 52.2 us -> 51.9 us (level)
  no operation moved by 1% of the time
where the time goes in v7:
time: 51.9 us; the launch traced here: 51.7 us
  blocking collectives  23.6 us (45%)
  Pallas kernels  12.5 us (24%)
  starting transfers between devices  8.67 us (17%)
  waiting for transfers between devices  5.5 us (11%)
  between operations  1.4 us (3%)
    all_to_all x2, blocking collectives, exchange(): return lax.all_to_all(x, 'dom', 0, 0, axis_index_groups=groups, tiled=True)  23.6 us
    pallas_call x13, Pallas kernels, call(): pl.pallas_call(kernel, out_shape=[jax.ShapeDtypeStruct(s, d) for s, d in...  12.5 us
    ppermute x8, starting transfers between devices, swap(): return lax.ppermute(x, 'dom', [(i, i ^ mask) for i in range(devices)])  8.67 us
    ppermute x8, waiting for transfers between devices, swap(): return lax.ppermute(x, 'dom', [(i, i ^ mask) for i in range(devices)])  5.5 us
  transfers between devices with their start and end apart: 8, of which 4 were waited for; matrix products, arithmetic and copies ran while one was open for 0% of the time, Pallas kernels for 11%

profile of v7, /device:TPU:0, one launch (start us, length us, event | category | flops | bytes accessed | tf_op | source)
XLA Modules:
  0.0 51.7 jit_solution(12111697832993282974)
XLA Ops:
  1.3 2.6 %forward_far.1 = (bf16[256,1024]{1,0:T(8,128)(2,1)S(1)}, bf16[128,1024]{1,0:T(8,128)(2,1)S(1)}, bf16[256,1024]{1,0:T(8,128)(2,1)S(1)}, f32[32,1024]{1,0:T(8,128)...) custom-call(s32[1]{0:T(128)S(6)} %copy.17.counts, ...), custom_call_target="tpu_custom_call" | custom-call | tf_op jit(solution)/shard_map/forward_far/pallas_call | solution.py:364
  3.9 0.5 %collective-permute-start = (f32[136,128]{1,0:T(8,128)S(1)}, f32[136,128]{1,0:T(8,128)S(1)}, u32[]{:S(2)}, u32[]{:S(2)}) collective-permute-start(f32[136,128]{1,0:T(8,128)S(1)} %get-tuple-element.71), channel_id=1, source_target_pairs={{0,1},{1,0},{2,3},{3,2},{4,5},{5,4},{6,7},{7,6},{8,9},{9,8},{10,11... | collective-permute-start | bytes 208904 | tf_op jit(solution)/shard_map/ppermute | solution.py:385
  4.5 1.1 %forward_own.1 = (bf16[256,1024]{1,0:T(8,128)(2,1)S(1)}, bf16[128,1024]{1,0:T(8,128)(2,1)S(1)}, bf16[256,1024]{1,0:T(8,128)(2,1)S(1)}, f32[32,1024]{1,0:T(8,128)S(1)}, f32[136,128]{1,0:T(8,128)S(1)}) custom-call(s32[1]{0:T(128)S(6)} %copy.17.counts, bf16[1024,256]{1,0:T(8,128)(2,1)S(1)} %get-tuple-element.63.refs_0_.cells, ...), custom_call_target="tpu_custom_call" | custom-call | flops 402653184 | tf_op jit(solution)/shard_map/forward_own/pallas_call | solution.py:364
  5.6 0.0 collective-permute-done.other
  5.6 0.0 copy-start
  5.6 2.7 %collective-permute-start.1 = (bf16[136,128]{1,0:T(8,128)(2,1)S(1)}, bf16[136,128]{1,0:T(8,128)(2,1)S(1)}, u32[]{:S(2)}, u32[]{:S(2)}) collective-permute-start(bf16[136,128]{1,0:T(8,128)(2,1)S(1)} %narrow.1.mine), channel_id=1, source_target_pairs={{0,2},{1,3},{2,0},{3,1},{4,6},{5,7},{6,4},{7,5},{8,10},{9,11},{10,... | collective-permute-start | bytes 104456 | tf_op jit(solution)/shard_map/ppermute | solution.py:385
  8.3 0.0 copy-done
  8.3 0.8 %softmax.1 = (f32[256,1024]{1,0:T(8,128)S(1)}, f32[256,1024]{1,0:T(8,128)S(1)}, f32[256,1024]{1,0:T(8,128)S(1)}, f32[256,1024]{1,0:T(8,128)S(1)}, f32[256,1024]{...) custom-call(bf16[256,128]{1,0:T(8,128)(2,1)S(1)} %get-tuple-element.75.refs_5_.wsb, ...), custom_call_target="tpu_custom_call" | custom-call | flops 134217728 | tf_op jit(solution)/shard_map/softmax/pallas_call | solution.py:364
  9.2 1.1 %collective-permute-done.1.other = bf16[136,128]{1,0:T(8,128)(2,1)S(1)} collective-permute-done((bf16[136,128]{1,0:T(8,128)(2,1)S(1)}, bf16[136,128]{1,0:T(8,128)(2,1)S(1)}, u32[]{:S(2)}, u32[]{:S(2)}) %collective-permute-start.1) | collective-permute-done | bytes 34848 | tf_op jit(solution)/shard_map/ppermute | solution.py:385
  10.3 4.1 %collective-permute-start.4 = (bf16[136,128]{1,0:T(8,128)(2,1)S(1)}, bf16[136,128]{1,0:T(8,128)(2,1)S(1)}, u32[]{:S(2)}, u32[]{:S(2)}) collective-permute-start(bf16[136,128]{1,0:T(8,128)(2,1)S(1)} %near.1.refs_0_), channel_id=1, source_target_pairs={{0,12},{1,13},{2,14},{3,15},{4,8},{5,9},{6,10},{7,11},{8,4},{9,5},... | collective-permute-start | bytes 104456 | tf_op jit(solution)/shard_map/ppermute | solution.py:385
  14.4 0.0 collective-permute-start.3
  14.4 0.6 %collective-permute-start.2 = (bf16[136,128]{1,0:T(8,128)(2,1)S(1)}, bf16[136,128]{1,0:T(8,128)(2,1)S(1)}, u32[]{:S(2)}, u32[]{:S(2)}) collective-permute-start(bf16[136,128]{1,0:T(8,128)(2,1)S(1)} %near.1.refs_0_), channel_id=1, source_target_pairs={{0,4},{1,5},{2,6},{3,7},{4,0},{5,1},{6,2},{7,3},{8,12},{9,13},{10,... | collective-permute-start | bytes 104456 | tf_op jit(solution)/shard_map/ppermute | solution.py:385
  15.1 1.6 %collective-permute-done.4.refs_3_ = bf16[136,128]{1,0:T(8,128)(2,1)S(1)} collective-permute-done((bf16[136,128]{1,0:T(8,128)(2,1)S(1)}, bf16[136,128]{1,0:T(8,128)(2,1)S(1)}, u32[]{:S(2)}, u32[]{:S(2)}) %collective-permute-start.4) | collective-permute-done | bytes 34848 | tf_op jit(solution)/shard_map/ppermute | solution.py:385
  16.7 2.6 %collective-permute-done.3.refs_2_ = bf16[136,128]{1,0:T(8,128)(2,1)S(1)} collective-permute-done((bf16[136,128]{1,0:T(8,128)(2,1)S(1)}, bf16[136,128]{1,0:T(8,128)(2,1)S(1)}, u32[]{:S(2)}, u32[]{:S(2)}) %collective-permute-start.3) | collective-permute-done | bytes 34848 | tf_op jit(solution)/shard_map/ppermute | solution.py:385
  19.3 0.0 collective-permute-done.2.refs_1_
  19.3 1.3 %mix.1.e.e_own = f32[104,256]{1,0:T(8,128)S(1)} custom-call(bf16[3,32,32]{2,1,0:T(8,128)(2,1)S(1)} %copy-done, f32[96,32]{1,0:T(8,128)S(1)} %get-tuple-element.92.turned, bf16[136,128]{1,0:T(8,128)(2,1)S(1)} %near.1.refs_0_, bf16[136,128]{1,0:T(8,128)(2,1)S(1)} %collective-permute-done.2.refs_1_, bf16[136,128]{1,0:T(8,128)(2,1)S(1)} %collective-permute-done.3.refs_2_, ...), custom_call_target="tpu_custom_call" | custom-call | tf_op jit(solution)/shard_map/mix/pallas_call | solution.py:364
  20.6 0.1 collective-permute-start.5
  20.7 1.5 %backward_own.1 = (bf16[128,1024]{1,0:T(8,128)(2,1)S(1)}, bf16[256,1024]{1,0:T(8,128)(2,1)S(1)}, bf16[832,128]{1,0:T(8,128)(2,1)S(1)}) custom-call(bf16[1024,256]{1,0:T(8,128)(2,1)S(1)} %get-tuple-element.63.refs_0_.cells, bf16[1024,256]{1,0:T(8,128)(2,1)S(1)} %get-tuple-element.64.refs_1_.cot, bf16[128,256]{1,0:T(8,128)(2,1)S(1)} %get-tuple-element.65.wsd, ...), custom_call_target="tpu_custom_call" | custom-call | flops 536870912 | tf_op jit(solution)/shard_map/backward_own/pallas_call | solution.py:364
  22.2 0.0 collective-permute-done.5.e.e_far
  22.2 1.5 %backward_far.1 = (bf16[128,1024]{1,0:T(8,128)(2,1)S(1)}, bf16[256,1024]{1,0:T(8,128)(2,1)S(1)}, bf16[832,128]{1,0:T(8,128)(2,1)S(1)}) custom-call(bf16[1024,256]{1,0:T(8,128)(2,1)S(1)} %get-tuple-element.63.refs_0_.cells, bf16[1024,256]{1,0:T(8,128)(2,1)S(1)} %get-tuple-element.64.refs_1_.cot, bf16[128,256]{1,0:T(8,128)(2,1)S(1)} %get-tuple-element.65.wsd, ...), custom_call_target="tpu_custom_call" | custom-call | tf_op jit(solution)/shard_map/backward_far/pallas_call | solution.py:364
  23.7 0.6 %collective-permute-start.6 = (bf16[832,128]{1,0:T(8,128)(2,1)S(1)}, bf16[832,128]{1,0:T(8,128)(2,1)S(1)}, u32[]{:S(2)}, u32[]{:S(2)}) collective-permute-start(bf16[832,128]{1,0:T(8,128)(2,1)S(1)} %get-tuple-element.101), channel_id=1, source_target_pairs={{0,1},{1,0},{2,3},{3,2},{4,5},{5,4},{6,7},{7,6},{8,9},{9,8},{10,11... | collective-permute-start | bytes 638984 | tf_op jit(solution)/shard_map/ppermute | solution.py:385
  24.2 1.2 %result.1 = (bf16[1024,256]{1,0:T(8,128)(2,1)}, f32[3,32,32]{2,1,0:T(8,128)}) custom-call(bf16[128,1024]{1,0:T(8,128)(2,1)S(1)} %get-tuple-element.102.own, bf16[128,1024]{1,0:T(8,128)(2,1)S(1)} %get-tuple-element.103.far, bf16[256,256]{1,0:T(8,128)(2,1)S(1)} %get-tuple-element.72.refs_2_.w_out, f32[104,256]{1,0:T(8,128)S(1)} %mix.1.e.e_own, ...), custom_call_target="tpu_custom_call" | custom-call | flops 134217728 | tf_op jit(solution)/shard_map/result/pallas_call | solution.py:364
  25.4 0.0 collective-permute-done.6.other
  25.4 0.1 pair_add.1
  25.5 12.7 %all_to_all.22 = bf16[8,104,128]{2,1,0:T(8,128)(2,1)S(1)} all-to-all(bf16[8,104,128]{2,1,0:T(8,128)(2,1)S(1)} %bitcast.6), channel_id=1, replica_groups={{0,2,4,6,8,10,12,14},{1,3,5,7,9,11,13,15},{16,18,20,22,24,26,28,30},{17..., dimensions={0} | all-to-all | bytes 425984 | tf_op jit(solution)/shard_map/all_to_all | solution.py:388
  38.2 11.0 %all_to_all.23 = bf16[8,104,128]{2,1,0:T(8,128)(2,1)S(1)} all-to-all(bf16[8,104,128]{2,1,0:T(8,128)(2,1)S(1)} %bitcast.10), channel_id=1, replica_groups={{0,2,4,6,8,10,12,14},{1,3,5,7,9,11,13,15},{16,18,20,22,24,26,28,30},{17..., dimensions={0} | all-to-all | bytes 425984 | tf_op jit(solution)/shard_map/all_to_all | solution.py:388
  49.2 0.0 collective-permute-start.7
  49.2 1.3 %grad_cells.1 = bf16[1024,256]{1,0:T(8,128)(2,1)} custom-call(bf16[256,1024]{1,0:T(8,128)(2,1)S(1)} %get-tuple-element.106.own, bf16[256,1024]{1,0:T(8,128)(2,1)S(1)} %get-tuple-element.107.far, bf16[256,256]{1,0:T(8,128)(2,1)S(1)} %get-tuple-element.108.w_x, bf16[256,256]{1,0:T(8,128)(2,1)S(1)} %get-tuple-element.109.w_fx), custom_call_target="tpu_custom_call" | custom-call | flops 268435456 | tf_op jit(solution)/shard_map/grad_cells/pallas_call | solution.py:364
  50.4 0.2 collective-permute-done.7.other
  50.6 1.0 %place.1 = (f32[256,256]{1,0:T(8,128)}, f32[256,256]{1,0:T(8,128)}, f32[32,64]{1,0:T(8,128)}, f32[1,32]{1,0:T(1,128)}, f32[256,256]{1,0:T(8,128)}) custom-call(bf16[832,128]{1,0:T(8,128)(2,1)S(1)} %bitcast.8, bf16[832,128]{1,0:T(8,128)(2,1)S(1)} %collective-permute-done.7.other), custom_call_target="tpu_custom_call" | custom-call | tf_op jit(solution)/shard_map/place/pallas_call | solution.py:364
  (3 shorter events, 0.1 us)
Async XLA Ops:
  3.9 1.6 %collective-permute-start = (f32[136,128]{1,0:T(8,128)S(1)}, f32[136,128]{1,0:T(8,128)S(1)}, u32[]{:S(2)}, u32[]{:S(2)}) collective-permute-start(f32[136,128]{1,0:T(8,128)S(1)} %get-tuple-element.71), channel_id=1, source_target_pairs={{0,1},{1,0},{2,3},{3,2},{4,5},{5,4},{6,7},{7,6},{8,9},{9,8},{10,11... | collective-permute-start | bytes 208904 | tf_op jit(solution)/shard_map/ppermute | solution.py:385
  5.6 2.8 %copy-start = (bf16[3,32,32]{2,1,0:T(8,128)(2,1)S(1)}, bf16[3,32,32]{2,1,0:T(8,128)(2,1)}, u32[]{:S(2)}) copy-start(bf16[3,32,32]{2,1,0:T(8,128)(2,1)} %w_qkv.3) | copy-start | bytes 18436
  5.6 4.7 %collective-permute-start.1 = (bf16[136,128]{1,0:T(8,128)(2,1)S(1)}, bf16[136,128]{1,0:T(8,128)(2,1)S(1)}, u32[]{:S(2)}, u32[]{:S(2)}) collective-permute-start(bf16[136,128]{1,0:T(8,128)(2,1)S(1)} %narrow.1.mine), channel_id=1, source_target_pairs={{0,2},{1,3},{2,0},{3,1},{4,6},{5,7},{6,4},{7,5},{8,10},{9,11},{10,... | collective-permute-start | bytes 104456 | tf_op jit(solution)/shard_map/ppermute | solution.py:385
  10.3 6.4 %collective-permute-start.4 = (bf16[136,128]{1,0:T(8,128)(2,1)S(1)}, bf16[136,128]{1,0:T(8,128)(2,1)S(1)}, u32[]{:S(2)}, u32[]{:S(2)}) collective-permute-start(bf16[136,128]{1,0:T(8,128)(2,1)S(1)} %near.1.refs_0_), channel_id=1, source_target_pairs={{0,12},{1,13},{2,14},{3,15},{4,8},{5,9},{6,10},{7,11},{8,4},{9,5},... | collective-permute-start | bytes 104456 | tf_op jit(solution)/shard_map/ppermute | solution.py:385
  14.4 4.8 %collective-permute-start.3 = (bf16[136,128]{1,0:T(8,128)(2,1)S(1)}, bf16[136,128]{1,0:T(8,128)(2,1)S(1)}, u32[]{:S(2)}, u32[]{:S(2)}) collective-permute-start(bf16[136,128]{1,0:T(8,128)(2,1)S(1)} %near.1.refs_0_), channel_id=1, source_target_pairs={{0,8},{1,9},{2,10},{3,11},{4,12},{5,13},{6,14},{7,15},{8,0},{9,1},... | collective-permute-start | bytes 104456 | tf_op jit(solution)/shard_map/ppermute | solution.py:385
  14.4 4.8 %collective-permute-start.2 = (bf16[136,128]{1,0:T(8,128)(2,1)S(1)}, bf16[136,128]{1,0:T(8,128)(2,1)S(1)}, u32[]{:S(2)}, u32[]{:S(2)}) collective-permute-start(bf16[136,128]{1,0:T(8,128)(2,1)S(1)} %near.1.refs_0_), channel_id=1, source_target_pairs={{0,4},{1,5},{2,6},{3,7},{4,0},{5,1},{6,2},{7,3},{8,12},{9,13},{10,... | collective-permute-start | bytes 104456 | tf_op jit(solution)/shard_map/ppermute | solution.py:385
  20.6 1.6 %collective-permute-start.5 = (f32[104,256]{1,0:T(8,128)S(1)}, f32[104,256]{1,0:T(8,128)S(1)}, u32[]{:S(2)}, u32[]{:S(2)}) collective-permute-start(f32[104,256]{1,0:T(8,128)S(1)} %mix.1.e.e_own), channel_id=1, source_target_pairs={{0,1},{1,0},{2,3},{3,2},{4,5},{5,4},{6,7},{7,6},{8,9},{9,8},{10,11... | collective-permute-start | bytes 319496 | tf_op jit(solution)/shard_map/ppermute | solution.py:385
  23.7 1.8 %collective-permute-start.6 = (bf16[832,128]{1,0:T(8,128)(2,1)S(1)}, bf16[832,128]{1,0:T(8,128)(2,1)S(1)}, u32[]{:S(2)}, u32[]{:S(2)}) collective-permute-start(bf16[832,128]{1,0:T(8,128)(2,1)S(1)} %get-tuple-element.101), channel_id=1, source_target_pairs={{0,1},{1,0},{2,3},{3,2},{4,5},{5,4},{6,7},{7,6},{8,9},{9,8},{10,11... | collective-permute-start | bytes 638984 | tf_op jit(solution)/shard_map/ppermute | solution.py:385
  49.2 1.5 %collective-permute-start.7 = (bf16[832,128]{1,0:T(8,128)(2,1)S(1)}, bf16[832,128]{1,0:T(8,128)(2,1)S(1)}, u32[]{:S(2)}, u32[]{:S(2)}) collective-permute-start(bf16[832,128]{1,0:T(8,128)(2,1)S(1)} %bitcast.7), channel_id=1, source_target_pairs={{0,1},{1,0},{2,3},{3,2},{4,5},{5,4},{6,7},{7,6},{8,9},{9,8},{10,11... | collective-permute-start | bytes 638984 | tf_op jit(solution)/shard_map/ppermute | solution.py:385
